TPU v7x, 128 devices: a whole 4x4x4 slice. The times are simulated.
128 devices in a mesh: seq: 8 (over x, core), chan: 16 (over y, z).
Axes of the slice: x: 4, y: 4, z: 4, core: 2. Of those that a mesh axis runs over, the one named last changes fastest.
Arguments:
- tokens: bfloat16 [6144, 8192], P('seq', 'chan'), may hold values from -6 to 6
- norm_gain: bfloat16 [8192], P('chan'), may hold values from 0.099609375 to 1.8984375
- in_weight: bfloat16 [8192, 3, 8192], P('seq', None, 'chan'), may hold values from -0.0625 to 0.0625
- conv_weight: bfloat16 [3, 3, 8192], P(None, None, 'chan'), may hold values from -3 to 3
- filters: bfloat16 [512, 128], P('chan'), may hold values from -0.5 to 0.5
- out_weight: bfloat16 [8192, 8192], P('chan'), may hold values from -0.09375 to 0.09375
Outputs:
- result: bfloat16 [6144, 8192], P('seq', 'chan')
All inputs are finite; a program needn't handle non-finite values.
Results may differ from a plain program's by a relative error of at most 0.0084.
Values may be sent and summed in bfloat16 or wider, within the bound.
A program may use at most 192 MiB of HBM per device.

v0:
```python
import jax
import jax.numpy as jnp
import numpy as np
from jax import lax
from jax.sharding import PartitionSpec as P


def lag_tables(filters):
    length = filters.shape[1]
    offsets = np.arange(length)[:, None] - np.arange(length)[None, :]
    lookup = filters[:, offsets % length]
    lower = jnp.asarray(offsets >= 0)
    zero_value = jnp.zeros((), filters.dtype)
    return (jnp.where(lower, lookup, zero_value), jnp.where(lower, zero_value, lookup))


def hyena_core(extended, conv_weight, filters):
    length = filters.shape[1]
    values = extended.astype(jnp.float32)
    weights = conv_weight.astype(jnp.float32)
    shaped = (
        weights[:, 0, :] * values[2:]
        + weights[:, 1, :] * values[1:-1]
        + weights[:, 2, :] * values[:-2]
    )
    total = shaped.shape[0]
    out_rows = total - length
    query = shaped[length:, 0, :]
    mixed = (shaped[:, 1, :] * shaped[:, 2, :]).astype(jnp.bfloat16)
    group_count = filters.shape[0]
    channel_count = mixed.shape[1]
    blocks = mixed.reshape(total // length, length, group_count, channel_count // group_count)
    now_table, prev_table = lag_tables(filters)
    filtered = jnp.einsum(
        "gts,bsgw->btgw", now_table, blocks[1:], preferred_element_type=jnp.float32
    )
    filtered = filtered + jnp.einsum(
        "gts,bsgw->btgw", prev_table, blocks[:-1], preferred_element_type=jnp.float32
    )
    filtered = filtered.reshape(out_rows, channel_count)
    return (query * filtered).astype(jnp.bfloat16)


def local(tokens, norm_gain, in_weight, conv_weight, filters, out_weight):
    row_count = tokens.shape[0]
    chan_count = in_weight.shape[2]
    length = filters.shape[1]
    whole, gain_whole = (
        lax.all_gather(tokens, "chan", axis=1, tiled=True),
        lax.all_gather(norm_gain, "chan", axis=0, tiled=True),
    )
    values = whole.astype(jnp.float32)
    mean_square = jnp.mean(values * values, axis=1, keepdims=True)
    normed = (values * lax.rsqrt(mean_square + 1e-06) * gain_whole.astype(jnp.float32)).astype(
        jnp.bfloat16
    )
    piece = lax.all_gather(in_weight, "seq", axis=0, tiled=True)
    panel = piece.reshape(piece.shape[0], 3 * chan_count)
    projected = jnp.dot(normed, panel, preferred_element_type=jnp.float32)
    streams = projected.astype(jnp.bfloat16).reshape(row_count, 3, chan_count)
    moved = lax.all_to_all(streams, "seq", split_axis=2, concat_axis=0, tiled=True)
    parts_count = lax.axis_size("seq")
    slice_width = chan_count // parts_count
    group_width = filters.shape[0] // parts_count
    position = lax.axis_index("seq")
    conv_part = lax.dynamic_slice_in_dim(conv_weight, position * slice_width, slice_width, 2)
    filter_part = lax.dynamic_slice_in_dim(filters, position * group_width, group_width, 0)
    padding = jnp.zeros((length + 2, 3, slice_width), jnp.bfloat16)
    gated_slice = hyena_core(jnp.concatenate([padding, moved], axis=0), conv_part, filter_part)
    gated = lax.all_to_all(gated_slice, "seq", split_axis=0, concat_axis=1, tiled=True)
    partial_out = jnp.dot(gated, out_weight, preferred_element_type=jnp.float32)
    summed = lax.psum_scatter(partial_out, "chan", scatter_dimension=1, tiled=True)
    return (tokens.astype(jnp.float32) + summed).astype(jnp.bfloat16)


def solution(mesh):
    return jax.shard_map(
        local,
        mesh=mesh,
        in_specs=(
            P("seq", "chan"),
            P("chan"),
            P("seq", None, "chan"),
            P(None, None, "chan"),
            P("chan", None),
            P("chan", None),
        ),
        out_specs=P("seq", "chan"),
        check_vma=False,
    )
```

profile of v0, /device:TPU:1, one launch (start us, length us, event | category | flops | bytes accessed | tf_op | source)
XLA Modules:
  0.0 536.1 jit_solution(4963473210731182807)
XLA Ops:
  6.5 0.7 all-gather.4.cloned.1.call-update
  7.3 4.7 copy.23
  12.1 21.2 %all-gather = bf16[16,1,512]{2,1,0:T(2,128)(2,1)S(1)} all-gather(bf16[1,1,512]{2,1,0:T(2,128)(2,1)S(1)} %reshape.47), channel_id=1, replica_groups=mesh['seq'=8,'chan'=16] {'chan'}, dimensions={0}, use_global_device_ids=true | all-gather | bytes 17408 | tf_op jit(solution)/shard_map/all_gather | solution.py:50
  33.3 76.8 %all-gather.4.cloned.1.call-done = bf16[768,8192]{1,0:T(8,128)(2,1)} async-done(((bf16[768,512]{1,0:T(8,128)(2,1)}), bf16[768,8192]{1,0:T(8,128)(2,1)}) %all-gather.4.cloned.1.call-update) | async-done | bytes 12582928 | tf_op jit(solution)/shard_map/all_gather | solution.py:49
  110.1 7.1 %fusion = f32[768]{0:T(1024)S(1)} fusion(bf16[768,8192]{1,0:T(8,128)(2,1)} %all-gather.4.cloned.1.call-done), kind=kLoop, calls=%fused_computation.3 | loop fusion | flops 18873600 | bytes 12585984 | tf_op jit(solution)/shard_map/reduce_sum | solution.py:53
  117.2 115.8 %all-gather.6.cloned.1.call-done = bf16[8192,3,512]{0,2,1:T(8,128)(2,1)} async-done(((bf16[1024,3,512]{0,2,1:T(8,128)(2,1)}), bf16[8192,3,512]{0,2,1:T(8,128)(2,1)}) %all-gather.6.cloned.1.call-update) | async-done | bytes 25165840 | tf_op jit(solution)/shard_map/all_gather | solution.py:57
  233.0 25.8 %fusion.9 = bf16[768,1536]{1,0:T(8,128)(2,1)} fusion(bf16[8192,1536]{0,1:T(8,128)(2,1)} %bitcast.78, bf16[768,8192]{1,0:T(8,128)(2,1)} %all-gather.4.cloned.1.call-done, f32[8192]{0:T(1024)S(1)} %bitcast.76, f32[768]{0:T(1024)S(1)} %add_rsqrt_fusion), kind=kOutput, calls=%fused_computation.14 | convolution fusion | flops 19353698304 | bytes 40143872 | tf_op jit(solution)/shard_map/dot_general | solution.py:59
  258.8 2.8 copy.24
  261.6 3.7 copy.25
  265.3 4.2 all-to-all-start
  269.6 0.8 dynamic-slice_convert_fusion
  270.5 57.8 %gather_fusion = bf16[16384,4]{1,0:T(8,128)(2,1)} fusion(bf16[4,128]{0,1:T(8,128)(2,1)S(1)} %copy.40, s32[16384]{0:T(1024)S(1)} %broadcast_clamp_fusion), kind=kCustom, calls=%fused_computation | custom fusion | bytes 327680 | tf_op jit(solution)/shard_map/gather | solution.py:11
  328.3 3.7 copy.29
  332.7 0.7 pad_convert_fusion
  333.4 2.7 fusion.7
  337.4 0.4 add_bitcast_fusion
  337.8 0.5 copy.33
  338.3 1.5 reshape.37
  339.8 0.5 copy.42
  340.2 1.6 fusion.13
  342.0 16.7 %all_to_all.34 = bf16[8,768,64]{1,2,0:T(8,128)(2,1)S(1)} all-to-all(bf16[8,768,64]{1,2,0:T(8,128)(2,1)S(1)} %copy.34), channel_id=1, replica_groups=mesh['seq'=8,'chan'=16] {'seq'}, dimensions={0} | all-to-all | bytes 1572864 | tf_op jit(solution)/shard_map/all_to_all | solution.py:70
  358.7 15.1 %fusion.28 = f32[768,8192]{1,0:T(8,128)} fusion(bf16[768,512]{0,1:T(8,128)(2,1)S(1)} %bitcast.73, bf16[512,8192]{1,0:T(8,128)(2,1)} %param.14), kind=kOutput, calls=%fused_computation.45 | convolution fusion | flops 6442450944 | bytes 34340864 | tf_op jit(solution)/shard_map/dot_general | solution.py:71
  373.8 153.2 %reduce-scatter.2.cloned.1.call-done = f32[768,512]{1,0:T(8,128)} async-done(((f32[768,8192]{1,0:T(8,128)}), f32[768,512]{1,0:T(8,128)}) %reduce-scatter.2.cloned.1.call-update) | async-done | bytes 1572880 | tf_op jit(solution)/shard_map/reduce_scatter | solution.py:72
  527.0 2.5 add_convert_fusion
  (36 shorter events, 2.3 us)
Async XLA Ops:
  6.5 263.8 %copy-start = (bf16[32,128]{1,0:T(8,128)(2,1)S(1)}, bf16[32,128]{1,0:T(8,128)(2,1)}, u32[]{:S(2)}) copy-start(bf16[32,128]{1,0:T(8,128)(2,1)} %param.13) | copy-start | bytes 24580
  6.5 103.5 %all-gather.4.cloned.1.call-start = ((), (), s32[]{:S(2)}) async-start(), calls=%async_computation.3 | async-start | bytes 13369344 | tf_op jit(solution)/shard_map/all_gather | solution.py:49
  7.3 4.8 copy-start.5
  7.3 225.7 %all-gather.6.cloned.1.call-start = ((), (), s32[]{:S(2)}) async-start(), calls=%async_computation.4 | async-start | bytes 28311552 | tf_op jit(solution)/shard_map/all_gather | solution.py:57
  261.6 8.9 %copy-start.4 = (s32[16384]{0:T(1024)S(1)}, s32[16384]{0:T(1024)}, u32[]{:S(2)}) copy-start(s32[16384]{0:T(1024)} %constant.40) | copy-start | bytes 196612
  265.3 66.7 %all-to-all-start = ((bf16[768,3,512]{0,1,2:T(4,128)(2,1)}), bf16[768,3,512]{0,1,2:T(4,128)(2,1)S(1)}, u32[]{:S(2)}, u32[]{:S(2)}) async-start(bf16[768,3,512]{0,1,2:T(4,128)(2,1)} %copy.25), calls=%async_computation | async-start | bytes 6291456 | tf_op jit(solution)/shard_map/all_to_all | solution.py:61
  269.5 257.4 %reduce-scatter.2.cloned.1.call-start = ((), (), s32[]{:S(2)}) async-start(), calls=%async_computation.5 | async-start | bytes 26738688 | tf_op jit(solution)/shard_map/reduce_scatter | solution.py:72
  336.3 0.7 copy-start.3
  373.8 153.2 %copy-start.2 = (bf16[768,512]{1,0:T(8,128)(2,1)S(1)}, bf16[768,512]{1,0:T(8,128)(2,1)}, u32[]{:S(2)}) copy-start(bf16[768,512]{1,0:T(8,128)(2,1)} %param.9) | copy-start | bytes 2359300
  373.8 155.7 %copy-start.1 = (bf16[32,128]{1,0:T(8,128)(2,1)S(1)}, bf16[32,128]{1,0:T(8,128)(2,1)}, u32[]{:S(2)}) copy-start(bf16[32,128]{1,0:T(8,128)(2,1)} %param.13) | copy-start | bytes 24580
Sparse Core Ops, SparseCore 0:
  9.4 100.5 all-gather.3
  111.8 121.1 all-gather.5
  373.9 153.0 reduce-scatter.1
where the time goes:
time: 537 us; the launch traced here: 536 us
  waiting for transfers between devices  346 us (64%)
  local copies, waits for them, and re-layouts  76.9 us (14%)
  matrix products  41.7 us (8%)
  blocking collectives  37.9 us (7%)
  other arithmetic  15.6 us (3%)
  between operations  13.3 us (2%)
    reduce_scatter x1, waiting for transfers between devices, local(): lax.psum_scatter(partial_out, 'chan', scatter_dimension=1, tiled=True)  153 us
    all_gather x1, waiting for transfers between devices, local(): piece = lax.all_gather(in_weight, 'seq', axis=0, tiled=True)  116 us
    all_gather x1, waiting for transfers between devices, local(): lax.all_gather(tokens, 'chan', axis=1, tiled=True)  76.8 us
    gather x2, local copies, waits for them, and re-layouts, lag_tables(): lookup = filters[:, offsets % length]  61.5 us
    dot_general x1, matrix products, local(): projected = jnp.dot(normed, panel, preferred_element_type=jnp.float32)  25.8 us
    all_gather x1, blocking collectives, local(): lax.all_gather(norm_gain, 'chan', axis=0, tiled=True)  21.2 us
    all_to_all x1, blocking collectives, local(): lax.all_to_all(gated_slice, 'seq', split_axis=0, concat_axis=1, tiled=True)  16.7 us
    dot_general x1, matrix products, local(): partial_out = jnp.dot(gated, out_weight, preferred_element_type=jnp.float32)  15.1 us
  transfers between devices with their start and end apart: 4, of which 3 were waited for; matrix products, arithmetic and copies ran while one was open for 14% of the time, Pallas kernels for 0%

commit v1 on v0

v1 whole, which is shorter than its diff:
```python
import jax
import jax.numpy as jnp
import numpy as np
from jax import lax
from jax.sharding import PartitionSpec as P


def lag_table(filters):
    groups, length = filters.shape
    width = 3 * length
    zeros = jnp.zeros((groups, length), filters.dtype)
    skew = jnp.concatenate([zeros, filters[:, ::-1], zeros], axis=1)
    tiled = jnp.tile(skew, (1, length + 1))[:, : length * (width + 1)]
    windows = tiled.reshape(groups, length, width + 1)[:, :, : 2 * length]
    return windows[:, ::-1, :]


def hyena_core(extended, conv_weight, filters):
    length = filters.shape[1]
    values = extended.astype(jnp.float32)
    weights = conv_weight.astype(jnp.float32)
    shaped = (
        weights[:, 0, :] * values[2:]
        + weights[:, 1, :] * values[1:-1]
        + weights[:, 2, :] * values[:-2]
    )
    total = shaped.shape[0]
    out_rows = total - length
    query = shaped[length:, 0, :]
    mixed = (shaped[:, 1, :] * shaped[:, 2, :]).astype(jnp.bfloat16)
    group_count = filters.shape[0]
    channel_count = mixed.shape[1]
    blocks = mixed.reshape(total // length, length, group_count, channel_count // group_count)
    paired = jnp.concatenate([blocks[:-1], blocks[1:]], axis=1)
    table = lag_table(filters)
    filtered = jnp.einsum(
        "gts,bsgw->btgw", table, paired, preferred_element_type=jnp.float32
    )
    filtered = filtered.reshape(out_rows, channel_count)
    return (query * filtered).astype(jnp.bfloat16)


def local(tokens, norm_gain, in_weight, conv_weight, filters, out_weight):
    row_count = tokens.shape[0]
    chan_count = in_weight.shape[2]
    length = filters.shape[1]
    joined = jnp.concatenate([tokens, norm_gain[None, :]], axis=0)
    whole_joined = lax.all_gather(joined, "chan", axis=1, tiled=True)
    whole, gain_whole = whole_joined[:row_count], whole_joined[row_count]
    values = whole.astype(jnp.float32)
    mean_square = jnp.mean(values * values, axis=1, keepdims=True)
    normed = (values * lax.rsqrt(mean_square + 1e-06) * gain_whole.astype(jnp.float32)).astype(
        jnp.bfloat16
    )
    piece = lax.all_gather(in_weight, "seq", axis=0, tiled=True)
    panel = piece.reshape(piece.shape[0], 3 * chan_count)
    projected = jnp.dot(normed, panel, preferred_element_type=jnp.float32)
    streams = projected.astype(jnp.bfloat16).reshape(row_count, 3, chan_count)
    parts_count = lax.axis_size("seq")
    halo_rows = length + 2
    shift = [(i, i + 1) for i in range(parts_count - 1)]
    halo = lax.ppermute(streams[row_count - halo_rows :], "seq", shift)
    extended = jnp.concatenate([halo, streams], axis=0)
    gated = hyena_core(extended, conv_weight, filters)
    partial_out = jnp.dot(gated, out_weight, preferred_element_type=jnp.float32)
    summed = lax.psum_scatter(partial_out, "chan", scatter_dimension=1, tiled=True)
    return (tokens.astype(jnp.float32) + summed).astype(jnp.bfloat16)


def solution(mesh):
    return jax.shard_map(
        local,
        mesh=mesh,
        in_specs=(
            P("seq", "chan"),
            P("chan"),
            P("seq", None, "chan"),
            P(None, None, "chan"),
            P("chan", None),
            P("chan", None),
        ),
        out_specs=P("seq", "chan"),
        check_vma=False,
    )
```

time: 537 us -> 497 us (0.926)
  blocking collectives: 37.9 us -> 0 us
  local copies, waits for them, and re-layouts: 76.9 us -> 52.1 us
  waiting for transfers between devices: 346 us -> 364 us
    gather x2 -> x0, local copies, waits for them, and re-layouts: 61.5 us -> none  [lag_tables(): lookup = filters[:, offsets % length]]
    all_gather x1 -> x0, blocking collectives: 21.2 us -> none  [local(): lax.all_gather(norm_gain, 'chan', axis=0, tiled=True)]
    rev x0 -> x2, local copies, waits for them, and re-layouts: none -> 20.3 us  [the longest x1 20.2 us: lag_table(): return windows[:, ::-1, :]]
    all_gather x1, waiting for transfers between devices: 76.8 us -> 96.5 us  [local(): whole_joined = lax.all_gather(joined, 'chan', axis=1, tiled=True)]
    all_to_all x1 -> x0, blocking collectives: 16.7 us -> none  [local(): lax.all_to_all(gated_slice, 'seq', split_axis=0, concat_axis=1, tiled=True)]
    slice x1 -> x11, local copies, waits for them, and re-layouts: 0.1 us -> 9.65 us  [the longest x5 6.35 us: hyena_core(): paired = jnp.concatenate([blocks[:-1], blocks[1:]], axis=1)]
  transfers between devices with their start and end apart: 4 -> 4, of which waited for: 3 -> 3; matrix products, arithmetic and copies ran while one was open for 14% -> 9% of each run, Pallas kernels for 0% -> 0%
where the time goes in v1:
time: 497 us
  waiting for transfers between devices  364 us (73%)
  local copies, waits for them, and re-layouts  52.1 us (10%)
  matrix products  44.7 us (9%)
  other arithmetic  18.7 us (4%)
  between operations  13.4 us (3%)
    reduce_scatter x1, waiting for transfers between devices, local(): lax.psum_scatter(partial_out, 'chan', scatter_dimension=1, tiled=True)  153 us
    all_gather x1, waiting for transfers between devices, local(): piece = lax.all_gather(in_weight, 'seq', axis=0, tiled=True)  115 us
    all_gather x1, waiting for transfers between devices, local(): whole_joined = lax.all_gather(joined, 'chan', axis=1, tiled=True)  96.5 us
    dot_general x1, matrix products, local(): projected = jnp.dot(normed, panel, preferred_element_type=jnp.float32)  27.1 us
    rev x1, local copies, waits for them, and re-layouts, lag_table(): return windows[:, ::-1, :]  20.2 us
    dot_general x1, matrix products, local(): partial_out = jnp.dot(gated, out_weight, preferred_element_type=jnp.float32)  15.5 us
  transfers between devices with their start and end apart: 4, of which 3 were waited for; matrix products, arithmetic and copies ran while one was open for 9% of the time, Pallas kernels for 0%

profile of v1, /device:TPU:1, one launch (start us, length us, event | category | flops | bytes accessed | tf_op | source)
XLA Modules:
  0.0 496.6 jit_solution(15601686603221840330)
XLA Ops:
  7.2 2.1 pad_maximum_fusion
  9.4 4.6 copy.13
  14.1 96.5 %all-gather.3.cloned.1.call-done = bf16[769,8192]{1,0:T(8,128)(2,1)} async-done(((bf16[769,512]{1,0:T(8,128)(2,1)}), bf16[769,8192]{1,0:T(8,128)(2,1)}) %all-gather.3.cloned.1.call-update) | async-done | bytes 12599312 | tf_op jit(solution)/shard_map/all_gather | solution.py:48
  110.6 7.1 %fusion = f32[768]{0:T(1024)S(1)} fusion(bf16[769,8192]{1,0:T(8,128)(2,1)} %all-gather.3.cloned.1.call-done), kind=kLoop, calls=%fused_computation.2 | loop fusion | flops 18873600 | bytes 12585984 | tf_op jit(solution)/shard_map/reduce_sum | solution.py:51
  118.7 114.9 %all-gather.5.cloned.1.call-done = bf16[8192,3,512]{0,2,1:T(8,128)(2,1)} async-done(((bf16[1024,3,512]{0,2,1:T(8,128)(2,1)}), bf16[8192,3,512]{0,2,1:T(8,128)(2,1)}) %all-gather.5.cloned.1.call-update) | async-done | bytes 25165840 | tf_op jit(solution)/shard_map/all_gather | solution.py:55
  233.5 27.1 %fusion.10 = bf16[768,1536]{1,0:T(8,128)(2,1)S(1)} fusion(bf16[8192,1536]{0,1:T(8,128)(2,1)} %bitcast.49, f32[8192]{0:T(1024)S(1)} %bitcast.48, f32[768]{0:T(1024)S(1)} %add_rsqrt_fusion, bf16[769,8192]{1,0:T(8,128)(2,1)} %all-gather.3.cloned.1.call-done), kind=kOutput, calls=%fused_computation.14 | convolution fusion | flops 19353698304 | bytes 40143872 | tf_op jit(solution)/shard_map/dot_general | solution.py:57
  261.1 1.1 copy.14
  262.2 3.4 collective-permute-start
  266.7 8.9 %reshape.39 = bf16[32,128,385]{2,1,0:T(8,128)(2,1)} reshape(bf16[32,49280]{1,0:T(8,128)(2,1)S(1)} %slice.92) | data formatting | bytes 6307840 | tf_op jit(solution)/shard_map/reshape | solution.py:14
  275.6 1.6 slice-done.2
  277.2 20.2 %rev.7 = bf16[32,128,256]{2,1,0:T(8,128)(2,1)} reverse(bf16[32,128,256]{2,1,0:T(8,128)(2,1)S(1)} %slice-done.2), dimensions={1} | reverse | bytes 4194304 | tf_op jit(solution)/shard_map/rev | solution.py:15
  297.4 2.8 copy.15
  300.3 1.3 copy.16
  301.6 1.3 maximum_convert_fusion
  302.9 4.5 fusion.8
  307.4 2.4 copy-done
  310.0 1.3 fusion.28
  311.3 2.0 slice.73
  313.2 1.0 copy.17
  314.3 2.0 slice.75
  316.4 2.1 fusion.20
  319.1 15.5 %fusion.25 = f32[768,8192]{1,0:T(8,128)} fusion(bf16[512,8192]{1,0:T(8,128)(2,1)} %param.11, f32[64,8,6,128]{3,2,1,0:T(8,128)S(1)} %bitcast.44, f32[896,3,512]{0,2,1:T(8,128)S(1)} %bitcast.42), kind=kOutput, calls=%fused_computation.29 | convolution fusion | flops 6443237376 | bytes 37224448 | tf_op jit(solution)/shard_map/dot_general | solution.py:65
  334.6 152.9 %reduce-scatter.2.cloned.1.call-done = f32[768,512]{1,0:T(8,128)} async-done(((f32[768,8192]{1,0:T(8,128)}), f32[768,512]{1,0:T(8,128)}) %reduce-scatter.2.cloned.1.call-update) | async-done | bytes 1572880 | tf_op jit(solution)/shard_map/reduce_scatter | solution.py:66
  487.5 2.5 add_convert_fusion
  (41 shorter events, 4.1 us)
Async XLA Ops:
  6.5 104.1 %all-gather.3.cloned.1.call-start = ((), (), s32[]{:S(2)}) async-start(), calls=%async_computation.1 | async-start | bytes 13508608 | tf_op jit(solution)/shard_map/all_gather | solution.py:48
  9.3 224.2 %all-gather.5.cloned.1.call-start = ((), (), s32[]{:S(2)}) async-start(), calls=%async_computation.2 | async-start | bytes 28311552 | tf_op jit(solution)/shard_map/all_gather | solution.py:55
  14.1 473.4 %reduce-scatter.2.cloned.1.call-start = ((), (), s32[]{:S(2)}) async-start(), calls=%async_computation.3 | async-start | bytes 26738688 | tf_op jit(solution)/shard_map/reduce_scatter | solution.py:66
  233.5 32.1 %copy-start.4 = (bf16[3,3,512]{2,1,0:T(4,128)(2,1)S(1)}, bf16[3,3,512]{2,1,0:T(4,128)(2,1)}, u32[]{:S(2)}) copy-start(bf16[3,3,512]{2,1,0:T(4,128)(2,1)} %param.9) | copy-start | bytes 27652
  233.5 32.1 %copy-start.5 = (bf16[32,128]{1,0:T(8,128)(2,1)S(1)}, bf16[32,128]{1,0:T(8,128)(2,1)}, u32[]{:S(2)}) copy-start(bf16[32,128]{1,0:T(8,128)(2,1)} %param.10) | copy-start | bytes 24580
  260.7 5.8 %copy-start.2 = (bf16[768,1536]{1,0:T(8,128)(2,1)}, bf16[768,1536]{1,0:T(8,128)(2,1)S(1)}, u32[]{:S(2)}) copy-start(bf16[768,1536]{1,0:T(8,128)(2,1)S(1)} %fusion.10) | copy-start | bytes 7077892
  262.2 38.1 %collective-permute-start = (bf16[130,3,512]{2,0,1:T(8,128)(2,1)}, bf16[130,3,512]{2,0,1:T(8,128)(2,1)}, u32[]{:S(2)}, u32[]{:S(2)}) collective-permute-start(bf16[130,3,512]{2,0,1:T(8,128)(2,1)} %copy.14), channel_id=1, source_target_pairs={{0,16},{16,32},{32,48},{48,64},{64,80},{80,96},{96,112},{1,17},{17... | collective-permute-start | bytes 1198088 | tf_op jit(solution)/shard_map/ppermute | solution.py:62
  275.6 1.6 slice-start.2
  307.4 2.4 copy-start
  310.0 6.4 %copy-start.1 = (bf16[32,128,256]{2,1,0:T(8,128)(2,1)S(1)}, bf16[32,128,256]{2,1,0:T(8,128)(2,1)}, u32[]{:S(2)}) copy-start(bf16[32,128,256]{2,1,0:T(8,128)(2,1)} %rev.7) | copy-start | bytes 6291460
  316.2 2.9 slice-start
  316.4 2.7 slice-start.1
  334.6 152.9 %copy-start.3 = (bf16[768,512]{1,0:T(8,128)(2,1)S(1)}, bf16[768,512]{1,0:T(8,128)(2,1)}, u32[]{:S(2)}) copy-start(bf16[768,512]{1,0:T(8,128)(2,1)} %param.6) | copy-start | bytes 2359300
Sparse Core Ops, SparseCore 0:
  9.5 101.1 all-gather.2
  112.3 121.1 all-gather.4
  334.8 152.6 reduce-scatter.1

commit v2 on v1

--- a/solution.py
+++ b/solution.py
@@ -10,9 +10,9 @@
     width = 3 * length
     zeros = jnp.zeros((groups, length), filters.dtype)
     skew = jnp.concatenate([zeros, filters[:, ::-1], zeros], axis=1)
-    tiled = jnp.tile(skew, (1, length + 1))[:, : length * (width + 1)]
-    windows = tiled.reshape(groups, length, width + 1)[:, :, : 2 * length]
-    return windows[:, ::-1, :]
+    tiled = jnp.tile(skew, (1, length))[:, : length * (width - 1)]
+    rows = tiled.reshape(groups, length, width - 1)
+    return rows[:, :, length - 1 : 3 * length - 1]
 
 
 def hyena_core(extended, conv_weight, filters):
@@ -63,8 +63,10 @@
     extended = jnp.concatenate([halo, streams], axis=0)
     gated = hyena_core(extended, conv_weight, filters)
     partial_out = jnp.dot(gated, out_weight, preferred_element_type=jnp.float32)
-    summed = lax.psum_scatter(partial_out, "chan", scatter_dimension=1, tiled=True)
-    return (tokens.astype(jnp.float32) + summed).astype(jnp.bfloat16)
+    summed = lax.psum_scatter(
+        partial_out.astype(jnp.bfloat16), "chan", scatter_dimension=1, tiled=True
+    )
+    return (tokens.astype(jnp.float32) + summed.astype(jnp.float32)).astype(jnp.bfloat16)
 
 
 def solution(mesh):

time: 497 us -> 415 us (0.84)
  waiting for transfers between devices: 364 us -> 306 us
  local copies, waits for them, and re-layouts: 52.1 us -> 29.7 us
    reduce_scatter x1, waiting for transfers between devices: 153 us -> 94.3 us  [local(): lax.psum_scatter(partial_out.astype(jnp.bfloat16), 'chan', scatter_dimens...]
    rev x1 -> x0, local copies, waits for them, and re-layouts: 20.2 us -> none  [lag_table(): return windows[:, ::-1, :]]
  transfers between devices with their start and end apart: 4 -> 4, of which waited for: 3 -> 3; matrix products, arithmetic and copies ran while one was open for 9% -> 7% of each run, Pallas kernels for 0% -> 0%
where the time goes in v2:
time: 415 us; the launch traced here: 414 us
  waiting for transfers between devices  306 us (74%)
  matrix products  43.4 us (10%)
  local copies, waits for them, and re-layouts  29.7 us (7%)
  other arithmetic  18.3 us (4%)
  between operations  13.4 us (3%)
    all_gather x1, waiting for transfers between devices, local(): piece = lax.all_gather(in_weight, 'seq', axis=0, tiled=True)  115 us
    all_gather x1, waiting for transfers between devices, local(): whole_joined = lax.all_gather(joined, 'chan', axis=1, tiled=True)  96.5 us
    reduce_scatter x1, waiting for transfers between devices, local(): lax.psum_scatter(partial_out.astype(jnp.bfloat16), 'chan', scatter_dimens...  94.3 us
    dot_general x1, matrix products, local(): projected = jnp.dot(normed, panel, preferred_element_type=jnp.float32)  27.1 us
    dot_general x1, matrix products, local(): partial_out = jnp.dot(gated, out_weight, preferred_element_type=jnp.float32)  13.5 us
    unnamed x20, local copies, waits for them, and re-layouts  10.9 us
  transfers between devices with their start and end apart: 4, of which 3 were waited for; matrix products, arithmetic and copies ran while one was open for 7% of the time, Pallas kernels for 0%

profile of v2, /device:TPU:1, one launch (start us, length us, event | category | flops | bytes accessed | tf_op | source)
XLA Modules:
  0.0 414.1 jit_solution(12468193166060779278)
XLA Ops:
  7.2 2.1 pad_maximum_fusion
  9.4 4.7 %copy.13 = bf16[1024,3,512]{0,2,1:T(8,128)(2,1)} copy(bf16[1024,3,512]{2,0,1:T(8,128)(2,1)} %param.8) | data formatting | bytes 6291456 | tf_op args[2]
  14.2 96.5 %all-gather.3.cloned.1.call-done = bf16[769,8192]{1,0:T(8,128)(2,1)} async-done(((bf16[769,512]{1,0:T(8,128)(2,1)}), bf16[769,8192]{1,0:T(8,128)(2,1)}) %all-gather.3.cloned.1.call-update) | async-done | bytes 12599312 | tf_op jit(solution)/shard_map/all_gather | solution.py:48
  110.6 7.1 %fusion = f32[768]{0:T(1024)S(1)} fusion(bf16[769,8192]{1,0:T(8,128)(2,1)} %all-gather.3.cloned.1.call-done), kind=kLoop, calls=%fused_computation.2 | loop fusion | flops 18873600 | bytes 12585984 | tf_op jit(solution)/shard_map/reduce_sum | solution.py:51
  117.7 0.9 slice_convert_fusion
  118.7 114.9 %all-gather.5.cloned.1.call-done = bf16[8192,3,512]{0,2,1:T(8,128)(2,1)} async-done(((bf16[1024,3,512]{0,2,1:T(8,128)(2,1)}), bf16[8192,3,512]{0,2,1:T(8,128)(2,1)}) %all-gather.5.cloned.1.call-update) | async-done | bytes 25165840 | tf_op jit(solution)/shard_map/all_gather | solution.py:55
  233.5 27.1 %fusion.10 = bf16[768,1536]{1,0:T(8,128)(2,1)S(1)} fusion(bf16[8192,1536]{0,1:T(8,128)(2,1)} %bitcast.49, f32[8192]{0:T(1024)S(1)} %bitcast.48, f32[768]{0:T(1024)S(1)} %add_rsqrt_fusion, bf16[769,8192]{1,0:T(8,128)(2,1)} %all-gather.3.cloned.1.call-done), kind=kOutput, calls=%fused_computation.15 | convolution fusion | flops 19353698304 | bytes 40143872 | tf_op jit(solution)/shard_map/dot_general | solution.py:57
  261.1 3.4 collective-permute-start
  264.6 1.4 fusion.25
  266.6 0.8 rev.3
  267.7 1.9 copy.24
  269.8 8.0 %reshape.39 = bf16[32,128,383]{2,1,0:T(8,128)(2,1)} reshape(bf16[32,49024]{1,0:T(8,128)(2,1)S(1)} %slice.92) | data formatting | bytes 6275072 | tf_op jit(solution)/shard_map/reshape | solution.py:14
  277.8 1.3 copy_bitcast_fusion
  279.1 2.8 copy.15
  282.0 1.3 copy.16
  283.3 1.3 maximum_convert_fusion
  284.7 4.5 %fusion.8 = f32[896,3,512]{0,2,1:T(8,128)S(1)} fusion(f32[898,3,512]{0,2,1:T(8,128)S(1)} %maximum_convert_fusion, f32[3,512]{1,0:T(4,128)S(1)} %copy-done.3, f32[3,512]{1,0:T(4,128)S(1)} %copy-done.4, f32[3,512]{1,0:T(4,128)S(1)} %bitcast.47), kind=kLoop, calls=%fused_computation.11 | loop fusion | flops 6881280 | bytes 22038528 | tf_op jit(solution)/shard_map/add | solution.py:23
  289.2 2.4 copy-done
  291.9 0.9 slice.73
  292.9 0.9 slice.75
  294.0 2.9 fusion.19
  297.5 13.5 %convolution_convert_fusion = bf16[768,8192]{1,0:T(8,128)(2,1)} fusion(bf16[512,8192]{1,0:T(8,128)(2,1)} %param.11, f32[64,8,6,128]{3,2,1,0:T(8,128)S(1)} %bitcast.43, f32[896,3,512]{0,2,1:T(8,128)S(1)} %bitcast.42), kind=kOutput, calls=%fused_computation.5 | convolution fusion | flops 6449528832 | bytes 24641536 | tf_op jit(solution)/shard_map/dot_general | solution.py:65
  311.0 94.3 %reduce-scatter.2.cloned.1.call-done = bf16[768,512]{1,0:T(8,128)(2,1)} async-done(((bf16[768,8192]{1,0:T(8,128)(2,1)}), bf16[768,512]{1,0:T(8,128)(2,1)}) %reduce-scatter.2.cloned.1.call-update) | async-done | bytes 786448 | tf_op jit(solution)/shard_map/reduce_scatter | solution.py:66
  405.3 2.2 add_convert_fusion
  (38 shorter events, 3.6 us)
Async XLA Ops:
  6.5 104.1 %all-gather.3.cloned.1.call-start = ((), (), s32[]{:S(2)}) async-start(), calls=%async_computation.1 | async-start | bytes 13508608 | tf_op jit(solution)/shard_map/all_gather | solution.py:48
  9.4 224.2 %all-gather.5.cloned.1.call-start = ((), (), s32[]{:S(2)}) async-start(), calls=%async_computation.2 | async-start | bytes 28311552 | tf_op jit(solution)/shard_map/all_gather | solution.py:55
  14.1 391.2 %reduce-scatter.2.cloned.1.call-start = ((), (), s32[]{:S(2)}) async-start(), calls=%async_computation.3 | async-start | bytes 13369344 | tf_op jit(solution)/shard_map/reduce_scatter | solution.py:66
  260.6 9.0 %copy-start.1 = (bf16[768,1536]{1,0:T(8,128)(2,1)}, bf16[768,1536]{1,0:T(8,128)(2,1)S(1)}, u32[]{:S(2)}) copy-start(bf16[768,1536]{1,0:T(8,128)(2,1)S(1)} %fusion.10) | copy-start | bytes 7077892
  261.1 20.8 %collective-permute-start = (bf16[130,3,512]{2,0,1:T(8,128)(2,1)S(1)}, bf16[130,3,512]{2,0,1:T(8,128)(2,1)}, u32[]{:S(2)}, u32[]{:S(2)}) collective-permute-start(bf16[130,3,512]{2,0,1:T(8,128)(2,1)S(1)} %copy.14), channel_id=1, source_target_pairs={{0,16},{16,32},{32,48},{48,64},{64,80},{80,96},{96,112},{1,17},{17... | collective-permute-start | bytes 1198088 | tf_op jit(solution)/shard_map/ppermute | solution.py:62
  282.0 2.6 copy-start.3
  282.0 2.6 copy-start.4
  282.0 2.6 copy-start.5
  289.2 2.4 copy-start
  293.8 3.7 slice-start
  293.9 3.5 slice-start.1
  311.0 94.3 %copy-start.2 = (bf16[768,512]{1,0:T(8,128)(2,1)S(1)}, bf16[768,512]{1,0:T(8,128)(2,1)}, u32[]{:S(2)}) copy-start(bf16[768,512]{1,0:T(8,128)(2,1)} %param.6) | copy-start | bytes 2359300
Sparse Core Ops, SparseCore 0:
  9.5 101.1 all-gather.2
  112.3 121.1 all-gather.4
  311.1 94.1 reduce-scatter.1

commit v3 on v2

--- a/solution.py
+++ b/solution.py
@@ -1,8 +1,64 @@
+import functools
+
 import jax
 import jax.numpy as jnp
 import numpy as np
 from jax import lax
+from jax.experimental import pallas as pl
+from jax.experimental.pallas import tpu as pltpu
 from jax.sharding import PartitionSpec as P
+
+MESH = pl.DeviceIdType.MESH
+
+
+def gather_kernel(parts, src_ref, out_ref, send_sem, recv_sem, local_sem):
+    me = lax.axis_index("chan")
+    row = lax.axis_index("seq")
+    width = src_ref.shape[1]
+    barrier = pltpu.get_barrier_semaphore()
+    for k in range(1, parts):
+        peer = lax.rem(me + k, parts)
+        pl.semaphore_signal(barrier, inc=1, device_id=(row, peer), device_id_type=MESH)
+    pl.semaphore_wait(barrier, parts - 1)
+    mine = pl.ds(pl.multiple_of(me * width, width), width)
+    local = pltpu.make_async_copy(src_ref, out_ref.at[:, mine], local_sem)
+    local.start()
+    copies = []
+    for k in range(1, parts):
+        peer = lax.rem(me + k, parts)
+        copy = pltpu.make_async_remote_copy(
+            src_ref=src_ref,
+            dst_ref=out_ref.at[:, mine],
+            send_sem=send_sem.at[k],
+            recv_sem=recv_sem.at[k],
+            device_id=(row, peer),
+            device_id_type=MESH,
+        )
+        copy.start()
+        copies.append(copy)
+    local.wait()
+    for copy in copies:
+        copy.wait()
+
+
+def gather_chan(block):
+    parts = lax.axis_size("chan")
+    rows, width = block.shape
+    return pl.pallas_call(
+        functools.partial(gather_kernel, parts),
+        out_shape=jax.ShapeDtypeStruct((rows, parts * width), block.dtype),
+        in_specs=[pl.BlockSpec(memory_space=pl.ANY)],
+        out_specs=pl.BlockSpec(memory_space=pl.ANY),
+        scratch_shapes=[
+            pltpu.SemaphoreType.DMA((parts,)),
+            pltpu.SemaphoreType.DMA((parts,)),
+            pltpu.SemaphoreType.DMA(()),
+        ],
+        compiler_params=pltpu.CompilerParams(collective_id=0, has_side_effects=True),
+        cost_estimate=pl.CostEstimate(
+            flops=0, transcendentals=0, bytes_accessed=2 * rows * parts * width * 2
+        ),
+    )(block)
 
 
 def lag_table(filters):
@@ -44,8 +100,9 @@
     row_count = tokens.shape[0]
     chan_count = in_weight.shape[2]
     length = filters.shape[1]
-    joined = jnp.concatenate([tokens, norm_gain[None, :]], axis=0)
-    whole_joined = lax.all_gather(joined, "chan", axis=1, tiled=True)
+    spare = jnp.zeros((15, tokens.shape[1]), tokens.dtype)
+    joined = jnp.concatenate([tokens, norm_gain[None, :], spare], axis=0)
+    whole_joined = gather_chan(joined)
     whole, gain_whole = whole_joined[:row_count], whole_joined[row_count]
     values = whole.astype(jnp.float32)
     mean_square = jnp.mean(values * values, axis=1, keepdims=True)

time: 415 us -> 497 us (1.20)
  Pallas kernels: 0 us -> 248 us
  waiting for transfers between devices: 306 us -> 140 us
    pallas_call x0 -> x1, Pallas kernels: none -> 248 us  [gather_chan(): pl.pallas_call(functools.partial(gather_kernel, parts), out_shape=jax.Sha...]
    all_gather x1, waiting for transfers between devices: 115 us -> 0.02 us  [local(): piece = lax.all_gather(in_weight, 'seq', axis=0, tiled=True)]
    all_gather x1 -> x0, waiting for transfers between devices: 96.5 us -> none  [local(): whole_joined = lax.all_gather(joined, 'chan', axis=1, tiled=True)]
    reduce_scatter x1, waiting for transfers between devices: 94.3 us -> 140 us  [local(): lax.psum_scatter(partial_out.astype(jnp.bfloat16), 'chan', scatter_dimens...]
    unnamed x20 -> x24, local copies, waits for them, and re-layouts: 10.9 us -> 11 us
  transfers between devices with their start and end apart: 4 -> 3, of which waited for: 3 -> 1; matrix products, arithmetic and copies ran while one was open for 7% -> 5% of each run, Pallas kernels for 0% -> 50%
where the time goes in v3:
time: 497 us; the launch traced here: 496 us
  Pallas kernels  248 us (50%)
  waiting for transfers between devices  140 us (28%)
  matrix products  43.5 us (9%)
  local copies, waits for them, and re-layouts  29.2 us (6%)
  other arithmetic  17.4 us (4%)
  between operations  13.7 us (3%)
    pallas_call x1, Pallas kernels, gather_chan(): pl.pallas_call(functools.partial(gather_kernel, parts), out_shape=jax.Sha...  248 us
    reduce_scatter x1, waiting for transfers between devices, local(): lax.psum_scatter(partial_out.astype(jnp.bfloat16), 'chan', scatter_dimens...  140 us
    dot_general x1, matrix products, local(): projected = jnp.dot(normed, panel, preferred_element_type=jnp.float32)  27.1 us
    dot_general x1, matrix products, local(): partial_out = jnp.dot(gated, out_weight, preferred_element_type=jnp.float32)  13.5 us
    unnamed x24, local copies, waits for them, and re-layouts  11 us
  transfers between devices with their start and end apart: 3, of which 1 were waited for; matrix products, arithmetic and copies ran while one was open for 5% of the time, Pallas kernels for 50%

profile of v3, /device:TPU:1, one launch (start us, length us, event | category | flops | bytes accessed | tf_op | source)
XLA Modules:
  0.0 496.1 jit_solution(15263401145014721933)
XLA Ops:
  6.5 4.7 copy.13
  11.5 1.2 maximum_maximum_fusion.src_ref
  12.6 247.9 %shard_map.64 = bf16[784,8192]{1,0:T(8,128)(2,1)} custom-call(bf16[784,512]{1,0:T(8,128)(2,1)} %maximum_maximum_fusion.src_ref), custom_call_target="tpu_custom_call" | custom-call | bytes 25690112 | tf_op jit(solution)/shard_map/pallas_call | solution.py:47
  260.6 7.1 %fusion = f32[768]{0:T(1024)S(1)} fusion(bf16[784,8192]{1,0:T(8,128)(2,1)} %shard_map.64), kind=kLoop, calls=%fused_computation.2 | loop fusion | flops 18873600 | bytes 12585984 | tf_op jit(solution)/shard_map/reduce_sum | solution.py:108
  267.7 0.9 slice_convert_fusion
  268.6 27.1 %fusion.10 = bf16[768,1536]{1,0:T(8,128)(2,1)S(1)} fusion(bf16[8192,1536]{0,1:T(8,128)(2,1)} %bitcast.49, f32[8192]{0:T(1024)S(1)} %bitcast.48, f32[768]{0:T(1024)S(1)} %add_rsqrt_fusion, bf16[784,8192]{1,0:T(8,128)(2,1)} %shard_map.64), kind=kOutput, calls=%fused_computation.15 | convolution fusion | flops 19353698304 | bytes 40143872 | tf_op jit(solution)/shard_map/dot_general | solution.py:114
  296.3 4.7 collective-permute-start
  301.0 1.4 fusion.25
  303.0 0.8 rev.3
  304.1 1.9 copy.24
  306.2 8.0 %reshape.39 = bf16[32,128,383]{2,1,0:T(8,128)(2,1)} reshape(bf16[32,49024]{1,0:T(8,128)(2,1)S(1)} %slice.90) | data formatting | bytes 6275072 | tf_op jit(solution)/shard_map/reshape | solution.py:70
  314.2 1.3 copy_bitcast_fusion
  315.6 2.8 copy.15
  318.4 1.3 copy.16
  319.7 1.3 maximum_convert_fusion
  321.1 4.5 fusion.8
  325.6 2.4 copy-done
  328.3 0.9 slice.73
  329.3 0.9 slice.75
  330.4 2.9 fusion.19
  333.2 0.6 copy.19
  333.9 13.5 %convolution_convert_fusion = bf16[768,8192]{1,0:T(8,128)(2,1)} fusion(bf16[512,8192]{1,0:T(8,128)(2,1)} %param.11, f32[64,8,6,128]{3,2,1,0:T(8,128)S(1)} %bitcast.43, f32[896,3,512]{0,2,1:T(8,128)S(1)} %bitcast.42), kind=kOutput, calls=%fused_computation.5 | convolution fusion | flops 6449528832 | bytes 24641536 | tf_op jit(solution)/shard_map/dot_general | solution.py:122
  347.4 139.7 %reduce-scatter.2.cloned.1.call-done = bf16[768,512]{1,0:T(8,128)(2,1)} async-done(((bf16[768,8192]{1,0:T(8,128)(2,1)}), bf16[768,512]{1,0:T(8,128)(2,1)}) %reduce-scatter.2.cloned.1.call-update) | async-done | bytes 786448 | tf_op jit(solution)/shard_map/reduce_scatter | solution.py:123
  487.1 2.2 add_convert_fusion
  (42 shorter events, 2.4 us)
Async XLA Ops:
  6.5 4.8 copy-start.7
  6.5 4.9 copy-start.2
  6.5 262.1 %all-gather.2.cloned.1.call-start = ((), (), s32[]{:S(2)}) async-start(), calls=%async_computation.1 | async-start | bytes 28311552 | tf_op jit(solution)/shard_map/all_gather | solution.py:112
  11.3 475.8 %reduce-scatter.2.cloned.1.call-start = ((), (), s32[]{:S(2)}) async-start(), calls=%async_computation.2 | async-start | bytes 13369344 | tf_op jit(solution)/shard_map/reduce_scatter | solution.py:123
  295.7 10.3 %copy-start.1 = (bf16[768,1536]{1,0:T(8,128)(2,1)}, bf16[768,1536]{1,0:T(8,128)(2,1)S(1)}, u32[]{:S(2)}) copy-start(bf16[768,1536]{1,0:T(8,128)(2,1)S(1)} %fusion.10) | copy-start | bytes 7077892
  296.3 22.1 %collective-permute-start = (bf16[130,3,512]{2,0,1:T(8,128)(2,1)S(1)}, bf16[130,3,512]{2,0,1:T(8,128)(2,1)}, u32[]{:S(2)}, u32[]{:S(2)}) collective-permute-start(bf16[130,3,512]{2,0,1:T(8,128)(2,1)S(1)} %copy.14), channel_id=1, source_target_pairs={{0,16},{16,32},{32,48},{48,64},{64,80},{80,96},{96,112},{1,17},{17... | collective-permute-start | bytes 1198088 | tf_op jit(solution)/shard_map/ppermute | solution.py:119
  318.4 2.6 copy-start.4
  318.4 2.6 copy-start.5
  318.4 2.6 copy-start.6
  325.6 2.4 copy-start
  330.2 3.7 slice-start
  330.4 3.5 slice-start.1
  347.4 139.7 %copy-start.3 = (bf16[768,512]{1,0:T(8,128)(2,1)S(1)}, bf16[768,512]{1,0:T(8,128)(2,1)}, u32[]{:S(2)}) copy-start(bf16[768,512]{1,0:T(8,128)(2,1)} %param.6) | copy-start | bytes 2359300
Sparse Core Ops, SparseCore 0:
  11.4 123.7 all-gather.1
  347.5 139.4 reduce-scatter.1

commit v4 on v2

--- a/solution.py
+++ b/solution.py
@@ -15,8 +15,8 @@
     return rows[:, :, length - 1 : 3 * length - 1]
 
 
-def hyena_core(extended, conv_weight, filters):
-    length = filters.shape[1]
+def hyena_core(extended, conv_weight, table):
+    length = table.shape[1]
     values = extended.astype(jnp.float32)
     weights = conv_weight.astype(jnp.float32)
     shaped = (
@@ -28,11 +28,10 @@
     out_rows = total - length
     query = shaped[length:, 0, :]
     mixed = (shaped[:, 1, :] * shaped[:, 2, :]).astype(jnp.bfloat16)
-    group_count = filters.shape[0]
+    group_count = table.shape[0]
     channel_count = mixed.shape[1]
     blocks = mixed.reshape(total // length, length, group_count, channel_count // group_count)
     paired = jnp.concatenate([blocks[:-1], blocks[1:]], axis=1)
-    table = lag_table(filters)
     filtered = jnp.einsum(
         "gts,bsgw->btgw", table, paired, preferred_element_type=jnp.float32
     )
@@ -46,27 +45,39 @@
     length = filters.shape[1]
     joined = jnp.concatenate([tokens, norm_gain[None, :]], axis=0)
     whole_joined = lax.all_gather(joined, "chan", axis=1, tiled=True)
+    table = lag_table(filters)
+    table, whole_joined = lax.optimization_barrier((table, whole_joined))
     whole, gain_whole = whole_joined[:row_count], whole_joined[row_count]
     values = whole.astype(jnp.float32)
     mean_square = jnp.mean(values * values, axis=1, keepdims=True)
     normed = (values * lax.rsqrt(mean_square + 1e-06) * gain_whole.astype(jnp.float32)).astype(
         jnp.bfloat16
     )
-    piece = lax.all_gather(in_weight, "seq", axis=0, tiled=True)
-    panel = piece.reshape(piece.shape[0], 3 * chan_count)
-    projected = jnp.dot(normed, panel, preferred_element_type=jnp.float32)
-    streams = projected.astype(jnp.bfloat16).reshape(row_count, 3, chan_count)
+    half = chan_count // 2
+    projected = []
+    for part in (in_weight[:, :, :half], in_weight[:, :, half:]):
+        piece = lax.all_gather(part, "seq", axis=0, tiled=True)
+        panel = piece.reshape(piece.shape[0], 3 * half)
+        product = jnp.dot(normed, panel, preferred_element_type=jnp.float32)
+        projected.append(product.astype(jnp.bfloat16).reshape(row_count, 3, half))
+    streams = jnp.concatenate(projected, axis=2)
     parts_count = lax.axis_size("seq")
     halo_rows = length + 2
     shift = [(i, i + 1) for i in range(parts_count - 1)]
     halo = lax.ppermute(streams[row_count - halo_rows :], "seq", shift)
     extended = jnp.concatenate([halo, streams], axis=0)
-    gated = hyena_core(extended, conv_weight, filters)
-    partial_out = jnp.dot(gated, out_weight, preferred_element_type=jnp.float32)
-    summed = lax.psum_scatter(
-        partial_out.astype(jnp.bfloat16), "chan", scatter_dimension=1, tiled=True
-    )
-    return (tokens.astype(jnp.float32) + summed.astype(jnp.float32)).astype(jnp.bfloat16)
+    rows_half = row_count // 2
+    results = []
+    for start in (0, rows_half):
+        window = extended[start : start + rows_half + halo_rows]
+        gated = hyena_core(window, conv_weight, table)
+        partial_out = jnp.dot(gated, out_weight, preferred_element_type=jnp.float32)
+        summed = lax.psum_scatter(
+            partial_out.astype(jnp.bfloat16), "chan", scatter_dimension=1, tiled=True
+        )
+        own = tokens[start : start + rows_half].astype(jnp.float32)
+        results.append((own + summed.astype(jnp.float32)).astype(jnp.bfloat16))
+    return jnp.concatenate(results, axis=0)
 
 
 def solution(mesh):

time: 415 us -> 479 us (1.15)
  waiting for transfers between devices: 306 us -> 355 us
  matrix products: 43.4 us -> 54.3 us
    reduce_scatter x1 -> x2, waiting for transfers between devices: 94.3 us -> 153 us  [local(): lax.psum_scatter(partial_out.astype(jnp.bfloat16), 'chan', scatter_dimens...]
    all_gather x1, waiting for transfers between devices: 96.5 us -> 81.9 us  [local(): whole_joined = lax.all_gather(joined, 'chan', axis=1, tiled=True)]
    dot_general x1 -> x2, matrix products: 13.5 us -> 19.6 us  [local(): partial_out = jnp.dot(gated, out_weight, preferred_element_type=jnp.float32)]
    dot_general x1 -> x2, matrix products: 27.1 us -> 33.1 us  [local(): product = jnp.dot(normed, panel, preferred_element_type=jnp.float32)]
    slice x0 -> x2, local copies, waits for them, and re-layouts: none -> 5.01 us  [the longest x1 2.93 us: lag_table(): return rows[:, :, length - 1:3 * length - 1]]
    ppermute x1, waiting for transfers between devices: 0.01 us -> 5 us  [local(): halo = lax.ppermute(streams[row_count - halo_rows:], 'seq', shift)]
    unnamed x20 -> x17, local copies, waits for them, and re-layouts: 10.9 us -> 9.04 us
    all_gather x1 -> x2, waiting for transfers between devices: 115 us -> 115 us  [local(): piece = lax.all_gather(part, 'seq', axis=0, tiled=True)]
  transfers between devices with their start and end apart: 4 -> 6, of which waited for: 3 -> 6; matrix products, arithmetic and copies ran while one was open for 7% -> 12% of each run, Pallas kernels for 0% -> 0%
where the time goes in v4:
time: 479 us; the launch traced here: 478 us
  waiting for transfers between devices  355 us (74%)
  matrix products  54.3 us (11%)
  local copies, waits for them, and re-layouts  29.4 us (6%)
  other arithmetic  22.7 us (5%)
  between operations  13.4 us (3%)
    reduce_scatter x2, waiting for transfers between devices, local(): lax.psum_scatter(partial_out.astype(jnp.bfloat16), 'chan', scatter_dimens...  153 us
    all_gather x2, waiting for transfers between devices, local(): piece = lax.all_gather(part, 'seq', axis=0, tiled=True)  115 us
    all_gather x1, waiting for transfers between devices, local(): whole_joined = lax.all_gather(joined, 'chan', axis=1, tiled=True)  81.9 us
    dot_general x2, matrix products, local(): product = jnp.dot(normed, panel, preferred_element_type=jnp.float32)  33.1 us
    dot_general x2, matrix products, local(): partial_out = jnp.dot(gated, out_weight, preferred_element_type=jnp.float32)  19.6 us
  transfers between devices with their start and end apart: 6, of which 6 were waited for; matrix products, arithmetic and copies ran while one was open for 12% of the time, Pallas kernels for 0%

profile of v4, /device:TPU:1, one launch (start us, length us, event | category | flops | bytes accessed | tf_op | source)
XLA Modules:
  0.0 477.8 jit_solution(1988895733347811839)
XLA Ops:
  7.2 2.1 pad_maximum_fusion.3
  9.4 2.1 fusion.43
  11.4 1.8 copy.30
  13.3 1.8 copy.29
  15.5 1.9 copy.31
  17.6 8.1 %reshape.54 = bf16[32,128,383]{2,1,0:T(8,128)(2,1)} reshape(bf16[32,49024]{1,0:T(8,128)(2,1)S(1)} %slice.144) | data formatting | bytes 6275072 | tf_op jit(solution)/shard_map/reshape | solution.py:14
  25.7 2.9 slice.145
  28.7 81.9 %all-gather.4.cloned.1.call-done = bf16[769,8192]{1,0:T(8,128)(2,1)} async-done(((bf16[769,512]{1,0:T(8,128)(2,1)}), bf16[769,8192]{1,0:T(8,128)(2,1)}) %all-gather.4.cloned.1.call-update) | async-done | bytes 12599312 | tf_op jit(solution)/shard_map/all_gather | solution.py:47
  110.6 7.1 %fusion = f32[768]{0:T(1024)S(1)} fusion(bf16[769,8192]{1,0:T(8,128)(2,1)} %all-gather.4.cloned.1.call-done), kind=kLoop, calls=%fused_computation.2 | loop fusion | flops 18873600 | bytes 12585984 | tf_op jit(solution)/shard_map/reduce_sum | solution.py:52
  118.6 61.9 %all-gather.8.cloned.1.call-done = bf16[8192,3,256]{0,2,1:T(8,128)(2,1)} async-done(((bf16[1024,3,256]{0,2,1:T(8,128)(2,1)}), bf16[8192,3,256]{0,2,1:T(8,128)(2,1)}) %all-gather.8.cloned.1.call-update) | async-done | bytes 12582928 | tf_op jit(solution)/shard_map/all_gather | solution.py:59
  180.6 16.6 %fusion.20 = bf16[768,768]{0,1:T(8,128)(2,1)S(1)} fusion(bf16[8192,768]{0,1:T(8,128)(2,1)} %bitcast.80, f32[8192]{0:T(1024)S(1)} %bitcast.78, f32[768]{0:T(1024)S(1)} %add_rsqrt_fusion, bf16[769,8192]{1,0:T(8,128)(2,1)} %all-gather.4.cloned.1.call-done), kind=kOutput, calls=%fused_computation.29 | convolution fusion | flops 9689432064 | bytes 26381312 | tf_op jit(solution)/shard_map/dot_general | solution.py:61
  197.1 52.8 %all-gather.6.cloned.1.call-done = bf16[8192,3,256]{0,2,1:T(8,128)(2,1)} async-done(((bf16[1024,3,256]{0,2,1:T(8,128)(2,1)}), bf16[8192,3,256]{0,2,1:T(8,128)(2,1)}) %all-gather.6.cloned.1.call-update) | async-done | bytes 12582928 | tf_op jit(solution)/shard_map/all_gather | solution.py:59
  249.9 16.6 %fusion.17 = bf16[768,768]{0,1:T(8,128)(2,1)S(1)} fusion(bf16[8192,768]{0,1:T(8,128)(2,1)} %bitcast.81, f32[8192]{0:T(1024)S(1)} %bitcast.79, f32[768]{0:T(1024)S(1)} %add_rsqrt_fusion, bf16[769,8192]{1,0:T(8,128)(2,1)} %all-gather.4.cloned.1.call-done), kind=kOutput, calls=%fused_computation.28 | convolution fusion | flops 9689432064 | bytes 26381312 | tf_op jit(solution)/shard_map/dot_general | solution.py:61
  268.8 2.1 copy.17
  270.9 2.9 collective-permute-start
  273.8 5.0 %collective-permute-done = bf16[130,3,512]{2,0,1:T(8,128)(2,1)} collective-permute-done((bf16[130,3,512]{2,0,1:T(8,128)(2,1)}, bf16[130,3,512]{2,0,1:T(8,128)(2,1)}, u32[]{:S(2)}, u32[]{:S(2)}) %collective-permute-start) | collective-permute-done | bytes 399392 | tf_op jit(solution)/shard_map/ppermute | solution.py:67
  278.8 2.2 copy.18
  281.0 3.1 fusion.16
  284.1 5.1 %fusion.5 = (f32[512,3,512]{0,2,1:T(8,128)S(1)}, f32[512,3,512]{0,2,1:T(8,128)}) fusion(f32[514,3,512]{0,2,1:T(8,128)S(1)} %get-tuple-element.11, f32[3,512]{1,0:T(4,128)S(1)} %get-tuple-element.24, f32[3,512]{1,0:T(4,128)S(1)} %get-tuple-element.25, f32[3,512]{1,0:T(4,128)S(1)} %bitcast.77, f32[514,3,512]{0,2,1:T(8,128)S(1)} %get-tuple-element.12), kind=kLoop, calls=%fused_computation.13 | loop fusion | flops 7864320 | bytes 25184256 | tf_op jit(solution)/shard_map/add | solution.py:23
  289.2 1.7 copy-done
  292.8 9.8 %convolution_convert_fusion.1 = bf16[384,8192]{1,0:T(8,128)(2,1)} fusion(bf16[512,8192]{1,0:T(8,128)(2,1)} %param.11, f32[64,8,3,128]{3,2,1,0:T(4,128)S(1)} %bitcast.75, f32[512,3,512]{0,2,1:T(8,128)} %copy-done), kind=kOutput, calls=%fused_computation.6 | convolution fusion | flops 3224764416 | bytes 16252928 | tf_op jit(solution)/shard_map/dot_general | solution.py:74
  306.3 9.8 %convolution_convert_fusion = bf16[384,8192]{1,0:T(8,128)(2,1)} fusion(bf16[512,8192]{1,0:T(8,128)(2,1)} %param.11, f32[64,8,3,128]{3,2,1,0:T(4,128)S(1)} %bitcast.76, f32[512,3,512]{0,2,1:T(8,128)} %get-tuple-element.20), kind=kOutput, calls=%fused_computation.5 | convolution fusion | flops 3224764416 | bytes 16252928 | tf_op jit(solution)/shard_map/dot_general | solution.py:74
  316.1 68.5 %reduce-scatter.3.cloned.1.call-done = bf16[384,512]{1,0:T(8,128)(2,1)} async-done(((bf16[384,8192]{1,0:T(8,128)(2,1)}), bf16[384,512]{1,0:T(8,128)(2,1)}) %reduce-scatter.3.cloned.1.call-update) | async-done | bytes 393232 | tf_op jit(solution)/shard_map/reduce_scatter | solution.py:75
  384.6 84.4 %reduce-scatter.5.cloned.1.call-done = bf16[384,512]{1,0:T(8,128)(2,1)} async-done(((bf16[384,8192]{1,0:T(8,128)(2,1)}), bf16[384,512]{1,0:T(8,128)(2,1)}) %reduce-scatter.5.cloned.1.call-update) | async-done | bytes 393232 | tf_op jit(solution)/shard_map/reduce_scatter | solution.py:75
  (51 shorter events, 12.4 us)
Async XLA Ops:
  6.5 104.1 %all-gather.4.cloned.1.call-start = ((), (), s32[]{:S(2)}) async-start(), calls=%async_computation.2 | async-start | bytes 13508608 | tf_op jit(solution)/shard_map/all_gather | solution.py:47
  9.3 171.3 %all-gather.8.cloned.1.call-start = ((), (), s32[]{:S(2)}) async-start(), calls=%async_computation.4 | async-start | bytes 14155776 | tf_op jit(solution)/shard_map/all_gather | solution.py:59
  13.2 1.9 copy-start.4
  13.2 236.7 %all-gather.6.cloned.1.call-start = ((), (), s32[]{:S(2)}) async-start(), calls=%async_computation.3 | async-start | bytes 14155776 | tf_op jit(solution)/shard_map/all_gather | solution.py:59
  15.1 369.5 %reduce-scatter.3.cloned.1.call-start = ((), (), s32[]{:S(2)}) async-start(), calls=%async_computation.5 | async-start | bytes 6684672 | tf_op jit(solution)/shard_map/reduce_scatter | solution.py:75
  266.5 1.0 copy-start.1
  266.5 7.3 %copy-start.3 = (bf16[3,3,512]{2,1,0:T(4,128)(2,1)S(1)}, bf16[3,3,512]{2,1,0:T(4,128)(2,1)}, u32[]{:S(2)}) copy-start(bf16[3,3,512]{2,1,0:T(4,128)(2,1)} %param.9) | copy-start | bytes 27652
  270.9 7.9 %collective-permute-start = (bf16[130,3,512]{2,0,1:T(8,128)(2,1)}, bf16[130,3,512]{2,0,1:T(8,128)(2,1)}, u32[]{:S(2)}, u32[]{:S(2)}) collective-permute-start(bf16[130,3,512]{2,0,1:T(8,128)(2,1)} %copy.17), channel_id=1, source_target_pairs={{0,16},{16,32},{32,48},{48,64},{64,80},{80,96},{96,112},{1,17},{17... | collective-permute-start | bytes 1198088 | tf_op jit(solution)/shard_map/ppermute | solution.py:67
  289.2 1.7 copy-start
  302.6 166.4 %reduce-scatter.5.cloned.1.call-start = ((), (), s32[]{:S(2)}) async-start(), calls=%async_computation.6 | async-start | bytes 6684672 | tf_op jit(solution)/shard_map/reduce_scatter | solution.py:75
  316.1 152.9 %copy-start.2 = (bf16[768,512]{1,0:T(8,128)(2,1)S(1)}, bf16[768,512]{1,0:T(8,128)(2,1)}, u32[]{:S(2)}) copy-start(bf16[768,512]{1,0:T(8,128)(2,1)} %param.6) | copy-start | bytes 2359300
  470.3 0.9 copy-start.5
Sparse Core Ops, SparseCore 0:
  9.4 101.1 all-gather.3
  112.3 68.2 all-gather.7
  182.3 67.6 all-gather.5
  302.7 81.8 reduce-scatter.2
  387.9 81.0 reduce-scatter.4

commit v5 on v2

v5 whole, which is shorter than its diff:
```python
import jax
import jax.numpy as jnp
import numpy as np
from jax import lax
from jax.sharding import Mesh, PartitionSpec as P


def lag_table(filters):
    groups, length = filters.shape
    width = 3 * length
    zeros = jnp.zeros((groups, length), filters.dtype)
    skew = jnp.concatenate([zeros, filters[:, ::-1], zeros], axis=1)
    tiled = jnp.tile(skew, (1, length))[:, : length * (width - 1)]
    rows = tiled.reshape(groups, length, width - 1)
    return rows[:, :, length - 1 : 3 * length - 1]


def hyena_core(extended, conv_weight, table):
    length = table.shape[1]
    values = extended.astype(jnp.float32)
    weights = conv_weight.astype(jnp.float32)
    shaped = (
        weights[:, 0, :] * values[2:]
        + weights[:, 1, :] * values[1:-1]
        + weights[:, 2, :] * values[:-2]
    )
    total = shaped.shape[0]
    out_rows = total - length
    query = shaped[length:, 0, :]
    mixed = (shaped[:, 1, :] * shaped[:, 2, :]).astype(jnp.bfloat16)
    group_count = table.shape[0]
    channel_count = mixed.shape[1]
    blocks = mixed.reshape(total // length, length, group_count, channel_count // group_count)
    paired = jnp.concatenate([blocks[:-1], blocks[1:]], axis=1)
    filtered = jnp.einsum(
        "gts,bsgw->btgw", table, paired, preferred_element_type=jnp.float32
    )
    filtered = filtered.reshape(out_rows, channel_count)
    return (query * filtered).astype(jnp.bfloat16)


def local(tokens, norm_gain, in_weight, conv_weight, filters, out_weight):
    row_count = tokens.shape[0]
    depth, _, chan_count = in_weight.shape
    length = filters.shape[1]
    joined = jnp.concatenate([tokens, norm_gain[None, :]], axis=0)
    whole_joined = lax.all_gather(joined, "chan", axis=1, tiled=True)
    table = lag_table(filters)
    table, whole_joined = lax.optimization_barrier((table, whole_joined))
    whole, gain_whole = whole_joined[:row_count], whole_joined[row_count]
    values = whole.astype(jnp.float32)
    mean_square = jnp.mean(values * values, axis=1, keepdims=True)
    normed = (values * lax.rsqrt(mean_square + 1e-06) * gain_whole.astype(jnp.float32)).astype(
        jnp.bfloat16
    )
    x_count = lax.axis_size("x")
    x_me = lax.axis_index("x")
    core_me = lax.axis_index("core")
    own = [in_weight]
    for k in range(1, x_count):
        own.append(lax.ppermute(in_weight, "x", [(i, (i + k) % x_count) for i in range(x_count)]))
    mine = jnp.stack(own)
    other = lax.ppermute(mine, "core", [(0, 1), (1, 0)])
    projected = None
    for parity, blocks in ((core_me, mine), (1 - core_me, other)):
        for k in range(x_count):
            owner = 2 * lax.rem(x_me - k + x_count, x_count) + parity
            rows = lax.dynamic_slice_in_dim(normed, owner * depth, depth, axis=1)
            panel = blocks[k].reshape(depth, 3 * chan_count)
            term = jnp.dot(rows, panel, preferred_element_type=jnp.float32)
            projected = term if projected is None else projected + term
    streams = projected.astype(jnp.bfloat16).reshape(row_count, 3, chan_count)
    parts_count = lax.axis_size(SEQ)
    halo_rows = length + 2
    shift = [(i, i + 1) for i in range(parts_count - 1)]
    halo = lax.ppermute(streams[row_count - halo_rows :], SEQ, shift)
    extended = jnp.concatenate([halo, streams], axis=0)
    gated = hyena_core(extended, conv_weight, table)
    partial_out = jnp.dot(gated, out_weight, preferred_element_type=jnp.float32)
    summed = lax.psum_scatter(
        partial_out.astype(jnp.bfloat16), "chan", scatter_dimension=1, tiled=True
    )
    return (tokens.astype(jnp.float32) + summed.astype(jnp.float32)).astype(jnp.bfloat16)


SEQ = ("x", "core")


def solution(mesh):
    seq_count, chan_count = mesh.devices.shape
    split = Mesh(mesh.devices.reshape(seq_count // 2, 2, chan_count), ("x", "core", "chan"))
    return jax.shard_map(
        local,
        mesh=split,
        in_specs=(
            P(SEQ, "chan"),
            P("chan"),
            P(SEQ, None, "chan"),
            P(None, None, "chan"),
            P("chan", None),
            P("chan", None),
        ),
        out_specs=P(SEQ, "chan"),
        check_vma=False,
    )
```

time: 415 us -> 397 us (0.957)
  waiting for transfers between devices: 306 us -> 239 us
  matrix products: 43.4 us -> 59.4 us
  local copies, waits for them, and re-layouts: 29.7 us -> 44.8 us
  other arithmetic: 18.3 us -> 31.9 us
    ppermute x1 -> x5, waiting for transfers between devices: 0.01 us -> 141 us  [the longest x3 138 us: local(): lax.ppermute(in_weight, 'x', [(i, (i + k) % x_count) for i in range(x_cou...]
    all_gather x1 -> x0, waiting for transfers between devices: 115 us -> none  [local(): piece = lax.all_gather(in_weight, 'seq', axis=0, tiled=True)]
    all_gather x1, waiting for transfers between devices: 96.5 us -> 0.01 us  [local(): whole_joined = lax.all_gather(joined, 'chan', axis=1, tiled=True)]
    dot_general x1 -> x8, matrix products: 27.1 us -> 44.1 us  [local(): term = jnp.dot(rows, panel, preferred_element_type=jnp.float32)]
    slice x3 -> x5, local copies, waits for them, and re-layouts: 0.5 us -> 13.9 us  [the longest x1 8.17 us: local(): panel = blocks[k].reshape(depth, 3 * chan_count)]
    convert_element_type x0 -> x1, other arithmetic: none -> 7.62 us  [local(): (values * lax.rsqrt(mean_square + 1e-06) * gain_whole.astype(jnp.float32)...]
    another operation x0 -> x1, other arithmetic: none -> 5.99 us  [local(): mine = jnp.stack(own)]
    slice x5, local copies, waits for them, and re-layouts: 2.14 us -> 6.52 us  [hyena_core(): paired = jnp.concatenate([blocks[:-1], blocks[1:]], axis=1)]
  transfers between devices with their start and end apart: 4 -> 7, of which waited for: 3 -> 6; matrix products, arithmetic and copies ran while one was open for 7% -> 10% of each run, Pallas kernels for 0% -> 0%
where the time goes in v5:
time: 397 us; the launch traced here: 396 us
  waiting for transfers between devices  239 us (60%)
  matrix products  59.4 us (15%)
  local copies, waits for them, and re-layouts  44.8 us (11%)
  other arithmetic  31.9 us (8%)
  between operations  13.7 us (3%)
  starting transfers between devices  7.03 us (2%)
    ppermute x3, waiting for transfers between devices, local(): lax.ppermute(in_weight, 'x', [(i, (i + k) % x_count) for i in range(x_cou...  138 us
    reduce_scatter x1, waiting for transfers between devices, local(): lax.psum_scatter(partial_out.astype(jnp.bfloat16), 'chan', scatter_dimens...  98 us
    dot_general x8, matrix products, local(): term = jnp.dot(rows, panel, preferred_element_type=jnp.float32)  44.1 us
    dot_general x1, matrix products, local(): partial_out = jnp.dot(gated, out_weight, preferred_element_type=jnp.float32)  13.3 us
    reshape x1, local copies, waits for them, and re-layouts, lag_table(): rows = tiled.reshape(groups, length, width - 1)  9.24 us
    slice x1, local copies, waits for them, and re-layouts, local(): panel = blocks[k].reshape(depth, 3 * chan_count)  8.17 us
  transfers between devices with their start and end apart: 7, of which 6 were waited for; matrix products, arithmetic and copies ran while one was open for 10% of the time, Pallas kernels for 0%

profile of v5, /device:TPU:1, one launch (start us, length us, event | category | flops | bytes accessed | tf_op | source)
XLA Modules:
  0.0 396.3 jit_solution(367107769385361240)
XLA Ops:
  9.4 3.2 copy.17
  12.6 3.4 collective-permute-start.2
  17.0 66.8 %collective-permute-done.2 = bf16[1024,3,512]{0,2,1:T(8,128)(2,1)S(1)} collective-permute-done((bf16[1024,3,512]{0,2,1:T(8,128)(2,1)S(1)}, bf16[1024,3,512]{0,2,1:T(8,128)(2,1)S(1)}, u32[]{:S(2)}, u32[]{:S(2)}) %collective-permute-start.2) | collective-permute-done | bytes 3145760 | tf_op jit(solution)/shard_map/ppermute | solution.py:61
  83.8 2.3 collective-permute-done.1
  86.2 68.7 %collective-permute-done = bf16[1024,3,512]{0,2,1:T(8,128)(2,1)S(1)} collective-permute-done((bf16[1024,3,512]{0,2,1:T(8,128)(2,1)S(1)}, bf16[1024,3,512]{0,2,1:T(8,128)(2,1)S(1)}, u32[]{:S(2)}, u32[]{:S(2)}) %collective-permute-start) | collective-permute-done | bytes 3145760 | tf_op jit(solution)/shard_map/ppermute | solution.py:61
  154.9 6.0 %pad_maximum_fusion = bf16[4,1024,3,512]{1,3,2,0:T(8,128)(2,1)} fusion(bf16[1,1024,3,512]{1,3,2,0:T(8,128)(2,1)S(1)} %bitcast.70, bf16[1,1024,3,512]{1,3,2,0:T(8,128)(2,1)S(1)} %bitcast.72, bf16[1,1024,3,512]{1,3,2,0:T(8,128)(2,1)S(1)} %bitcast.68, bf16[1,1024,3,512]{1,3,2,0:T(8,128)(2,1)S(1)} %bitcast.62), kind=kLoop, calls=%fused_computation.6 | loop fusion | flops 18874368 | bytes 25165824 | tf_op jit(solution)/shard_map/stack | solution.py:62
  165.6 9.2 %reshape.34 = bf16[32,128,383]{2,1,0:T(8,128)(2,1)} reshape(bf16[32,49024]{1,0:T(8,128)(2,1)} %slice.95) | data formatting | bytes 6275072 | tf_op jit(solution)/shard_map/reshape | solution.py:14
  174.8 4.3 %slice.96 = bf16[32,128,256]{2,1,0:T(8,128)(2,1)} slice(bf16[32,128,383]{2,1,0:T(8,128)(2,1)} %reshape.34), slice={[0:32], [0:128], [127:383]} | slice | bytes 4194304 | tf_op jit(solution)/shard_map/slice | solution.py:15
  180.6 8.2 %fusion.45 = (bf16[1,1024,3,512]{1,3,2,0:T(8,128)(2,1)}, bf16[1,1024,3,512]{1,3,2,0:T(8,128)(2,1)}, bf16[1,1024,3,512]{1,3,2,0:T(8,128)(2,1)}, bf16[1,1024,3,512]{1,3,2,0:T(8,128)(2,1)}) fusion(bf16[4,1024,3,512]{1,3,2,0:T(8,128)(2,1)} %collective-permute-done.3), kind=kLoop, calls=%fused_computation.58 | loop fusion | bytes 25165824 | tf_op jit(solution)/shard_map/slice | solution.py:69
  189.7 7.1 %fusion = f32[768]{0:T(1024)S(1)} fusion(bf16[769,8192]{1,0:T(8,128)(2,1)} %all-gather.2.cloned.1.call-done), kind=kLoop, calls=%fused_computation.2 | loop fusion | flops 18873600 | bytes 12585984 | tf_op jit(solution)/shard_map/reduce_sum | solution.py:52
  196.8 7.6 %fusion.2 = bf16[768,8192]{1,0:T(8,128)(2,1)S(1)} fusion(f32[8192]{0:T(1024)S(1)} %bitcast.77, f32[768]{0:T(1024)S(1)} %add_rsqrt_fusion, bf16[769,8192]{1,0:T(8,128)(2,1)} %all-gather.2.cloned.1.call-done), kind=kLoop, calls=%fused_computation.4 | loop fusion | flops 25165824 | bytes 25201664 | tf_op jit(solution)/shard_map/convert_element_type | solution.py:53
  204.4 4.3 %fusion.16 = f32[768,1536]{1,0:T(8,128)} fusion(bf16[1024,1536]{0,1:T(8,128)(2,1)S(1)} %bitcast.76, bf16[768,8192]{1,0:T(8,128)(2,1)S(1)} %fusion.2, s32[]{:T(128)S(6)} %select_n.30), kind=kOutput, calls=%fused_computation.27 | convolution fusion | flops 2415919104 | bytes 9437188 | tf_op jit(solution)/shard_map/dot_general | solution.py:70
  208.8 4.3 %fusion.18 = f32[768,1536]{1,0:T(8,128)} fusion(bf16[1024,1536]{0,1:T(8,128)(2,1)S(1)} %bitcast.75, bf16[768,8192]{1,0:T(8,128)(2,1)S(1)} %fusion.2, s32[]{:T(128)S(6)} %select_n.29), kind=kOutput, calls=%fused_computation.29 | convolution fusion | flops 2415919104 | bytes 9437188 | tf_op jit(solution)/shard_map/dot_general | solution.py:70
  213.1 4.3 %fusion.20 = f32[768,1536]{1,0:T(8,128)} fusion(bf16[1024,1536]{0,1:T(8,128)(2,1)S(1)} %bitcast.74, bf16[768,8192]{1,0:T(8,128)(2,1)S(1)} %fusion.2, s32[]{:T(128)S(6)} %select_n.28), kind=kOutput, calls=%fused_computation.31 | convolution fusion | flops 2415919104 | bytes 9437188 | tf_op jit(solution)/shard_map/dot_general | solution.py:70
  217.4 4.3 %fusion.22 = f32[768,1536]{1,0:T(8,128)} fusion(bf16[1024,1536]{0,1:T(8,128)(2,1)S(1)} %bitcast.71, bf16[768,8192]{1,0:T(8,128)(2,1)S(1)} %fusion.2, s32[]{:T(128)S(6)} %select_n.27), kind=kOutput, calls=%fused_computation.33 | convolution fusion | flops 2415919104 | bytes 9437188 | tf_op jit(solution)/shard_map/dot_general | solution.py:70
  221.7 4.4 %fusion.24 = f32[768,1536]{1,0:T(8,128)} fusion(bf16[1024,1536]{0,1:T(8,128)(2,1)S(1)} %bitcast.73, bf16[768,8192]{1,0:T(8,128)(2,1)S(1)} %fusion.2, s32[]{:T(128)S(6)} %select_n.26), kind=kOutput, calls=%fused_computation.35 | convolution fusion | flops 2415919104 | bytes 9437188 | tf_op jit(solution)/shard_map/dot_general | solution.py:70
  226.1 4.3 %fusion.28 = f32[768,1536]{1,0:T(8,128)} fusion(bf16[1024,1536]{0,1:T(8,128)(2,1)S(1)} %bitcast.63, bf16[768,8192]{1,0:T(8,128)(2,1)S(1)} %fusion.2, s32[]{:T(128)S(6)} %select_n.24), kind=kOutput, calls=%fused_computation.39 | convolution fusion | flops 2415919104 | bytes 9437188 | tf_op jit(solution)/shard_map/dot_general | solution.py:70
  230.4 4.3 %fusion.26 = f32[768,1536]{1,0:T(8,128)} fusion(bf16[1024,1536]{0,1:T(8,128)(2,1)S(1)} %bitcast.69, bf16[768,8192]{1,0:T(8,128)(2,1)S(1)} %fusion.2, s32[]{:T(128)S(6)} %select_n.25), kind=kOutput, calls=%fused_computation.37 | convolution fusion | flops 2415919104 | bytes 9437188 | tf_op jit(solution)/shard_map/dot_general | solution.py:70
  234.8 13.8 %add_convert_fusion = bf16[768,1536]{1,0:T(8,128)(2,1)} fusion(f32[768,1536]{1,0:T(8,128)} %fusion.16, f32[768,1536]{1,0:T(8,128)} %fusion.18, f32[768,1536]{1,0:T(8,128)} %fusion.20, f32[768,1536]{1,0:T(8,128)} %fusion.22, f32[768,1536]{1,0:T(8,128)} %fusion.24, f32[768,1536]{1,0:T(8,128)} %fusion.28, f32[768,1536]{1,0:T(8,128)} %fusion.26, ...), kind=kOutput, calls=%fused_computation.12 | convolution fusion | flops 2425356288 | bytes 40108036 | tf_op jit(solution)/shard_map/dot_general | solution.py:70
  252.1 2.8 copy.23
  259.6 4.5 %fusion.3 = f32[896,3,512]{0,2,1:T(8,128)S(1)} fusion(f32[898,3,512]{0,2,1:T(8,128)S(1)} %maximum_convert_fusion, f32[3,512]{1,0:T(4,128)S(1)} %get-tuple-element.18, f32[3,512]{1,0:T(4,128)S(1)} %get-tuple-element.19, f32[3,512]{1,0:T(4,128)S(1)} %bitcast.78), kind=kLoop, calls=%fused_computation.8 | loop fusion | flops 6881280 | bytes 22038528 | tf_op jit(solution)/shard_map/add | solution.py:23
  264.1 2.3 copy-done
  275.9 13.3 %convolution_convert_fusion = bf16[768,8192]{1,0:T(8,128)(2,1)} fusion(bf16[512,8192]{1,0:T(8,128)(2,1)} %param.11, f32[64,8,6,128]{3,2,1,0:T(8,128)S(1)} %bitcast.61, f32[896,3,512]{0,2,1:T(8,128)S(1)} %bitcast.60), kind=kOutput, calls=%fused_computation.5 | convolution fusion | flops 6449528832 | bytes 24641536 | tf_op jit(solution)/shard_map/dot_general | solution.py:79
  289.2 98.0 %reduce-scatter.2.cloned.1.call-done = bf16[768,512]{1,0:T(8,128)(2,1)} async-done(((bf16[768,8192]{1,0:T(8,128)(2,1)}), bf16[768,512]{1,0:T(8,128)(2,1)}) %reduce-scatter.2.cloned.1.call-update) | async-done | bytes 786448 | tf_op jit(solution)/shard_map/reduce_scatter | solution.py:80
  (74 shorter events, 30.8 us)
Async XLA Ops:
  6.5 182.2 %all-gather.2.cloned.1.call-start = ((), (), s32[]{:S(2)}) async-start(), calls=%async_computation.1 | async-start | bytes 13508608 | tf_op jit(solution)/shard_map/all_gather | solution.py:47
  9.3 377.9 %reduce-scatter.2.cloned.1.call-start = ((), (), s32[]{:S(2)}) async-start(), calls=%async_computation.2 | async-start | bytes 13369344 | tf_op jit(solution)/shard_map/reduce_scatter | solution.py:80
  12.6 71.3 %collective-permute-start.2 = (bf16[1024,3,512]{0,2,1:T(8,128)(2,1)S(1)}, bf16[1024,3,512]{0,2,1:T(8,128)(2,1)S(1)}, u32[]{:S(2)}, u32[]{:S(2)}) collective-permute-start(bf16[1024,3,512]{0,2,1:T(8,128)(2,1)S(1)} %copy.17), channel_id=1, source_target_pairs={{0,96},{32,0},{64,32},{96,64},{1,97},{33,1},{65,33},{97,65},{2,98}... | collective-permute-start | bytes 9437192 | tf_op jit(solution)/shard_map/ppermute | solution.py:61
  15.9 70.3 %collective-permute-start.1 = (bf16[1024,3,512]{0,2,1:T(8,128)(2,1)S(1)}, bf16[1024,3,512]{0,2,1:T(8,128)(2,1)S(1)}, u32[]{:S(2)}, u32[]{:S(2)}) collective-permute-start(bf16[1024,3,512]{0,2,1:T(8,128)(2,1)S(1)} %copy.17), channel_id=1, source_target_pairs={{0,64},{32,96},{64,0},{96,32},{1,65},{33,97},{65,1},{97,33},{2,66}... | collective-permute-start | bytes 9437192 | tf_op jit(solution)/shard_map/ppermute | solution.py:61
  16.4 138.4 %collective-permute-start = (bf16[1024,3,512]{0,2,1:T(8,128)(2,1)S(1)}, bf16[1024,3,512]{0,2,1:T(8,128)(2,1)S(1)}, u32[]{:S(2)}, u32[]{:S(2)}) collective-permute-start(bf16[1024,3,512]{0,2,1:T(8,128)(2,1)S(1)} %copy.17), channel_id=1, source_target_pairs={{0,32},{32,64},{64,96},{96,0},{1,33},{33,65},{65,97},{97,1},{2,34}... | collective-permute-start | bytes 9437192 | tf_op jit(solution)/shard_map/ppermute | solution.py:61
  83.8 77.0 %copy-start.6 = (bf16[1024,3,512]{0,2,1:T(8,128)(2,1)}, bf16[1024,3,512]{0,2,1:T(8,128)(2,1)S(1)}, u32[]{:S(2)}) copy-start(bf16[1024,3,512]{0,2,1:T(8,128)(2,1)S(1)} %collective-permute-done.2) | copy-start | bytes 9437188
  86.2 74.7 %copy-start.8 = (bf16[1024,3,512]{0,2,1:T(8,128)(2,1)}, bf16[1024,3,512]{0,2,1:T(8,128)(2,1)S(1)}, u32[]{:S(2)}) copy-start(bf16[1024,3,512]{0,2,1:T(8,128)(2,1)S(1)} %collective-permute-done.1) | copy-start | bytes 9437188
  154.9 6.0 %copy-start.4 = (bf16[1024,3,512]{0,2,1:T(8,128)(2,1)}, bf16[1024,3,512]{0,2,1:T(8,128)(2,1)S(1)}, u32[]{:S(2)}) copy-start(bf16[1024,3,512]{0,2,1:T(8,128)(2,1)S(1)} %collective-permute-done) | copy-start | bytes 9437188
  154.9 6.6 %copy-start.15 = (bf16[32,128]{1,0:T(8,128)(2,1)S(1)}, bf16[32,128]{1,0:T(8,128)(2,1)}, u32[]{:S(2)}) copy-start(bf16[32,128]{1,0:T(8,128)(2,1)} %param.10) | copy-start | bytes 24580
  160.9 19.7 %collective-permute-start.3 = (bf16[4,1024,3,512]{1,3,2,0:T(8,128)(2,1)}, bf16[4,1024,3,512]{1,3,2,0:T(8,128)(2,1)}, u32[]{:S(2)}, u32[]{:S(2)}) collective-permute-start(bf16[4,1024,3,512]{1,3,2,0:T(8,128)(2,1)} %pad_maximum_fusion), channel_id=1, source_target_pairs={{0,16},{16,0},{1,17},{17,1},{2,18},{18,2},{3,19},{19,3},{4,20},{20... | collective-permute-start | bytes 37748744 | tf_op jit(solution)/shard_map/ppermute | solution.py:63
  196.8 7.7 %copy-start.12 = (bf16[1,1024,3,512]{1,3,2,0:T(8,128)(2,1)S(1)}, bf16[1,1024,3,512]{1,3,2,0:T(8,128)(2,1)}, u32[]{:S(2)}) copy-start(bf16[1,1024,3,512]{1,3,2,0:T(8,128)(2,1)} %get-tuple-element.10) | copy-start | bytes 9437188
  204.4 26.0 %copy-start.1 = (bf16[768,8192]{1,0:T(8,128)(2,1)}, bf16[768,8192]{1,0:T(8,128)(2,1)S(1)}, u32[]{:S(2)}) copy-start(bf16[768,8192]{1,0:T(8,128)(2,1)S(1)} %fusion.2) | copy-start | bytes 37748740
  204.4 4.4 %copy-start.11 = (bf16[1,1024,3,512]{1,3,2,0:T(8,128)(2,1)S(1)}, bf16[1,1024,3,512]{1,3,2,0:T(8,128)(2,1)}, u32[]{:S(2)}) copy-start(bf16[1,1024,3,512]{1,3,2,0:T(8,128)(2,1)} %get-tuple-element.11) | copy-start | bytes 9437188
  208.8 4.3 %copy-start.10 = (bf16[1,1024,3,512]{1,3,2,0:T(8,128)(2,1)S(1)}, bf16[1,1024,3,512]{1,3,2,0:T(8,128)(2,1)}, u32[]{:S(2)}) copy-start(bf16[1,1024,3,512]{1,3,2,0:T(8,128)(2,1)} %get-tuple-element.12) | copy-start | bytes 9437188
  213.1 4.3 %copy-start.7 = (bf16[1024,3,512]{0,2,1:T(8,128)(2,1)S(1)}, bf16[1024,3,512]{0,2,1:T(8,128)(2,1)}, u32[]{:S(2)}) copy-start(bf16[1024,3,512]{0,2,1:T(8,128)(2,1)} %copy-done.6) | copy-start | bytes 9437188
  217.4 4.3 %copy-start.9 = (bf16[1024,3,512]{0,2,1:T(8,128)(2,1)S(1)}, bf16[1024,3,512]{0,2,1:T(8,128)(2,1)}, u32[]{:S(2)}) copy-start(bf16[1024,3,512]{0,2,1:T(8,128)(2,1)} %copy-done.8) | copy-start | bytes 9437188
  226.1 4.3 %copy-start.5 = (bf16[1024,3,512]{0,2,1:T(8,128)(2,1)S(1)}, bf16[1024,3,512]{0,2,1:T(8,128)(2,1)}, u32[]{:S(2)}) copy-start(bf16[1024,3,512]{0,2,1:T(8,128)(2,1)} %copy-done.4) | copy-start | bytes 9437188
  230.4 4.3 %copy-start.2 = (bf16[1,1024,3,512]{1,3,2,0:T(8,128)(2,1)S(1)}, bf16[1,1024,3,512]{1,3,2,0:T(8,128)(2,1)}, u32[]{:S(2)}) copy-start(bf16[1,1024,3,512]{1,3,2,0:T(8,128)(2,1)} %get-tuple-element.9) | copy-start | bytes 9437188
  234.8 17.2 %copy-start.14 = (bf16[3,3,512]{2,1,0:T(4,128)(2,1)S(1)}, bf16[3,3,512]{2,1,0:T(4,128)(2,1)}, u32[]{:S(2)}) copy-start(bf16[3,3,512]{2,1,0:T(4,128)(2,1)} %param.9) | copy-start | bytes 27652
  250.1 6.9 %collective-permute-start.4 = (bf16[130,3,512]{2,0,1:T(8,128)(2,1)S(1)}, bf16[130,3,512]{2,0,1:T(8,128)(2,1)}, u32[]{:S(2)}, u32[]{:S(2)}) collective-permute-start(bf16[130,3,512]{2,0,1:T(8,128)(2,1)S(1)} %copy.22), channel_id=1, source_target_pairs={{0,16},{16,32},{32,48},{48,64},{64,80},{80,96},{96,112},{1,17},{17... | collective-permute-start | bytes 1198088 | tf_op jit(solution)/shard_map/ppermute | solution.py:76
  266.6 6.6 %copy-start.3 = (bf16[32,128,256]{2,1,0:T(8,128)(2,1)S(1)}, bf16[32,128,256]{2,1,0:T(8,128)(2,1)}, u32[]{:S(2)}) copy-start(bf16[32,128,256]{2,1,0:T(8,128)(2,1)} %slice.96) | copy-start | bytes 6291460
  273.0 2.9 slice-start
  273.2 2.7 slice-start.1
  289.2 98.0 %copy-start.13 = (bf16[768,512]{1,0:T(8,128)(2,1)S(1)}, bf16[768,512]{1,0:T(8,128)(2,1)}, u32[]{:S(2)}) copy-start(bf16[768,512]{1,0:T(8,128)(2,1)} %param.6) | copy-start | bytes 2359300
  (1 other events, 2.3 us)
Sparse Core Ops, SparseCore 0:
  9.4 101.1 all-gather.1
  289.3 97.8 reduce-scatter.1

commit v6 on v5

--- a/solution.py
+++ b/solution.py
@@ -53,23 +53,43 @@
     normed = (values * lax.rsqrt(mean_square + 1e-06) * gain_whole.astype(jnp.float32)).astype(
         jnp.bfloat16
     )
+    quarter = chan_count // 4
+    rest = chan_count - quarter
+    direct = in_weight[:, :, :quarter]
+    direct, whole_joined = lax.optimization_barrier((direct, whole_joined))
+    direct_whole = lax.all_gather(direct, SEQ, axis=0, tiled=True)
+    moved = in_weight[:, :, quarter:]
     x_count = lax.axis_size("x")
     x_me = lax.axis_index("x")
     core_me = lax.axis_index("core")
-    own = [in_weight]
+    own = [moved]
     for k in range(1, x_count):
-        own.append(lax.ppermute(in_weight, "x", [(i, (i + k) % x_count) for i in range(x_count)]))
+        own.append(lax.ppermute(moved, "x", [(i, (i + k) % x_count) for i in range(x_count)]))
     mine = jnp.stack(own)
     other = lax.ppermute(mine, "core", [(0, 1), (1, 0)])
-    projected = None
+    by_owner = normed.reshape(row_count, x_count, 2, depth)
+    projected_rest = None
     for parity, blocks in ((core_me, mine), (1 - core_me, other)):
-        for k in range(x_count):
-            owner = 2 * lax.rem(x_me - k + x_count, x_count) + parity
-            rows = lax.dynamic_slice_in_dim(normed, owner * depth, depth, axis=1)
-            panel = blocks[k].reshape(depth, 3 * chan_count)
-            term = jnp.dot(rows, panel, preferred_element_type=jnp.float32)
-            projected = term if projected is None else projected + term
-    streams = projected.astype(jnp.bfloat16).reshape(row_count, 3, chan_count)
+        chosen = lax.dynamic_index_in_dim(by_owner, parity, axis=2, keepdims=False)
+        ordered = jnp.roll(chosen[:, ::-1], x_me + 1, axis=1)
+        term = jnp.dot(
+            ordered.reshape(row_count, x_count * depth),
+            blocks.reshape(x_count * depth, 3 * rest),
+            preferred_element_type=jnp.float32,
+        )
+        projected_rest = term if projected_rest is None else projected_rest + term
+    projected_direct = jnp.dot(
+        normed,
+        direct_whole.reshape(direct_whole.shape[0], 3 * quarter),
+        preferred_element_type=jnp.float32,
+    )
+    streams = jnp.concatenate(
+        [
+            projected_direct.astype(jnp.bfloat16).reshape(row_count, 3, quarter),
+            projected_rest.astype(jnp.bfloat16).reshape(row_count, 3, rest),
+        ],
+        axis=2,
+    )
     parts_count = lax.axis_size(SEQ)
     halo_rows = length + 2
     shift = [(i, i + 1) for i in range(parts_count - 1)]

time: 397 us -> 487 us (1.23); the launches traced: 396 us -> 478 us
  local copies, waits for them, and re-layouts: 44.8 us -> 152 us
  waiting for transfers between devices: 239 us -> 203 us
  other arithmetic: 31.9 us -> 48.1 us
  matrix products: 59.4 us -> 51.3 us
    dynamic_slice x0 -> x5, local copies, waits for them, and re-layouts: none -> 44.9 us  [the longest x3 27.5 us: local(): chosen = lax.dynamic_index_in_dim(by_owner, parity, axis=2, keepdims=False)]
    ppermute x3, waiting for transfers between devices: 138 us -> 99.6 us  [local(): lax.ppermute(moved, 'x', [(i, (i + k) % x_count) for i in range(x_count)])]
    unnamed x40 -> x26, local copies, waits for them, and re-layouts: 7.47 us -> 32.9 us
    another operation x0 -> x2, local copies, waits for them, and re-layouts: none -> 18.6 us  [local(): mine = jnp.stack(own)]
    ppermute x0 -> x1, local copies, waits for them, and re-layouts: none -> 16.6 us  [local(): other = lax.ppermute(mine, 'core', [(0, 1), (1, 0)])]
    concatenate x0 -> x2, other arithmetic: none -> 12.6 us  [the longest x1 12.3 us: local(): ordered = jnp.roll(chosen[:, ::-1], x_me + 1, axis=1)]
    rev x0 -> x2, local copies, waits for them, and re-layouts: none -> 12.2 us  [local(): ordered = jnp.roll(chosen[:, ::-1], x_me + 1, axis=1)]
    dot_general x8 -> x3, matrix products: 44.1 us -> 35.9 us  [the longest x2 25.1 us: local(): jnp.dot(ordered.reshape(row_count, x_count * depth), blocks.reshape(x_cou...]
  transfers between devices with their start and end apart: 7 -> 8, of which waited for: 6 -> 4; matrix products, arithmetic and copies ran while one was open for 10% -> 42% of each run, Pallas kernels for 0% -> 0%
where the time goes in v6:
time: 487 us; the launch traced here: 478 us
  waiting for transfers between devices  203 us (42%)
  local copies, waits for them, and re-layouts  152 us (31%)
  matrix products  51.3 us (11%)
  other arithmetic  48.1 us (10%)
  between operations  13.6 us (3%)
  starting transfers between devices  10.6 us (2%)
    ppermute x3, waiting for transfers between devices, local(): lax.ppermute(moved, 'x', [(i, (i + k) % x_count) for i in range(x_count)])  99.6 us
    reduce_scatter x1, waiting for transfers between devices, local(): lax.psum_scatter(partial_out.astype(jnp.bfloat16), 'chan', scatter_dimens...  97.6 us
    unnamed x26, local copies, waits for them, and re-layouts  32.9 us
    dynamic_slice x3, local copies, waits for them, and re-layouts, local(): chosen = lax.dynamic_index_in_dim(by_owner, parity, axis=2, keepdims=False)  27.5 us
    dot_general x2, matrix products, local(): jnp.dot(ordered.reshape(row_count, x_count * depth), blocks.reshape(x_cou...  25.1 us
    another operation x2, local copies, waits for them, and re-layouts, local(): mine = jnp.stack(own)  18.6 us
    dynamic_slice x2, local copies, waits for them, and re-layouts, local(): ordered = jnp.roll(chosen[:, ::-1], x_me + 1, axis=1)  17.4 us
    ppermute x1, local copies, waits for them, and re-layouts, local(): other = lax.ppermute(mine, 'core', [(0, 1), (1, 0)])  16.6 us
  transfers between devices with their start and end apart: 8, of which 4 were waited for; matrix products, arithmetic and copies ran while one was open for 42% of the time, Pallas kernels for 0%

profile of v6, /device:TPU:1, one launch (start us, length us, event | category | flops | bytes accessed | tf_op | source)
XLA Modules:
  0.0 478.3 jit_solution(3755131617937950073)
XLA Ops:
  18.3 47.9 %collective-permute-done.1 = bf16[1024,3,384]{2,0,1:T(8,128)(2,1)S(1)} collective-permute-done((bf16[1024,3,384]{2,0,1:T(8,128)(2,1)S(1)}, bf16[1024,3,384]{2,0,1:T(8,128)(2,1)S(1)}, u32[]{:S(2)}, u32[]{:S(2)}) %collective-permute-start.1) | collective-permute-done | bytes 2359328 | tf_op jit(solution)/shard_map/ppermute | solution.py:67
  66.2 51.7 %collective-permute-done = bf16[1024,3,384]{2,0,1:T(8,128)(2,1)S(1)} collective-permute-done((bf16[1024,3,384]{2,0,1:T(8,128)(2,1)S(1)}, bf16[1024,3,384]{2,0,1:T(8,128)(2,1)S(1)}, u32[]{:S(2)}, u32[]{:S(2)}) %collective-permute-start) | collective-permute-done | bytes 2359328 | tf_op jit(solution)/shard_map/ppermute | solution.py:67
  117.9 4.8 %pad_maximum_fusion = bf16[4,1024,3,384]{3,1,2,0:T(8,128)(2,1)} fusion(bf16[1,1024,3,384]{3,1,2,0:T(8,128)(2,1)S(1)} %bitcast.86, bf16[1,1024,3,384]{3,1,2,0:T(8,128)(2,1)S(1)} %bitcast.84, bf16[1,1024,3,384]{3,1,2,0:T(8,128)(2,1)S(1)} %bitcast.85, bf16[1,1024,3,384]{3,1,2,0:T(8,128)(2,1)S(1)} %get-tuple-element.14), kind=kLoop, calls=%fused_computation.10 | loop fusion | flops 14155776 | bytes 18874368 | tf_op jit(solution)/shard_map/stack | solution.py:68
  127.2 8.0 %reshape.54 = bf16[32,128,383]{2,1,0:T(8,128)(2,1)} reshape(bf16[32,49024]{1,0:T(8,128)(2,1)S(1)} %slice.83) | data formatting | bytes 6275072 | tf_op jit(solution)/shard_map/reshape | solution.py:14
  140.0 16.5 %copy.45 = bf16[4,1024,3,384]{1,0,3,2:T(4,128)(2,1)} copy(bf16[4,1024,3,384]{3,1,2,0:T(8,128)(2,1)} %pad_maximum_fusion) | data formatting | bytes 18874368 | tf_op jit(solution)/shard_map/stack | solution.py:68
  156.6 13.7 %copy.61 = bf16[144,8,4,1024]{3,1,2,0:T(8,128)(2,1)} copy(bf16[144,8,4,1024]{3,2,1,0:T(4,128)(2,1)} %bitcast.68) | data formatting | bytes 18874368
  170.3 16.6 %copy.48 = bf16[4,1024,3,384]{1,0,3,2:T(4,128)(2,1)} copy(bf16[4,1024,3,384]{3,1,2,0:T(8,128)(2,1)} %collective-permute-done.3) | data formatting | bytes 18874368 | tf_op jit(solution)/shard_map/ppermute | solution.py:69
  186.9 13.5 %copy.62 = bf16[144,8,4,1024]{3,1,2,0:T(8,128)(2,1)} copy(bf16[144,8,4,1024]{3,2,1,0:T(4,128)(2,1)} %bitcast.67) | data formatting | bytes 18874368
  200.4 7.1 %fusion = f32[768]{0:T(1024)S(1)} fusion(bf16[769,8192]{0,1:T(8,128)(2,1)} %all-gather.3.cloned.1.call-done), kind=kLoop, calls=%fused_computation.2 | loop fusion | flops 18873600 | bytes 12585984 | tf_op jit(solution)/shard_map/reduce_sum | solution.py:52
  209.7 11.9 %fusion.2 = bf16[768,8192]{0,1:T(8,128)(2,1)} fusion(f32[8192]{0:T(1024)S(1)} %convert_reduce_fusion, f32[768]{0:T(1024)S(1)} %add_rsqrt_fusion, bf16[769,8192]{0,1:T(8,128)(2,1)} %all-gather.3.cloned.1.call-done), kind=kLoop, calls=%fused_computation.4 | loop fusion | flops 25165824 | bytes 25201664 | tf_op jit(solution)/shard_map/convert_element_type | solution.py:53
  221.6 10.0 %constant_dynamic-slice_fusion = (bf16[768,4,1,1024]{0,3,2,1:T(8,128)(2,1)}, bf16[768,4,1,1024]{0,3,2,1:T(8,128)(2,1)}) fusion(bf16[768,4,2,1024]{0,3,2,1:T(8,128)(2,1)} %bitcast.66, s32[]{:T(128)S(6)} %select_n.18, s32[]{:T(128)S(6)} %select_n.17), kind=kLoop, calls=%fused_computation.42 | loop fusion | bytes 25165832 | tf_op jit(solution)/shard_map/jit(dynamic_index_in_dim)/dynamic_slice | solution.py:73
  231.6 8.8 %copy.46 = bf16[768,4,1,1024]{3,0,2,1:T(8,128)(2,1)} copy(bf16[768,4,1,1024]{0,3,2,1:T(8,128)(2,1)} %get-tuple-element.12) | data formatting | bytes 12582912 | tf_op jit(solution)/shard_map/jit(dynamic_index_in_dim)/dynamic_slice | solution.py:73
  240.4 6.1 %rev.11 = bf16[768,4,1024]{2,0,1:T(8,128)(2,1)} reverse(bf16[768,4,1024]{2,0,1:T(8,128)(2,1)} %bitcast.71), dimensions={1} | reverse | bytes 12582912 | tf_op jit(solution)/shard_map/rev | solution.py:74
  246.5 8.6 %copy.43 = bf16[768,4,1,1024]{3,0,2,1:T(8,128)(2,1)} copy(bf16[768,4,1,1024]{0,3,2,1:T(8,128)(2,1)} %get-tuple-element.13) | data formatting | bytes 12582912 | tf_op jit(solution)/shard_map/jit(dynamic_index_in_dim)/dynamic_slice | solution.py:73
  255.1 6.1 %rev.10 = bf16[768,4,1024]{2,0,1:T(8,128)(2,1)} reverse(bf16[768,4,1024]{2,0,1:T(8,128)(2,1)} %bitcast.72), dimensions={1} | reverse | bytes 12582912 | tf_op jit(solution)/shard_map/rev | solution.py:74
  261.3 12.3 %fusion.3 = (bf16[768,4,1024]{2,0,1:T(8,128)(2,1)}, bf16[768,4,1024]{2,0,1:T(8,128)(2,1)}) fusion(s32[]{:T(128)S(6)} %select_n.22, bf16[768,4,1024]{2,0,1:T(8,128)(2,1)} %rev.11, bf16[768,4,1024]{2,0,1:T(8,128)(2,1)} %rev.10), kind=kLoop, calls=%fused_computation.11 | loop fusion | flops 6291456 | bytes 25165828 | tf_op jit(solution)/shard_map/jit(_roll_dynamic)/concatenate | solution.py:74
  273.5 8.7 %copy.47 = bf16[768,4,1024]{0,2,1:T(8,128)(2,1)} copy(bf16[768,4,1024]{2,0,1:T(8,128)(2,1)} %get-tuple-element.21) | data formatting | bytes 12582912 | tf_op jit(solution)/shard_map/jit(_roll_dynamic)/dynamic_slice | solution.py:74
  282.2 8.7 %copy.44 = bf16[768,4,1024]{0,2,1:T(8,128)(2,1)} copy(bf16[768,4,1024]{2,0,1:T(8,128)(2,1)} %get-tuple-element.22) | data formatting | bytes 12582912 | tf_op jit(solution)/shard_map/jit(_roll_dynamic)/dynamic_slice | solution.py:74
  291.0 13.7 %fusion.24 = f32[768,1152]{1,0:T(8,128)} fusion(bf16[768,4096]{0,1:T(8,128)(2,1)} %bitcast.83, bf16[4096,1152]{0,1:T(8,128)(2,1)} %bitcast.78), kind=kOutput, calls=%fused_computation.48 | convolution fusion | flops 7247757312 | bytes 19267584 | tf_op jit(solution)/shard_map/dot_general | solution.py:75
  304.7 11.4 %fusion.7 = bf16[768,1152]{1,0:T(8,128)(2,1)S(1)} fusion(f32[768,1152]{1,0:T(8,128)} %fusion.24, bf16[768,4096]{0,1:T(8,128)(2,1)} %bitcast.82, bf16[4096,1152]{0,1:T(8,128)(2,1)S(1)} %bitcast.81), kind=kOutput, calls=%fused_computation.20 | convolution fusion | flops 7249526784 | bytes 21037056 | tf_op jit(solution)/shard_map/dot_general | solution.py:75
  317.1 10.8 %convolution_convert_fusion.1 = bf16[768,384]{0,1:T(8,128)(2,1)S(1)} fusion(bf16[8192,384]{0,1:T(8,128)(2,1)} %bitcast.90, bf16[768,8192]{0,1:T(8,128)(2,1)} %fusion.2), kind=kOutput, calls=%fused_computation.34 | convolution fusion | flops 4832133120 | bytes 19464192 | tf_op jit(solution)/shard_map/dot_general | solution.py:81
  332.2 5.2 %collective-permute-done.4 = bf16[130,3,512]{2,0,1:T(8,128)(2,1)} collective-permute-done((bf16[130,3,512]{2,0,1:T(8,128)(2,1)}, bf16[130,3,512]{2,0,1:T(8,128)(2,1)}, u32[]{:S(2)}, u32[]{:S(2)}) %collective-permute-start.4) | collective-permute-done | bytes 399392 | tf_op jit(solution)/shard_map/ppermute | solution.py:96
  358.5 13.2 %convolution_convert_fusion = bf16[768,8192]{1,0:T(8,128)(2,1)} fusion(bf16[512,8192]{1,0:T(8,128)(2,1)} %param.13, f32[64,8,6,128]{3,2,1,0:T(8,128)S(1)} %bitcast.75, f32[896,3,512]{0,2,1:T(8,128)S(1)} %bitcast.70), kind=kOutput, calls=%fused_computation.5 | convolution fusion | flops 6449528832 | bytes 24641536 | tf_op jit(solution)/shard_map/dot_general | solution.py:99
  371.7 97.6 %reduce-scatter.2.cloned.1.call-done = bf16[768,512]{1,0:T(8,128)(2,1)} async-done(((bf16[768,8192]{1,0:T(8,128)(2,1)}), bf16[768,512]{1,0:T(8,128)(2,1)}) %reduce-scatter.2.cloned.1.call-update) | async-done | bytes 786448 | tf_op jit(solution)/shard_map/reduce_scatter | solution.py:100
  (71 shorter events, 51.7 us)
Async XLA Ops:
  6.5 132.9 %all-gather.3.cloned.1.call-start = ((), (), s32[]{:S(2)}) async-start(), calls=%async_computation.1 | async-start | bytes 15597568 | tf_op jit(solution)/shard_map/all_gather | solution.py:47
  9.8 307.3 %all-gather.5.cloned.1.call-start = ((), (), s32[]{:S(2)}) async-start(), calls=%async_computation.2 | async-start | bytes 7077888 | tf_op jit(solution)/shard_map/all_gather | solution.py:60
  12.0 54.2 %collective-permute-start.1 = (bf16[1024,3,384]{2,0,1:T(8,128)(2,1)S(1)}, bf16[1024,3,384]{2,0,1:T(8,128)(2,1)S(1)}, u32[]{:S(2)}, u32[]{:S(2)}) collective-permute-start(bf16[1024,3,384]{2,0,1:T(8,128)(2,1)S(1)} %get-tuple-element.15), channel_id=1, source_target_pairs={{0,64},{32,96},{64,0},{96,32},{1,65},{33,97},{65,1},{97,33},{2,66}... | collective-permute-start | bytes 7077896 | tf_op jit(solution)/shard_map/ppermute | solution.py:67
  15.6 102.3 %collective-permute-start = (bf16[1024,3,384]{2,0,1:T(8,128)(2,1)S(1)}, bf16[1024,3,384]{2,0,1:T(8,128)(2,1)S(1)}, u32[]{:S(2)}, u32[]{:S(2)}) collective-permute-start(bf16[1024,3,384]{2,0,1:T(8,128)(2,1)S(1)} %get-tuple-element.15), channel_id=1, source_target_pairs={{0,32},{32,64},{64,96},{96,0},{1,33},{33,65},{65,97},{97,1},{2,34}... | collective-permute-start | bytes 7077896 | tf_op jit(solution)/shard_map/ppermute | solution.py:67
  15.9 102.0 %collective-permute-start.2 = (bf16[1024,3,384]{2,0,1:T(8,128)(2,1)S(1)}, bf16[1024,3,384]{2,0,1:T(8,128)(2,1)S(1)}, u32[]{:S(2)}, u32[]{:S(2)}) collective-permute-start(bf16[1024,3,384]{2,0,1:T(8,128)(2,1)S(1)} %get-tuple-element.15), channel_id=1, source_target_pairs={{0,96},{32,0},{64,32},{96,64},{1,97},{33,1},{65,33},{97,65},{2,98}... | collective-permute-start | bytes 7077896 | tf_op jit(solution)/shard_map/ppermute | solution.py:67
  117.9 5.6 %copy-start.4 = (bf16[32,128]{1,0:T(8,128)(2,1)S(1)}, bf16[32,128]{1,0:T(8,128)(2,1)}, u32[]{:S(2)}) copy-start(bf16[32,128]{1,0:T(8,128)(2,1)} %param.12) | copy-start | bytes 24580
  117.9 5.7 %slice-start.5 = ((bf16[1024,3,512]{2,0,1:T(8,128)(2,1)}), bf16[1024,3,128]{2,0,1:T(8,128)(2,1)S(1)}, s32[]{:S(2)}) async-start(bf16[1024,3,512]{2,0,1:T(8,128)(2,1)} %param.10), calls=%async_computation.9 | async-start | bytes 1572864 | tf_op jit(solution)/shard_map/slice | solution.py:58
  122.7 47.6 %collective-permute-start.3 = (bf16[4,1024,3,384]{3,1,2,0:T(8,128)(2,1)}, bf16[4,1024,3,384]{3,1,2,0:T(8,128)(2,1)}, u32[]{:S(2)}, u32[]{:S(2)}) collective-permute-start(bf16[4,1024,3,384]{3,1,2,0:T(8,128)(2,1)} %pad_maximum_fusion), channel_id=1, source_target_pairs={{0,16},{16,0},{1,17},{17,1},{2,18},{18,2},{3,19},{19,3},{4,20},{20... | collective-permute-start | bytes 28311560 | tf_op jit(solution)/shard_map/ppermute | solution.py:69
  139.5 329.9 %reduce-scatter.2.cloned.1.call-start = ((), (), s32[]{:S(2)}) async-start(), calls=%async_computation.3 | async-start | bytes 13369344 | tf_op jit(solution)/shard_map/reduce_scatter | solution.py:100
  282.2 22.5 %slice-start.2 = ((s8[9437184]{0:T(1024)(128)(4,1)}), s8[1048576]{0:T(1024)(128)(4,1)S(1)}, s32[]{:S(2)}) async-start(s8[9437184]{0:T(1024)(128)(4,1)} %bitcast.79), calls=%async_computation.6 | async-start | bytes 2097152
  291.0 13.7 %slice-start.3 = ((s8[9437184]{0:T(1024)(128)(4,1)}), s8[4194304]{0:T(1024)(128)(4,1)S(1)}, s32[]{:S(2)}) async-start(s8[9437184]{0:T(1024)(128)(4,1)} %bitcast.79), calls=%async_computation.7 | async-start | bytes 8388608
  291.0 13.7 %slice-start.4 = ((s8[9437184]{0:T(1024)(128)(4,1)}), s8[4194304]{0:T(1024)(128)(4,1)S(1)}, s32[]{:S(2)}) async-start(s8[9437184]{0:T(1024)(128)(4,1)} %bitcast.79), calls=%async_computation.8 | async-start | bytes 8388608
  317.1 15.0 %copy-start.3 = (bf16[3,3,512]{2,1,0:T(4,128)(2,1)S(1)}, bf16[3,3,512]{2,1,0:T(4,128)(2,1)}, u32[]{:S(2)}) copy-start(bf16[3,3,512]{2,1,0:T(4,128)(2,1)} %param.11) | copy-start | bytes 27652
  329.3 8.2 %collective-permute-start.4 = (bf16[130,3,512]{2,0,1:T(8,128)(2,1)}, bf16[130,3,512]{2,0,1:T(8,128)(2,1)}, u32[]{:S(2)}, u32[]{:S(2)}) collective-permute-start(bf16[130,3,512]{2,0,1:T(8,128)(2,1)} %copy.50), channel_id=1, source_target_pairs={{0,16},{16,32},{32,48},{48,64},{64,80},{80,96},{96,112},{1,17},{17... | collective-permute-start | bytes 1198088 | tf_op jit(solution)/shard_map/ppermute | solution.py:96
  344.7 2.4 copy-start
  347.2 8.5 %copy-start.1 = (bf16[32,128,256]{2,1,0:T(8,128)(2,1)S(1)}, bf16[32,128,256]{2,1,0:T(8,128)(2,1)}, u32[]{:S(2)}) copy-start(bf16[32,128,256]{2,1,0:T(8,128)(2,1)} %slice.84) | copy-start | bytes 6291460
  351.5 6.9 %slice-start = ((s8[5505024]{0:T(1024)(128)(4,1)}), s8[1310720]{0:T(1024)(128)(4,1)S(1)}, s32[]{:S(2)}) async-start(s8[5505024]{0:T(1024)(128)(4,1)} %bitcast.69), calls=%async_computation.4 | async-start | bytes 2621440
  355.7 2.7 slice-start.1
  371.7 97.7 %copy-start.2 = (bf16[768,512]{1,0:T(8,128)(2,1)S(1)}, bf16[768,512]{1,0:T(8,128)(2,1)}, u32[]{:S(2)}) copy-start(bf16[768,512]{1,0:T(8,128)(2,1)} %param.8) | copy-start | bytes 2359300
Sparse Core Ops, SparseCore 0:
  10.0 103.6 all-gather.2
  139.6 42.6 all-gather.4
  371.9 97.4 reduce-scatter.1

commit v7 on v5

--- a/solution.py
+++ b/solution.py
@@ -63,12 +63,14 @@
     other = lax.ppermute(mine, "core", [(0, 1), (1, 0)])
     projected = None
     for parity, blocks in ((core_me, mine), (1 - core_me, other)):
+        pieces = []
         for k in range(x_count):
             owner = 2 * lax.rem(x_me - k + x_count, x_count) + parity
-            rows = lax.dynamic_slice_in_dim(normed, owner * depth, depth, axis=1)
-            panel = blocks[k].reshape(depth, 3 * chan_count)
-            term = jnp.dot(rows, panel, preferred_element_type=jnp.float32)
-            projected = term if projected is None else projected + term
+            pieces.append(lax.dynamic_slice_in_dim(normed, owner * depth, depth, axis=1))
+        rows = jnp.concatenate(pieces, axis=1)
+        panel = blocks.reshape(x_count * depth, 3 * chan_count)
+        term = jnp.dot(rows, panel, preferred_element_type=jnp.float32)
+        projected = term if projected is None else projected + term
     streams = projected.astype(jnp.bfloat16).reshape(row_count, 3, chan_count)
     parts_count = lax.axis_size(SEQ)
     halo_rows = length + 2

time: 397 us -> 445 us (1.12)
  local copies, waits for them, and re-layouts: 44.8 us -> 103 us
  matrix products: 59.4 us -> 48.3 us
  waiting for transfers between devices: 239 us -> 234 us
    unnamed x40 -> x21, local copies, waits for them, and re-layouts: 7.47 us -> 30.6 us
    another operation x0 -> x1, local copies, waits for them, and re-layouts: none -> 21.8 us  [local(): mine = jnp.stack(own)]
    ppermute x0 -> x1, local copies, waits for them, and re-layouts: none -> 21.7 us  [local(): other = lax.ppermute(mine, 'core', [(0, 1), (1, 0)])]
    dot_general x8 -> x2, matrix products: 44.1 us -> 32.9 us  [local(): term = jnp.dot(rows, panel, preferred_element_type=jnp.float32)]
    slice x1 -> x0, local copies, waits for them, and re-layouts: 8.17 us -> none  [local(): panel = blocks[k].reshape(depth, 3 * chan_count)]
  transfers between devices with their start and end apart: 7 -> 7, of which waited for: 6 -> 4; matrix products, arithmetic and copies ran while one was open for 10% -> 22% of each run, Pallas kernels for 0% -> 0%
where the time goes in v7:
time: 445 us; the launch traced here: 443 us
  waiting for transfers between devices  234 us (53%)
  local copies, waits for them, and re-layouts  103 us (23%)
  matrix products  48.3 us (11%)
  other arithmetic  33.4 us (8%)
  between operations  13.7 us (3%)
  starting transfers between devices  10 us (2%)
    ppermute x3, waiting for transfers between devices, local(): lax.ppermute(in_weight, 'x', [(i, (i + k) % x_count) for i in range(x_cou...  134 us
    reduce_scatter x1, waiting for transfers between devices, local(): lax.psum_scatter(partial_out.astype(jnp.bfloat16), 'chan', scatter_dimens...  98.1 us
    dot_general x2, matrix products, local(): term = jnp.dot(rows, panel, preferred_element_type=jnp.float32)  32.9 us
    unnamed x21, local copies, waits for them, and re-layouts  30.6 us
    another operation x1, local copies, waits for them, and re-layouts, local(): mine = jnp.stack(own)  21.8 us
    ppermute x1, local copies, waits for them, and re-layouts, local(): other = lax.ppermute(mine, 'core', [(0, 1), (1, 0)])  21.7 us
    dot_general x1, matrix products, local(): partial_out = jnp.dot(gated, out_weight, preferred_element_type=jnp.float32)  13.3 us
  transfers between devices with their start and end apart: 7, of which 4 were waited for; matrix products, arithmetic and copies ran while one was open for 22% of the time, Pallas kernels for 0%

profile of v7, /device:TPU:1, one launch (start us, length us, event | category | flops | bytes accessed | tf_op | source)
XLA Modules:
  0.0 442.7 jit_solution(1531287302843607400)
XLA Ops:
  9.4 2.1 collective-permute-start
  11.5 2.5 collective-permute-start.1
  15.1 65.4 %collective-permute-done = bf16[1024,3,512]{2,0,1:T(8,128)(2,1)S(1)} collective-permute-done((bf16[1024,3,512]{2,0,1:T(8,128)(2,1)}, bf16[1024,3,512]{2,0,1:T(8,128)(2,1)S(1)}, u32[]{:S(2)}, u32[]{:S(2)}) %collective-permute-start) | collective-permute-done | bytes 3145760 | tf_op jit(solution)/shard_map/ppermute | solution.py:61
  80.5 68.6 %collective-permute-done.1 = bf16[1024,3,512]{2,0,1:T(8,128)(2,1)S(1)} collective-permute-done((bf16[1024,3,512]{2,0,1:T(8,128)(2,1)}, bf16[1024,3,512]{2,0,1:T(8,128)(2,1)S(1)}, u32[]{:S(2)}, u32[]{:S(2)}) %collective-permute-start.1) | collective-permute-done | bytes 3145760 | tf_op jit(solution)/shard_map/ppermute | solution.py:61
  149.1 7.4 %pad_maximum_fusion = bf16[4,1024,3,512]{3,1,2,0:T(8,128)(2,1)} fusion(bf16[1,1024,3,512]{3,1,2,0:T(8,128)(2,1)S(1)} %bitcast.68, bf16[1,1024,3,512]{3,1,2,0:T(8,128)(2,1)S(1)} %bitcast.67, bf16[1,1024,3,512]{3,1,2,0:T(8,128)(2,1)S(1)} %bitcast.66, bf16[1,1024,3,512]{3,1,2,0:T(8,128)(2,1)} %bitcast.65), kind=kLoop, calls=%fused_computation.6 | loop fusion | flops 18874368 | bytes 25165824 | tf_op jit(solution)/shard_map/stack | solution.py:62
  160.5 8.2 %reshape.40 = bf16[32,128,383]{2,1,0:T(8,128)(2,1)} reshape(bf16[32,49024]{1,0:T(8,128)(2,1)S(1)} %slice.79) | data formatting | bytes 6275072 | tf_op jit(solution)/shard_map/reshape | solution.py:14
  168.6 4.3 slice.80
  172.9 21.8 %copy.14 = bf16[4,1024,3,512]{1,0,3,2:T(4,128)(2,1)} copy(bf16[4,1024,3,512]{3,1,2,0:T(8,128)(2,1)} %pad_maximum_fusion) | data formatting | bytes 25165824 | tf_op jit(solution)/shard_map/stack | solution.py:62
  194.7 13.1 %copy.27 = bf16[192,8,4,1024]{3,1,2,0:T(8,128)(2,1)} copy(bf16[192,8,4,1024]{3,2,1,0:T(4,128)(2,1)} %bitcast.56) | data formatting | bytes 25165824
  207.9 21.7 %copy.15 = bf16[4,1024,3,512]{1,0,3,2:T(4,128)(2,1)} copy(bf16[4,1024,3,512]{3,1,2,0:T(8,128)(2,1)} %collective-permute-done.3) | data formatting | bytes 25165824 | tf_op jit(solution)/shard_map/ppermute | solution.py:63
  229.6 13.1 %copy.28 = bf16[192,8,4,1024]{3,1,2,0:T(8,128)(2,1)} copy(bf16[192,8,4,1024]{3,2,1,0:T(4,128)(2,1)} %bitcast.55) | data formatting | bytes 25165824
  243.6 7.1 %fusion = f32[768]{0:T(1024)S(1)} fusion(bf16[769,8192]{1,0:T(8,128)(2,1)} %all-gather.2.cloned.1.call-done), kind=kLoop, calls=%fused_computation.2 | loop fusion | flops 18873600 | bytes 12585984 | tf_op jit(solution)/shard_map/reduce_sum | solution.py:52
  250.7 7.7 %fusion.2 = bf16[768,8192]{1,0:T(8,128)(2,1)S(1)} fusion(f32[8192]{0:T(1024)S(1)} %bitcast.69, f32[768]{0:T(1024)S(1)} %add_rsqrt_fusion, bf16[769,8192]{1,0:T(8,128)(2,1)} %all-gather.2.cloned.1.call-done), kind=kLoop, calls=%fused_computation.4 | loop fusion | flops 25165824 | bytes 25201664 | tf_op jit(solution)/shard_map/convert_element_type | solution.py:53
  258.4 3.8 constant_dynamic-slice_fusion.3
  262.2 16.8 %fusion.3 = f32[768,1536]{1,0:T(8,128)} fusion(bf16[4096,1536]{0,1:T(8,128)(2,1)} %bitcast.60, bf16[768,1024]{1,0:T(8,128)(2,1)S(1)} %get-tuple-element.13, bf16[768,1024]{1,0:T(8,128)(2,1)S(1)} %get-tuple-element.14, bf16[768,1024]{1,0:T(8,128)(2,1)} %get-tuple-element.15, bf16[768,1024]{1,0:T(8,128)(2,1)} %get-tuple-element.16), kind=kOutput, calls=%fused_computation.7 | convolution fusion | flops 9688842240 | bytes 23592960 | tf_op jit(solution)/shard_map/dot_general | solution.py:72
  279.0 16.1 %add_convert_fusion = bf16[768,1536]{1,0:T(8,128)(2,1)S(1)} fusion(f32[768,1536]{1,0:T(8,128)} %fusion.3, bf16[4096,1536]{0,1:T(8,128)(2,1)} %bitcast.61, bf16[768,1024]{1,0:T(8,128)(2,1)} %get-tuple-element.10, bf16[768,1024]{1,0:T(8,128)(2,1)} %get-tuple-element.11, bf16[768,1024]{1,0:T(8,128)(2,1)} %get-tuple-element.12, ...), kind=kOutput, calls=%fused_computation.28 | convolution fusion | flops 9691201536 | bytes 25952256 | tf_op jit(solution)/shard_map/dot_general | solution.py:72
  295.7 2.8 collective-permute-start.4
  298.5 3.1 copy.17
  306.0 4.5 %fusion.19 = f32[896,3,512]{0,2,1:T(8,128)S(1)} fusion(f32[898,3,512]{0,2,1:T(8,128)S(1)} %maximum_convert_fusion, f32[3,512]{1,0:T(4,128)S(1)} %get-tuple-element.22, f32[3,512]{1,0:T(4,128)S(1)} %get-tuple-element.23, f32[3,512]{1,0:T(4,128)S(1)} %bitcast.70), kind=kLoop, calls=%fused_computation.24 | loop fusion | flops 6881280 | bytes 22038528 | tf_op jit(solution)/shard_map/add | solution.py:23
  310.6 2.4 copy-done
  319.5 2.1 fusion.30
  322.3 13.3 %convolution_convert_fusion = bf16[768,8192]{1,0:T(8,128)(2,1)} fusion(bf16[512,8192]{1,0:T(8,128)(2,1)} %param.11, f32[64,8,6,128]{3,2,1,0:T(8,128)S(1)} %bitcast.59, f32[896,3,512]{0,2,1:T(8,128)S(1)} %bitcast.58), kind=kOutput, calls=%fused_computation.5 | convolution fusion | flops 6449528832 | bytes 24641536 | tf_op jit(solution)/shard_map/dot_general | solution.py:81
  335.6 98.1 %reduce-scatter.2.cloned.1.call-done = bf16[768,512]{1,0:T(8,128)(2,1)} async-done(((bf16[768,8192]{1,0:T(8,128)(2,1)}), bf16[768,512]{1,0:T(8,128)(2,1)}) %reduce-scatter.2.cloned.1.call-update) | async-done | bytes 786448 | tf_op jit(solution)/shard_map/reduce_scatter | solution.py:82
  433.7 2.2 add_convert_fusion.1
  (51 shorter events, 21.0 us)
Async XLA Ops:
  6.5 236.2 %all-gather.2.cloned.1.call-start = ((), (), s32[]{:S(2)}) async-start(), calls=%async_computation.1 | async-start | bytes 13508608 | tf_op jit(solution)/shard_map/all_gather | solution.py:47
  9.3 424.4 %reduce-scatter.2.cloned.1.call-start = ((), (), s32[]{:S(2)}) async-start(), calls=%async_computation.2 | async-start | bytes 13369344 | tf_op jit(solution)/shard_map/reduce_scatter | solution.py:82
  9.4 71.1 %collective-permute-start = (bf16[1024,3,512]{2,0,1:T(8,128)(2,1)}, bf16[1024,3,512]{2,0,1:T(8,128)(2,1)S(1)}, u32[]{:S(2)}, u32[]{:S(2)}) collective-permute-start(bf16[1024,3,512]{2,0,1:T(8,128)(2,1)} %param.8), channel_id=1, source_target_pairs={{0,32},{32,64},{64,96},{96,0},{1,33},{33,65},{65,97},{97,1},{2,34}... | collective-permute-start | bytes 9437192 | tf_op jit(solution)/shard_map/ppermute | solution.py:61
  11.5 137.6 %collective-permute-start.1 = (bf16[1024,3,512]{2,0,1:T(8,128)(2,1)}, bf16[1024,3,512]{2,0,1:T(8,128)(2,1)S(1)}, u32[]{:S(2)}, u32[]{:S(2)}) collective-permute-start(bf16[1024,3,512]{2,0,1:T(8,128)(2,1)} %param.8), channel_id=1, source_target_pairs={{0,64},{32,96},{64,0},{96,32},{1,65},{33,97},{65,1},{97,33},{2,66}... | collective-permute-start | bytes 9437192 | tf_op jit(solution)/shard_map/ppermute | solution.py:61
  13.9 135.1 %collective-permute-start.2 = (bf16[1024,3,512]{2,0,1:T(8,128)(2,1)}, bf16[1024,3,512]{2,0,1:T(8,128)(2,1)S(1)}, u32[]{:S(2)}, u32[]{:S(2)}) collective-permute-start(bf16[1024,3,512]{2,0,1:T(8,128)(2,1)} %param.8), channel_id=1, source_target_pairs={{0,96},{32,0},{64,32},{96,64},{1,97},{33,1},{65,33},{97,65},{2,98}... | collective-permute-start | bytes 9437192 | tf_op jit(solution)/shard_map/ppermute | solution.py:61
  149.1 8.9 %copy-start.5 = (bf16[32,128]{1,0:T(8,128)(2,1)S(1)}, bf16[32,128]{1,0:T(8,128)(2,1)}, u32[]{:S(2)}) copy-start(bf16[32,128]{1,0:T(8,128)(2,1)} %param.10) | copy-start | bytes 24580
  156.5 51.4 %collective-permute-start.3 = (bf16[4,1024,3,512]{3,1,2,0:T(8,128)(2,1)}, bf16[4,1024,3,512]{3,1,2,0:T(8,128)(2,1)}, u32[]{:S(2)}, u32[]{:S(2)}) collective-permute-start(bf16[4,1024,3,512]{3,1,2,0:T(8,128)(2,1)} %pad_maximum_fusion), channel_id=1, source_target_pairs={{0,16},{16,0},{1,17},{17,1},{2,18},{18,2},{3,19},{19,3},{4,20},{20... | collective-permute-start | bytes 37748744 | tf_op jit(solution)/shard_map/ppermute | solution.py:63
  279.0 19.4 %copy-start.4 = (bf16[3,3,512]{2,1,0:T(4,128)(2,1)S(1)}, bf16[3,3,512]{2,1,0:T(4,128)(2,1)}, u32[]{:S(2)}) copy-start(bf16[3,3,512]{2,1,0:T(4,128)(2,1)} %param.9) | copy-start | bytes 27652
  295.2 3.3 copy-start.2
  295.7 7.7 %collective-permute-start.4 = (bf16[130,3,512]{2,0,1:T(8,128)(2,1)S(1)}, bf16[130,3,512]{2,0,1:T(8,128)(2,1)}, u32[]{:S(2)}, u32[]{:S(2)}) collective-permute-start(bf16[130,3,512]{2,0,1:T(8,128)(2,1)S(1)} %copy.16), channel_id=1, source_target_pairs={{0,16},{16,32},{32,48},{48,64},{64,80},{80,96},{96,112},{1,17},{17... | collective-permute-start | bytes 1198088 | tf_op jit(solution)/shard_map/ppermute | solution.py:78
  310.5 2.4 copy-start
  313.1 6.4 %copy-start.1 = (bf16[32,128,256]{2,1,0:T(8,128)(2,1)S(1)}, bf16[32,128,256]{2,1,0:T(8,128)(2,1)}, u32[]{:S(2)}) copy-start(bf16[32,128,256]{2,1,0:T(8,128)(2,1)} %slice.80) | copy-start | bytes 6291460
  319.4 2.9 slice-start
  319.5 2.7 slice-start.1
  335.5 98.1 %copy-start.3 = (bf16[768,512]{1,0:T(8,128)(2,1)S(1)}, bf16[768,512]{1,0:T(8,128)(2,1)}, u32[]{:S(2)}) copy-start(bf16[768,512]{1,0:T(8,128)(2,1)} %param.6) | copy-start | bytes 2359300
Sparse Core Ops, SparseCore 0:
  9.4 101.1 all-gather.1
  335.7 97.9 reduce-scatter.1

commit v8 on v7

--- a/solution.py
+++ b/solution.py
@@ -59,7 +59,7 @@
     own = [in_weight]
     for k in range(1, x_count):
         own.append(lax.ppermute(in_weight, "x", [(i, (i + k) % x_count) for i in range(x_count)]))
-    mine = jnp.stack(own)
+    mine = jnp.concatenate([block.transpose(1, 0, 2) for block in own], axis=1)
     other = lax.ppermute(mine, "core", [(0, 1), (1, 0)])
     projected = None
     for parity, blocks in ((core_me, mine), (1 - core_me, other)):
@@ -68,10 +68,9 @@
             owner = 2 * lax.rem(x_me - k + x_count, x_count) + parity
             pieces.append(lax.dynamic_slice_in_dim(normed, owner * depth, depth, axis=1))
         rows = jnp.concatenate(pieces, axis=1)
-        panel = blocks.reshape(x_count * depth, 3 * chan_count)
-        term = jnp.dot(rows, panel, preferred_element_type=jnp.float32)
+        term = jnp.einsum("rk,ikc->ric", rows, blocks, preferred_element_type=jnp.float32)
         projected = term if projected is None else projected + term
-    streams = projected.astype(jnp.bfloat16).reshape(row_count, 3, chan_count)
+    streams = projected.astype(jnp.bfloat16)
     parts_count = lax.axis_size(SEQ)
     halo_rows = length + 2
     shift = [(i, i + 1) for i in range(parts_count - 1)]

time: 445 us -> 372 us (0.84)
  local copies, waits for them, and re-layouts: 103 us -> 32 us
    unnamed x21 -> x18, local copies, waits for them, and re-layouts: 30.6 us -> 4.59 us
    ppermute x2 -> x0, local copies, waits for them, and re-layouts: 23 us -> none  [the longest x1 21.7 us: local(): other = lax.ppermute(mine, 'core', [(0, 1), (1, 0)])]
    another operation x1 -> x0, local copies, waits for them, and re-layouts: 21.8 us -> none  [local(): mine = jnp.stack(own)]
    concatenate x0 -> x1, other arithmetic: none -> 7.81 us  [local(): mine = jnp.concatenate([block.transpose(1, 0, 2) for block in own], axis=1)]
    another operation x1 -> x0, other arithmetic: 7.41 us -> none  [local(): mine = jnp.stack(own)]
    slice x5 -> x7, local copies, waits for them, and re-layouts: 6.35 us -> 9.59 us  [hyena_core(): paired = jnp.concatenate([blocks[:-1], blocks[1:]], axis=1)]
  transfers between devices with their start and end apart: 7 -> 7, of which waited for: 4 -> 4; matrix products, arithmetic and copies ran while one was open for 22% -> 11% of each run, Pallas kernels for 0% -> 0%
where the time goes in v8:
time: 372 us
  waiting for transfers between devices  237 us (64%)
  matrix products  47.2 us (13%)
  other arithmetic  32.3 us (9%)
  local copies, waits for them, and re-layouts  32 us (9%)
  between operations  13.6 us (4%)
  starting transfers between devices  9.91 us (3%)
    ppermute x3, waiting for transfers between devices, local(): lax.ppermute(in_weight, 'x', [(i, (i + k) % x_count) for i in range(x_cou...  134 us
    reduce_scatter x1, waiting for transfers between devices, local(): lax.psum_scatter(partial_out.astype(jnp.bfloat16), 'chan', scatter_dimens...  97.7 us
    dot_general x2, matrix products, local(): jnp.einsum('rk,ikc->ric', rows, blocks, preferred_element_type=jnp.float32)  32.1 us
    dot_general x1, matrix products, local(): partial_out = jnp.dot(gated, out_weight, preferred_element_type=jnp.float32)  13.2 us
    slice x7, local copies, waits for them, and re-layouts, hyena_core(): paired = jnp.concatenate([blocks[:-1], blocks[1:]], axis=1)  9.59 us
    reshape x1, local copies, waits for them, and re-layouts, lag_table(): rows = tiled.reshape(groups, length, width - 1)  8.16 us
    concatenate x1, other arithmetic, local(): mine = jnp.concatenate([block.transpose(1, 0, 2) for block in own], axis=1)  7.81 us
    convert_element_type x1, other arithmetic, local(): (values * lax.rsqrt(mean_square + 1e-06) * gain_whole.astype(jnp.float32)...  7.69 us
  transfers between devices with their start and end apart: 7, of which 4 were waited for; matrix products, arithmetic and copies ran while one was open for 11% of the time, Pallas kernels for 0%

profile of v8, /device:TPU:1, one launch (start us, length us, event | category | flops | bytes accessed | tf_op | source)
XLA Modules:
  0.0 371.7 jit_solution(13204546190551159827)
XLA Ops:
  7.2 2.1 pad_maximum_fusion.1
  9.4 2.1 collective-permute-start
  11.5 2.5 collective-permute-start.1
  15.1 65.4 %collective-permute-done = bf16[1024,3,512]{2,0,1:T(8,128)(2,1)S(1)} collective-permute-done((bf16[1024,3,512]{2,0,1:T(8,128)(2,1)}, bf16[1024,3,512]{2,0,1:T(8,128)(2,1)S(1)}, u32[]{:S(2)}, u32[]{:S(2)}) %collective-permute-start) | collective-permute-done | bytes 3145760 | tf_op jit(solution)/shard_map/ppermute | solution.py:61
  80.5 68.6 %collective-permute-done.1 = bf16[1024,3,512]{2,0,1:T(8,128)(2,1)S(1)} collective-permute-done((bf16[1024,3,512]{2,0,1:T(8,128)(2,1)}, bf16[1024,3,512]{2,0,1:T(8,128)(2,1)S(1)}, u32[]{:S(2)}, u32[]{:S(2)}) %collective-permute-start.1) | collective-permute-done | bytes 3145760 | tf_op jit(solution)/shard_map/ppermute | solution.py:61
  149.1 7.8 %pad_maximum_fusion = bf16[3,4096,512]{2,1,0:T(8,128)(2,1)} fusion(bf16[3,1024,512]{2,1,0:T(8,128)(2,1)S(1)} %bitcast.61, bf16[3,1024,512]{2,1,0:T(8,128)(2,1)S(1)} %bitcast.59, bf16[3,1024,512]{2,1,0:T(8,128)(2,1)S(1)} %bitcast.57, bf16[3,1024,512]{2,1,0:T(8,128)(2,1)} %bitcast.55), kind=kLoop, calls=%fused_computation.6 | loop fusion | flops 50331648 | bytes 25165824 | tf_op jit(solution)/shard_map/concatenate | solution.py:62
  161.0 8.2 %reshape.30 = bf16[32,128,383]{2,1,0:T(8,128)(2,1)} reshape(bf16[32,49024]{1,0:T(8,128)(2,1)S(1)} %slice.75) | data formatting | bytes 6275072 | tf_op jit(solution)/shard_map/reshape | solution.py:14
  169.2 2.9 slice.76
  172.2 7.1 %fusion = f32[768]{0:T(1024)S(1)} fusion(bf16[769,8192]{1,0:T(8,128)(2,1)} %all-gather.2.cloned.1.call-done), kind=kLoop, calls=%fused_computation.2 | loop fusion | flops 18873600 | bytes 12585984 | tf_op jit(solution)/shard_map/reduce_sum | solution.py:52
  180.2 7.7 %fusion.2 = bf16[768,8192]{1,0:T(8,128)(2,1)S(1)} fusion(f32[8192]{0:T(1024)S(1)} %bitcast.63, f32[768]{0:T(1024)S(1)} %add_rsqrt_fusion, bf16[769,8192]{1,0:T(8,128)(2,1)} %all-gather.2.cloned.1.call-done), kind=kLoop, calls=%fused_computation.4 | loop fusion | flops 25165824 | bytes 25201664 | tf_op jit(solution)/shard_map/convert_element_type | solution.py:53
  187.9 3.3 constant_dynamic-slice_fusion.7
  191.2 16.1 %fusion.10 = f32[768,3,512]{2,0,1:T(8,128)} fusion(bf16[3,4096,512]{2,1,0:T(8,128)(2,1)} %collective-permute-done.3, bf16[768,1024]{1,0:T(8,128)(2,1)S(1)} %get-tuple-element.10, bf16[768,1024]{1,0:T(8,128)(2,1)S(1)} %get-tuple-element.11, bf16[768,1024]{1,0:T(8,128)(2,1)S(1)} %get-tuple-element.12, bf16[768,1024]{1,0:T(8,128)(2,1)S(1)} %get-tuple-element.13), kind=kOutput, calls=%fused_computation.16 | convolution fusion | flops 9688842240 | bytes 23592960 | tf_op jit(solution)/shard_map/rk,ikc->ric/dot_general | solution.py:71
  207.3 16.0 %add_convert_fusion = bf16[768,3,512]{2,0,1:T(8,128)(2,1)} fusion(f32[768,3,512]{2,0,1:T(8,128)} %fusion.10, bf16[768,1024]{1,0:T(8,128)(2,1)} %get-tuple-element.14, bf16[768,1024]{1,0:T(8,128)(2,1)} %get-tuple-element.15, bf16[768,1024]{1,0:T(8,128)(2,1)} %get-tuple-element.16, bf16[768,1024]{1,0:T(8,128)(2,1)} %get-tuple-element.9, ...), kind=kOutput, calls=%fused_computation.28 | convolution fusion | flops 9741533184 | bytes 25952256 | tf_op jit(solution)/shard_map/rk,ikc->ric/dot_general | solution.py:71
  224.4 2.6 collective-permute-start.4
  227.0 4.9 %collective-permute-done.4 = bf16[130,3,512]{2,0,1:T(8,128)(2,1)S(1)} collective-permute-done((bf16[130,3,512]{2,0,1:T(8,128)(2,1)S(1)}, bf16[130,3,512]{2,0,1:T(8,128)(2,1)S(1)}, u32[]{:S(2)}, u32[]{:S(2)}) %collective-permute-start.4) | collective-permute-done | bytes 399392 | tf_op jit(solution)/shard_map/ppermute | solution.py:77
  231.9 2.5 maximum_convert_fusion
  236.1 2.3 copy-done
  240.9 2.0 slice.71
  243.9 2.3 copy.11
  246.2 2.0 slice.73
  248.3 1.9 fusion.27
  251.7 13.2 %convolution_convert_fusion = bf16[768,8192]{1,0:T(8,128)(2,1)} fusion(bf16[512,8192]{1,0:T(8,128)(2,1)} %param.11, f32[768,512]{1,0:T(8,128)S(1)} %copy.15, f32[896,3,512]{2,0,1:T(8,128)} %copy-done), kind=kOutput, calls=%fused_computation.5 | convolution fusion | flops 6449528832 | bytes 24117248 | tf_op jit(solution)/shard_map/dot_general | solution.py:80
  264.9 97.7 %reduce-scatter.2.cloned.1.call-done = bf16[768,512]{1,0:T(8,128)(2,1)} async-done(((bf16[768,8192]{1,0:T(8,128)(2,1)}), bf16[768,512]{1,0:T(8,128)(2,1)}) %reduce-scatter.2.cloned.1.call-update) | async-done | bytes 786448 | tf_op jit(solution)/shard_map/reduce_scatter | solution.py:81
  362.7 2.2 add_convert_fusion.1
  (44 shorter events, 14.8 us)
Async XLA Ops:
  6.5 165.6 %all-gather.2.cloned.1.call-start = ((), (), s32[]{:S(2)}) async-start(), calls=%async_computation.1 | async-start | bytes 13508608 | tf_op jit(solution)/shard_map/all_gather | solution.py:47
  9.3 353.3 %reduce-scatter.2.cloned.1.call-start = ((), (), s32[]{:S(2)}) async-start(), calls=%async_computation.2 | async-start | bytes 13369344 | tf_op jit(solution)/shard_map/reduce_scatter | solution.py:81
  9.4 71.1 %collective-permute-start = (bf16[1024,3,512]{2,0,1:T(8,128)(2,1)}, bf16[1024,3,512]{2,0,1:T(8,128)(2,1)S(1)}, u32[]{:S(2)}, u32[]{:S(2)}) collective-permute-start(bf16[1024,3,512]{2,0,1:T(8,128)(2,1)} %param.8), channel_id=1, source_target_pairs={{0,32},{32,64},{64,96},{96,0},{1,33},{33,65},{65,97},{97,1},{2,34}... | collective-permute-start | bytes 9437192 | tf_op jit(solution)/shard_map/ppermute | solution.py:61
  11.5 137.6 %collective-permute-start.1 = (bf16[1024,3,512]{2,0,1:T(8,128)(2,1)}, bf16[1024,3,512]{2,0,1:T(8,128)(2,1)S(1)}, u32[]{:S(2)}, u32[]{:S(2)}) collective-permute-start(bf16[1024,3,512]{2,0,1:T(8,128)(2,1)} %param.8), channel_id=1, source_target_pairs={{0,64},{32,96},{64,0},{96,32},{1,65},{33,97},{65,1},{97,33},{2,66}... | collective-permute-start | bytes 9437192 | tf_op jit(solution)/shard_map/ppermute | solution.py:61
  13.9 135.1 %collective-permute-start.2 = (bf16[1024,3,512]{2,0,1:T(8,128)(2,1)}, bf16[1024,3,512]{2,0,1:T(8,128)(2,1)S(1)}, u32[]{:S(2)}, u32[]{:S(2)}) collective-permute-start(bf16[1024,3,512]{2,0,1:T(8,128)(2,1)} %param.8), channel_id=1, source_target_pairs={{0,96},{32,0},{64,32},{96,64},{1,97},{33,1},{65,33},{97,65},{2,98}... | collective-permute-start | bytes 9437192 | tf_op jit(solution)/shard_map/ppermute | solution.py:61
  80.5 76.4 %copy-start.1 = (bf16[1024,3,512]{2,0,1:T(8,128)(2,1)}, bf16[1024,3,512]{2,0,1:T(8,128)(2,1)S(1)}, u32[]{:S(2)}) copy-start(bf16[1024,3,512]{2,0,1:T(8,128)(2,1)S(1)} %collective-permute-done) | copy-start | bytes 9437188
  149.1 7.8 %copy-start.2 = (bf16[1024,3,512]{2,0,1:T(8,128)(2,1)}, bf16[1024,3,512]{2,0,1:T(8,128)(2,1)S(1)}, u32[]{:S(2)}) copy-start(bf16[1024,3,512]{2,0,1:T(8,128)(2,1)S(1)} %collective-permute-done.1) | copy-start | bytes 9437188
  149.1 7.8 %copy-start.3 = (bf16[1024,3,512]{2,0,1:T(8,128)(2,1)}, bf16[1024,3,512]{2,0,1:T(8,128)(2,1)S(1)}, u32[]{:S(2)}) copy-start(bf16[1024,3,512]{2,0,1:T(8,128)(2,1)S(1)} %collective-permute-done.2) | copy-start | bytes 9437188
  149.1 9.4 %copy-start.6 = (bf16[32,128]{1,0:T(8,128)(2,1)S(1)}, bf16[32,128]{1,0:T(8,128)(2,1)}, u32[]{:S(2)}) copy-start(bf16[32,128]{1,0:T(8,128)(2,1)} %param.10) | copy-start | bytes 24580
  156.9 34.3 %collective-permute-start.3 = (bf16[3,4096,512]{2,1,0:T(8,128)(2,1)}, bf16[3,4096,512]{2,1,0:T(8,128)(2,1)}, u32[]{:S(2)}, u32[]{:S(2)}) collective-permute-start(bf16[3,4096,512]{2,1,0:T(8,128)(2,1)} %pad_maximum_fusion), channel_id=1, source_target_pairs={{0,16},{16,0},{1,17},{17,1},{2,18},{18,2},{3,19},{19,3},{4,20},{20... | collective-permute-start | bytes 37748744 | tf_op jit(solution)/shard_map/ppermute | solution.py:63
  207.3 19.6 %copy-start.5 = (bf16[3,3,512]{2,1,0:T(4,128)(2,1)S(1)}, bf16[3,3,512]{2,1,0:T(4,128)(2,1)}, u32[]{:S(2)}) copy-start(bf16[3,3,512]{2,1,0:T(4,128)(2,1)} %param.9) | copy-start | bytes 27652
  224.4 7.5 %collective-permute-start.4 = (bf16[130,3,512]{2,0,1:T(8,128)(2,1)S(1)}, bf16[130,3,512]{2,0,1:T(8,128)(2,1)S(1)}, u32[]{:S(2)}, u32[]{:S(2)}) collective-permute-start(bf16[130,3,512]{2,0,1:T(8,128)(2,1)S(1)} %slice.77), channel_id=1, source_target_pairs={{0,16},{16,32},{32,48},{48,64},{64,80},{80,96},{96,112},{1,17},{17... | collective-permute-start | bytes 1198088 | tf_op jit(solution)/shard_map/ppermute | solution.py:77
  236.1 2.3 copy-start
  264.9 97.7 %copy-start.4 = (bf16[768,512]{1,0:T(8,128)(2,1)S(1)}, bf16[768,512]{1,0:T(8,128)(2,1)}, u32[]{:S(2)}) copy-start(bf16[768,512]{1,0:T(8,128)(2,1)} %param.6) | copy-start | bytes 2359300
Sparse Core Ops, SparseCore 0:
  9.5 101.1 all-gather.1
  265.1 97.5 reduce-scatter.1

commit v9 on v8

--- a/solution.py
+++ b/solution.py
@@ -59,8 +59,11 @@
     own = [in_weight]
     for k in range(1, x_count):
         own.append(lax.ppermute(in_weight, "x", [(i, (i + k) % x_count) for i in range(x_count)]))
+    swap = [(0, 1), (1, 0)]
+    forwarded = [lax.ppermute(block, "core", swap) for block in own]
+    own, normed, table = lax.optimization_barrier((tuple(own), normed, table))
     mine = jnp.concatenate([block.transpose(1, 0, 2) for block in own], axis=1)
-    other = lax.ppermute(mine, "core", [(0, 1), (1, 0)])
+    other = jnp.concatenate([block.transpose(1, 0, 2) for block in forwarded], axis=1)
     projected = None
     for parity, blocks in ((core_me, mine), (1 - core_me, other)):
         pieces = []

time: 372 us -> 361 us (0.970)
  waiting for transfers between devices: 237 us -> 153 us
  starting transfers between devices: 9.91 us -> 79.8 us
  matrix products: 47.2 us -> 55.7 us
  other arithmetic: 32.3 us -> 24.9 us
    ppermute x3, waiting for transfers between devices: 134 us -> 50.9 us  [local(): lax.ppermute(in_weight, 'x', [(i, (i + k) % x_count) for i in range(x_cou...]
    ppermute x1 -> x4, starting transfers between devices: 1.61 us -> 72.7 us  [local(): forwarded = [lax.ppermute(block, 'core', swap) for block in own]]
    dot_general x2, matrix products: 32.1 us -> 40.5 us  [local(): jnp.einsum('rk,ikc->ric', rows, blocks, preferred_element_type=jnp.float32)]
    concatenate x1 -> x0, other arithmetic: 7.81 us -> none  [local(): mine = jnp.concatenate([block.transpose(1, 0, 2) for block in own], axis=1)]
  transfers between devices with their start and end apart: 7 -> 10, of which waited for: 4 -> 3; matrix products, arithmetic and copies ran while one was open for 11% -> 16% of each run, Pallas kernels for 0% -> 0%
where the time goes in v9:
time: 361 us
  waiting for transfers between devices  153 us (42%)
  starting transfers between devices  79.8 us (22%)
  matrix products  55.7 us (15%)
  local copies, waits for them, and re-layouts  33.9 us (9%)
  other arithmetic  24.9 us (7%)
  between operations  13.7 us (4%)
    reduce_scatter x1, waiting for transfers between devices, local(): lax.psum_scatter(partial_out.astype(jnp.bfloat16), 'chan', scatter_dimens...  96.9 us
    ppermute x4, starting transfers between devices, local(): forwarded = [lax.ppermute(block, 'core', swap) for block in own]  72.7 us
    ppermute x3, waiting for transfers between devices, local(): lax.ppermute(in_weight, 'x', [(i, (i + k) % x_count) for i in range(x_cou...  50.9 us
    dot_general x2, matrix products, local(): jnp.einsum('rk,ikc->ric', rows, blocks, preferred_element_type=jnp.float32)  40.5 us
    dot_general x1, matrix products, local(): partial_out = jnp.dot(gated, out_weight, preferred_element_type=jnp.float32)  13.2 us
    slice x7, local copies, waits for them, and re-layouts, hyena_core(): paired = jnp.concatenate([blocks[:-1], blocks[1:]], axis=1)  9.54 us
    reshape x1, local copies, waits for them, and re-layouts, lag_table(): rows = tiled.reshape(groups, length, width - 1)  7.98 us
    convert_element_type x1, other arithmetic, local(): (values * lax.rsqrt(mean_square + 1e-06) * gain_whole.astype(jnp.float32)...  7.88 us
  transfers between devices with their start and end apart: 10, of which 3 were waited for; matrix products, arithmetic and copies ran while one was open for 16% of the time, Pallas kernels for 0%

profile of v9, /device:TPU:1, one launch (start us, length us, event | category | flops | bytes accessed | tf_op | source)
XLA Modules:
  0.0 360.6 jit_solution(1044497222369783705)
XLA Ops:
  7.2 2.1 pad_maximum_fusion
  9.4 3.4 collective-permute-start.2
  19.2 8.0 %reshape.30 = bf16[32,128,383]{2,1,0:T(8,128)(2,1)} reshape(bf16[32,49024]{1,0:T(8,128)(2,1)S(1)} %slice.75) | data formatting | bytes 6275072 | tf_op jit(solution)/shard_map/reshape | solution.py:14
  27.2 2.9 slice.76
  30.2 50.9 %collective-permute-done.2 = bf16[1024,3,512]{2,0,1:T(8,128)(2,1)} collective-permute-done((bf16[1024,3,512]{2,0,1:T(8,128)(2,1)}, bf16[1024,3,512]{2,0,1:T(8,128)(2,1)}, u32[]{:S(2)}, u32[]{:S(2)}) %collective-permute-start.2) | collective-permute-done | bytes 3145760 | tf_op jit(solution)/shard_map/ppermute | solution.py:61
  81.0 67.8 %collective-permute-start.6 = (bf16[1024,3,512]{2,0,1:T(8,128)(2,1)}, bf16[1024,3,512]{2,0,1:T(8,128)(2,1)}, u32[]{:S(2)}, u32[]{:S(2)}) collective-permute-start(bf16[1024,3,512]{2,0,1:T(8,128)(2,1)} %collective-permute-done.2), channel_id=1, source_target_pairs={{0,16},{16,0},{1,17},{17,1},{2,18},{18,2},{3,19},{19,3},{4,20},{20... | collective-permute-start | bytes 9437192 | tf_op jit(solution)/shard_map/ppermute | solution.py:63
  148.8 3.4 collective-permute-start.4
  153.2 7.1 %fusion = f32[768]{0:T(1024)S(1)} fusion(bf16[769,8192]{1,0:T(8,128)(2,1)} %all-gather.2.cloned.1.call-done), kind=kLoop, calls=%fused_computation.2 | loop fusion | flops 18873600 | bytes 12585984 | tf_op jit(solution)/shard_map/reduce_sum | solution.py:52
  160.3 7.9 %fusion.2 = bf16[768,8192]{1,0:T(8,128)(2,1)S(1)} fusion(f32[8192]{0:T(1024)S(1)} %bitcast.58, f32[768]{0:T(1024)S(1)} %add_rsqrt_fusion, bf16[769,8192]{1,0:T(8,128)(2,1)} %all-gather.2.cloned.1.call-done), kind=kLoop, calls=%fused_computation.4 | loop fusion | flops 25165824 | bytes 25201664 | tf_op jit(solution)/shard_map/convert_element_type | solution.py:53
  168.2 4.6 %constant_dynamic-slice_fusion.3 = (bf16[768,1024]{1,0:T(8,128)(2,1)}, bf16[768,1024]{1,0:T(8,128)(2,1)}, bf16[768,1024]{1,0:T(8,128)(2,1)}, bf16[768,1024]{1,0:...) fusion(bf16[768,8192]{1,0:T(8,128)(2,1)S(1)} %fusion.2, ...), kind=kLoop, calls=%fused_computation.66 | loop fusion | bytes 25165856 | tf_op jit(solution)/shard_map/dynamic_slice | solution.py:72
  172.8 24.8 %fusion.3 = f32[768,3,512]{2,0,1:T(8,128)} fusion(bf16[3,1024,512]{2,1,0:T(8,128)(2,1)} %bitcast.5, bf16[3,1024,512]{2,1,0:T(8,128)(2,1)} %bitcast.4, bf16[3,1024,512]{2,1,0:T(8,128)(2,1)} %bitcast.3, bf16[3,1024,512]{2,1,0:T(8,128)(2,1)} %bitcast.60, bf16[768,1024]{1,0:T(8,128)(2,1)} %get-tuple-element.25, bf16[768,1024]{1,0:T(8,128)(2,1)} %get-tuple-element.26, ...), kind=kOutput, calls=%fused_computation.6 | convolution fusion | flops 9739173888 | bytes 23592960 | tf_op jit(solution)/shard_map/rk,ikc->ric/dot_general | solution.py:74
  197.6 15.8 %add_convert_fusion = bf16[768,3,512]{2,0,1:T(8,128)(2,1)} fusion(f32[768,3,512]{2,0,1:T(8,128)} %fusion.3, bf16[3,1024,512]{2,1,0:T(8,128)(2,1)} %bitcast.10, bf16[3,1024,512]{2,1,0:T(8,128)(2,1)} %bitcast.9, bf16[3,1024,512]{2,1,0:T(8,128)(2,1)} %bitcast.8, bf16[3,1024,512]{2,1,0:T(8,128)(2,1)} %bitcast.7, bf16[768,1024]{1,0:T(8,128)(2,1)} %get-tuple-element.22, ...), kind=kOutput, calls=%fused_computation.41 | convolution fusion | flops 9741533184 | bytes 25952256 | tf_op jit(solution)/shard_map/rk,ikc->ric/dot_general | solution.py:74
  214.5 1.9 collective-permute-start.7
  216.5 4.9 %collective-permute-done.7 = bf16[130,3,512]{2,0,1:T(8,128)(2,1)S(1)} collective-permute-done((bf16[130,3,512]{2,0,1:T(8,128)(2,1)S(1)}, bf16[130,3,512]{2,0,1:T(8,128)(2,1)S(1)}, u32[]{:S(2)}, u32[]{:S(2)}) %collective-permute-start.7) | collective-permute-done | bytes 399392 | tf_op jit(solution)/shard_map/ppermute | solution.py:80
  221.4 2.5 maximum_convert_fusion
  223.9 1.9 fusion.31
  225.8 2.4 copy-done
  230.6 2.0 slice.71
  233.6 2.3 copy.11
  235.9 2.0 slice.73
  238.0 1.9 fusion.41
  241.4 13.2 %convolution_convert_fusion = bf16[768,8192]{1,0:T(8,128)(2,1)} fusion(bf16[512,8192]{1,0:T(8,128)(2,1)} %param.11, f32[768,512]{1,0:T(8,128)S(1)} %copy.15, f32[896,3,512]{2,0,1:T(8,128)} %copy-done), kind=kOutput, calls=%fused_computation.5 | convolution fusion | flops 6449528832 | bytes 24117248 | tf_op jit(solution)/shard_map/dot_general | solution.py:83
  254.6 96.9 %reduce-scatter.2.cloned.1.call-done = bf16[768,512]{1,0:T(8,128)(2,1)} async-done(((bf16[768,8192]{1,0:T(8,128)(2,1)}), bf16[768,512]{1,0:T(8,128)(2,1)}) %reduce-scatter.2.cloned.1.call-update) | async-done | bytes 786448 | tf_op jit(solution)/shard_map/reduce_scatter | solution.py:84
  351.5 2.2 add_convert_fusion.1
  (41 shorter events, 14.3 us)
Async XLA Ops:
  6.5 145.7 %all-gather.2.cloned.1.call-start = ((), (), s32[]{:S(2)}) async-start(), calls=%async_computation.1 | async-start | bytes 13508608 | tf_op jit(solution)/shard_map/all_gather | solution.py:47
  9.4 342.2 %reduce-scatter.2.cloned.1.call-start = ((), (), s32[]{:S(2)}) async-start(), calls=%async_computation.2 | async-start | bytes 13369344 | tf_op jit(solution)/shard_map/reduce_scatter | solution.py:84
  9.4 71.6 %collective-permute-start.2 = (bf16[1024,3,512]{2,0,1:T(8,128)(2,1)}, bf16[1024,3,512]{2,0,1:T(8,128)(2,1)}, u32[]{:S(2)}, u32[]{:S(2)}) collective-permute-start(bf16[1024,3,512]{2,0,1:T(8,128)(2,1)} %param.8), channel_id=1, source_target_pairs={{0,96},{32,0},{64,32},{96,64},{1,97},{33,1},{65,33},{97,65},{2,98}... | collective-permute-start | bytes 9437192 | tf_op jit(solution)/shard_map/ppermute | solution.py:61
  12.8 136.0 %collective-permute-start = (bf16[1024,3,512]{2,0,1:T(8,128)(2,1)}, bf16[1024,3,512]{2,0,1:T(8,128)(2,1)}, u32[]{:S(2)}, u32[]{:S(2)}) collective-permute-start(bf16[1024,3,512]{2,0,1:T(8,128)(2,1)} %param.8), channel_id=1, source_target_pairs={{0,32},{32,64},{64,96},{96,0},{1,33},{33,65},{65,97},{97,1},{2,34}... | collective-permute-start | bytes 9437192 | tf_op jit(solution)/shard_map/ppermute | solution.py:61
  12.8 139.5 %collective-permute-start.1 = (bf16[1024,3,512]{2,0,1:T(8,128)(2,1)}, bf16[1024,3,512]{2,0,1:T(8,128)(2,1)}, u32[]{:S(2)}, u32[]{:S(2)}) collective-permute-start(bf16[1024,3,512]{2,0,1:T(8,128)(2,1)} %param.8), channel_id=1, source_target_pairs={{0,64},{32,96},{64,0},{96,32},{1,65},{33,97},{65,1},{97,33},{2,66}... | collective-permute-start | bytes 9437192 | tf_op jit(solution)/shard_map/ppermute | solution.py:61
  14.5 183.1 %collective-permute-start.3 = (bf16[1024,3,512]{2,0,1:T(8,128)(2,1)}, bf16[1024,3,512]{2,0,1:T(8,128)(2,1)}, u32[]{:S(2)}, u32[]{:S(2)}) collective-permute-start(bf16[1024,3,512]{2,0,1:T(8,128)(2,1)} %param.8), channel_id=1, source_target_pairs={{0,16},{16,0},{1,17},{17,1},{2,18},{18,2},{3,19},{19,3},{4,20},{20... | collective-permute-start | bytes 9437192 | tf_op jit(solution)/shard_map/ppermute | solution.py:63
  81.0 116.6 %collective-permute-start.6 = (bf16[1024,3,512]{2,0,1:T(8,128)(2,1)}, bf16[1024,3,512]{2,0,1:T(8,128)(2,1)}, u32[]{:S(2)}, u32[]{:S(2)}) collective-permute-start(bf16[1024,3,512]{2,0,1:T(8,128)(2,1)} %collective-permute-done.2), channel_id=1, source_target_pairs={{0,16},{16,0},{1,17},{17,1},{2,18},{18,2},{3,19},{19,3},{4,20},{20... | collective-permute-start | bytes 9437192 | tf_op jit(solution)/shard_map/ppermute | solution.py:63
  148.8 48.8 %collective-permute-start.4 = (bf16[1024,3,512]{2,0,1:T(8,128)(2,1)}, bf16[1024,3,512]{2,0,1:T(8,128)(2,1)}, u32[]{:S(2)}, u32[]{:S(2)}) collective-permute-start(bf16[1024,3,512]{2,0,1:T(8,128)(2,1)} %collective-permute-done), channel_id=1, source_target_pairs={{0,16},{16,0},{1,17},{17,1},{2,18},{18,2},{3,19},{19,3},{4,20},{20... | collective-permute-start | bytes 9437192 | tf_op jit(solution)/shard_map/ppermute | solution.py:63
  152.2 45.4 %collective-permute-start.5 = (bf16[1024,3,512]{2,0,1:T(8,128)(2,1)}, bf16[1024,3,512]{2,0,1:T(8,128)(2,1)}, u32[]{:S(2)}, u32[]{:S(2)}) collective-permute-start(bf16[1024,3,512]{2,0,1:T(8,128)(2,1)} %collective-permute-done.1), channel_id=1, source_target_pairs={{0,16},{16,0},{1,17},{17,1},{2,18},{18,2},{3,19},{19,3},{4,20},{20... | collective-permute-start | bytes 9437192 | tf_op jit(solution)/shard_map/ppermute | solution.py:63
  197.6 18.8 %copy-start.2 = (bf16[3,3,512]{2,1,0:T(4,128)(2,1)S(1)}, bf16[3,3,512]{2,1,0:T(4,128)(2,1)}, u32[]{:S(2)}) copy-start(bf16[3,3,512]{2,1,0:T(4,128)(2,1)} %param.9) | copy-start | bytes 27652
  214.5 6.9 %collective-permute-start.7 = (bf16[130,3,512]{2,0,1:T(8,128)(2,1)S(1)}, bf16[130,3,512]{2,0,1:T(8,128)(2,1)S(1)}, u32[]{:S(2)}, u32[]{:S(2)}) collective-permute-start(bf16[130,3,512]{2,0,1:T(8,128)(2,1)S(1)} %slice.77), channel_id=1, source_target_pairs={{0,16},{16,32},{32,48},{48,64},{64,80},{80,96},{96,112},{1,17},{17... | collective-permute-start | bytes 1198088 | tf_op jit(solution)/shard_map/ppermute | solution.py:80
  225.8 2.4 copy-start
  254.6 96.9 %copy-start.1 = (bf16[768,512]{1,0:T(8,128)(2,1)S(1)}, bf16[768,512]{1,0:T(8,128)(2,1)}, u32[]{:S(2)}) copy-start(bf16[768,512]{1,0:T(8,128)(2,1)} %param.6) | copy-start | bytes 2359300
Sparse Core Ops, SparseCore 0:
  9.5 101.1 all-gather.1
  254.8 96.7 reduce-scatter.1

commit v10 on v9

--- a/solution.py
+++ b/solution.py
@@ -60,7 +60,10 @@
     for k in range(1, x_count):
         own.append(lax.ppermute(in_weight, "x", [(i, (i + k) % x_count) for i in range(x_count)]))
     swap = [(0, 1), (1, 0)]
-    forwarded = [lax.ppermute(block, "core", swap) for block in own]
+    forwarded = [lax.ppermute(own[0], "core", swap)]
+    for block in own[1:]:
+        block, normed = lax.optimization_barrier((block, normed))
+        forwarded.append(lax.ppermute(block, "core", swap))
     own, normed, table = lax.optimization_barrier((tuple(own), normed, table))
     mine = jnp.concatenate([block.transpose(1, 0, 2) for block in own], axis=1)
     other = jnp.concatenate([block.transpose(1, 0, 2) for block in forwarded], axis=1)

time: 361 us -> 356 us (0.986)
  starting transfers between devices: 79.8 us -> 12.6 us
  waiting for transfers between devices: 153 us -> 206 us
  local copies, waits for them, and re-layouts: 33.9 us -> 38.7 us
    all_gather x1, waiting for transfers between devices: 0.01 us -> 79.9 us  [local(): whole_joined = lax.all_gather(joined, 'chan', axis=1, tiled=True)]
    ppermute x4, starting transfers between devices: 72.7 us -> 3.56 us  [the longest x3 2.04 us: local(): forwarded.append(lax.ppermute(block, 'core', swap))]
    ppermute x3, waiting for transfers between devices: 50.9 us -> 19 us  [local(): lax.ppermute(in_weight, 'x', [(i, (i + k) % x_count) for i in range(x_cou...]
    dynamic_slice x1, local copies, waits for them, and re-layouts: 4.64 us -> 9.46 us  [local(): lax.dynamic_slice_in_dim(normed, owner * depth, depth, axis=1)]
    ppermute x4, waiting for transfers between devices: 0.01 us -> 4.64 us  [the longest x3 4.63 us: local(): forwarded.append(lax.ppermute(block, 'core', swap))]
    convert_element_type x1, other arithmetic: 7.88 us -> 11.5 us  [local(): (values * lax.rsqrt(mean_square + 1e-06) * gain_whole.astype(jnp.float32)...]
  transfers between devices with their start and end apart: 10 -> 10, of which waited for: 3 -> 6; matrix products, arithmetic and copies ran while one was open for 16% -> 12% of each run, Pallas kernels for 0% -> 0%
where the time goes in v10:
time: 356 us; the launch traced here: 355 us
  waiting for transfers between devices  206 us (58%)
  matrix products  55.6 us (16%)
  local copies, waits for them, and re-layouts  38.7 us (11%)
  other arithmetic  28.4 us (8%)
  between operations  13.6 us (4%)
  starting transfers between devices  12.6 us (4%)
    reduce_scatter x1, waiting for transfers between devices, local(): lax.psum_scatter(partial_out.astype(jnp.bfloat16), 'chan', scatter_dimens...  98 us
    all_gather x1, waiting for transfers between devices, local(): whole_joined = lax.all_gather(joined, 'chan', axis=1, tiled=True)  79.9 us
    dot_general x2, matrix products, local(): jnp.einsum('rk,ikc->ric', rows, blocks, preferred_element_type=jnp.float32)  40.5 us
    ppermute x3, waiting for transfers between devices, local(): lax.ppermute(in_weight, 'x', [(i, (i + k) % x_count) for i in range(x_cou...  19 us
    dot_general x1, matrix products, local(): partial_out = jnp.dot(gated, out_weight, preferred_element_type=jnp.float32)  13.2 us
    convert_element_type x1, other arithmetic, local(): (values * lax.rsqrt(mean_square + 1e-06) * gain_whole.astype(jnp.float32)...  11.5 us
    slice x7, local copies, waits for them, and re-layouts, hyena_core(): paired = jnp.concatenate([blocks[:-1], blocks[1:]], axis=1)  9.54 us
    dynamic_slice x1, local copies, waits for them, and re-layouts, local(): lax.dynamic_slice_in_dim(normed, owner * depth, depth, axis=1)  9.46 us
  transfers between devices with their start and end apart: 10, of which 6 were waited for; matrix products, arithmetic and copies ran while one was open for 12% of the time, Pallas kernels for 0%

profile of v10, /device:TPU:1, one launch (start us, length us, event | category | flops | bytes accessed | tf_op | source)
XLA Modules:
  0.0 355.2 jit_solution(16631332926333468948)
XLA Ops:
  7.2 2.2 pad_maximum_fusion
  9.5 2.1 collective-permute-start
  11.6 2.5 collective-permute-start.1
  19.8 8.0 %reshape.30 = bf16[32,128,383]{2,1,0:T(8,128)(2,1)} reshape(bf16[32,49024]{1,0:T(8,128)(2,1)S(1)} %slice.75) | data formatting | bytes 6275072 | tf_op jit(solution)/shard_map/reshape | solution.py:14
  27.8 2.9 slice.76
  30.8 79.9 %all-gather.2.cloned.1.call-done = bf16[769,8192]{1,0:T(8,128)(2,1)} async-done(((bf16[769,512]{1,0:T(8,128)(2,1)}), bf16[769,8192]{1,0:T(8,128)(2,1)}) %all-gather.2.cloned.1.call-update) | async-done | bytes 12599312 | tf_op jit(solution)/shard_map/all_gather | solution.py:47
  111.6 7.1 %fusion = f32[768]{0:T(1024)S(1)} fusion(bf16[769,8192]{1,0:T(8,128)(2,1)} %all-gather.2.cloned.1.call-done), kind=kLoop, calls=%fused_computation.2 | loop fusion | flops 18873600 | bytes 12585984 | tf_op jit(solution)/shard_map/reduce_sum | solution.py:52
  118.7 11.5 %fusion.2 = bf16[768,8192]{1,0:T(8,128)(2,1)} fusion(f32[8192]{0:T(1024)S(1)} %bitcast.58, f32[768]{0:T(1024)S(1)} %add_rsqrt_fusion, bf16[769,8192]{1,0:T(8,128)(2,1)} %all-gather.2.cloned.1.call-done), kind=kLoop, calls=%fused_computation.4 | loop fusion | flops 25165824 | bytes 25201664 | tf_op jit(solution)/shard_map/convert_element_type | solution.py:53
  130.2 19.0 %collective-permute-done.1 = bf16[1024,3,512]{2,0,1:T(8,128)(2,1)} collective-permute-done((bf16[1024,3,512]{2,0,1:T(8,128)(2,1)}, bf16[1024,3,512]{2,0,1:T(8,128)(2,1)}, u32[]{:S(2)}, u32[]{:S(2)}) %collective-permute-start.1) | collective-permute-done | bytes 3145760 | tf_op jit(solution)/shard_map/ppermute | solution.py:61
  151.3 9.5 %constant_dynamic-slice_fusion.7 = (bf16[768,1024]{1,0:T(8,128)(2,1)}, bf16[768,1024]{1,0:T(8,128)(2,1)}, bf16[768,1024]{1,0:T(8,128)(2,1)}, bf16[768,1024]{1,0:...) fusion(bf16[768,8192]{1,0:T(8,128)(2,1)} %fusion.2, ...), kind=kLoop, calls=%fused_computation.70 | loop fusion | bytes 25165856 | tf_op jit(solution)/shard_map/dynamic_slice | solution.py:75
  160.9 4.5 %collective-permute-done.4 = bf16[1024,3,512]{2,0,1:T(8,128)(2,1)} collective-permute-done((bf16[1024,3,512]{2,0,1:T(8,128)(2,1)}, bf16[1024,3,512]{2,0,1:T(8,128)(2,1)}, u32[]{:S(2)}, u32[]{:S(2)}) %collective-permute-start.4) | collective-permute-done | bytes 3145760 | tf_op jit(solution)/shard_map/ppermute | solution.py:66
  165.4 24.8 %fusion.11 = f32[768,3,512]{2,0,1:T(8,128)} fusion(bf16[3,1024,512]{2,1,0:T(8,128)(2,1)} %bitcast.10, bf16[3,1024,512]{2,1,0:T(8,128)(2,1)} %bitcast.9, bf16[3,1024,512]{2,1,0:T(8,128)(2,1)} %bitcast.8, bf16[3,1024,512]{2,1,0:T(8,128)(2,1)} %bitcast.7, bf16[768,1024]{1,0:T(8,128)(2,1)} %get-tuple-element.34, bf16[768,1024]{1,0:T(8,128)(2,1)} %get-tuple-element.35, ...), kind=kOutput, calls=%fused_computation.14 | convolution fusion | flops 9739173888 | bytes 23592960 | tf_op jit(solution)/shard_map/rk,ikc->ric/dot_general | solution.py:77
  190.2 15.7 %add_convert_fusion = bf16[768,3,512]{2,0,1:T(8,128)(2,1)} fusion(f32[768,3,512]{2,0,1:T(8,128)} %fusion.11, bf16[3,1024,512]{2,1,0:T(8,128)(2,1)} %bitcast.5, bf16[3,1024,512]{2,1,0:T(8,128)(2,1)} %bitcast.4, bf16[3,1024,512]{2,1,0:T(8,128)(2,1)} %bitcast.3, bf16[3,1024,512]{2,1,0:T(8,128)(2,1)} %bitcast.60, bf16[768,1024]{1,0:T(8,128)(2,1)} %get-tuple-element.38, ...), kind=kOutput, calls=%fused_computation.41 | convolution fusion | flops 9741533184 | bytes 25952256 | tf_op jit(solution)/shard_map/rk,ikc->ric/dot_general | solution.py:77
  207.0 3.3 collective-permute-start.7
  210.4 4.7 %collective-permute-done.7 = bf16[130,3,512]{2,0,1:T(8,128)(2,1)S(1)} collective-permute-done((bf16[130,3,512]{2,0,1:T(8,128)(2,1)S(1)}, bf16[130,3,512]{2,0,1:T(8,128)(2,1)S(1)}, u32[]{:S(2)}, u32[]{:S(2)}) %collective-permute-start.7) | collective-permute-done | bytes 399392 | tf_op jit(solution)/shard_map/ppermute | solution.py:83
  215.1 2.5 maximum_convert_fusion
  219.3 2.4 copy-done
  224.1 2.0 slice.71
  227.1 2.3 copy.11
  229.4 2.0 slice.73
  231.5 1.9 fusion.41
  234.9 13.2 %convolution_convert_fusion = bf16[768,8192]{1,0:T(8,128)(2,1)} fusion(bf16[512,8192]{1,0:T(8,128)(2,1)} %param.11, f32[768,512]{1,0:T(8,128)S(1)} %copy.15, f32[896,3,512]{2,0,1:T(8,128)} %copy-done), kind=kOutput, calls=%fused_computation.5 | convolution fusion | flops 6449528832 | bytes 24117248 | tf_op jit(solution)/shard_map/dot_general | solution.py:86
  248.1 98.0 %reduce-scatter.2.cloned.1.call-done = bf16[768,512]{1,0:T(8,128)(2,1)} async-done(((bf16[768,8192]{1,0:T(8,128)(2,1)}), bf16[768,512]{1,0:T(8,128)(2,1)}) %reduce-scatter.2.cloned.1.call-update) | async-done | bytes 786448 | tf_op jit(solution)/shard_map/reduce_scatter | solution.py:87
  346.1 2.2 add_convert_fusion.1
  (41 shorter events, 17.5 us)
Async XLA Ops:
  6.5 104.2 %all-gather.2.cloned.1.call-start = ((), (), s32[]{:S(2)}) async-start(), calls=%async_computation.1 | async-start | bytes 13508608 | tf_op jit(solution)/shard_map/all_gather | solution.py:47
  9.4 336.7 %reduce-scatter.2.cloned.1.call-start = ((), (), s32[]{:S(2)}) async-start(), calls=%async_computation.2 | async-start | bytes 13369344 | tf_op jit(solution)/shard_map/reduce_scatter | solution.py:87
  9.5 120.8 %collective-permute-start = (bf16[1024,3,512]{2,0,1:T(8,128)(2,1)}, bf16[1024,3,512]{2,0,1:T(8,128)(2,1)}, u32[]{:S(2)}, u32[]{:S(2)}) collective-permute-start(bf16[1024,3,512]{2,0,1:T(8,128)(2,1)} %param.8), channel_id=1, source_target_pairs={{0,32},{32,64},{64,96},{96,0},{1,33},{33,65},{65,97},{97,1},{2,34}... | collective-permute-start | bytes 9437192 | tf_op jit(solution)/shard_map/ppermute | solution.py:61
  11.6 137.7 %collective-permute-start.1 = (bf16[1024,3,512]{2,0,1:T(8,128)(2,1)}, bf16[1024,3,512]{2,0,1:T(8,128)(2,1)}, u32[]{:S(2)}, u32[]{:S(2)}) collective-permute-start(bf16[1024,3,512]{2,0,1:T(8,128)(2,1)} %param.8), channel_id=1, source_target_pairs={{0,64},{32,96},{64,0},{96,32},{1,65},{33,97},{65,1},{97,33},{2,66}... | collective-permute-start | bytes 9437192 | tf_op jit(solution)/shard_map/ppermute | solution.py:61
  14.0 135.2 %collective-permute-start.2 = (bf16[1024,3,512]{2,0,1:T(8,128)(2,1)}, bf16[1024,3,512]{2,0,1:T(8,128)(2,1)}, u32[]{:S(2)}, u32[]{:S(2)}) collective-permute-start(bf16[1024,3,512]{2,0,1:T(8,128)(2,1)} %param.8), channel_id=1, source_target_pairs={{0,96},{32,0},{64,32},{96,64},{1,97},{33,1},{65,33},{97,65},{2,98}... | collective-permute-start | bytes 9437192 | tf_op jit(solution)/shard_map/ppermute | solution.py:61
  15.2 145.6 %collective-permute-start.3 = (bf16[1024,3,512]{2,0,1:T(8,128)(2,1)}, bf16[1024,3,512]{2,0,1:T(8,128)(2,1)}, u32[]{:S(2)}, u32[]{:S(2)}) collective-permute-start(bf16[1024,3,512]{2,0,1:T(8,128)(2,1)} %param.8), channel_id=1, source_target_pairs={{0,16},{16,0},{1,17},{17,1},{2,18},{18,2},{3,19},{19,3},{4,20},{20... | collective-permute-start | bytes 9437192 | tf_op jit(solution)/shard_map/ppermute | solution.py:63
  149.3 11.5 %collective-permute-start.6 = (bf16[1024,3,512]{2,0,1:T(8,128)(2,1)}, bf16[1024,3,512]{2,0,1:T(8,128)(2,1)}, u32[]{:S(2)}, u32[]{:S(2)}) collective-permute-start(bf16[1024,3,512]{2,0,1:T(8,128)(2,1)} %collective-permute-done.2), channel_id=1, source_target_pairs={{0,16},{16,0},{1,17},{17,1},{2,18},{18,2},{3,19},{19,3},{4,20},{20... | collective-permute-start | bytes 9437192 | tf_op jit(solution)/shard_map/ppermute | solution.py:66
  150.8 10.1 %collective-permute-start.5 = (bf16[1024,3,512]{2,0,1:T(8,128)(2,1)}, bf16[1024,3,512]{2,0,1:T(8,128)(2,1)}, u32[]{:S(2)}, u32[]{:S(2)}) collective-permute-start(bf16[1024,3,512]{2,0,1:T(8,128)(2,1)} %collective-permute-done.1), channel_id=1, source_target_pairs={{0,16},{16,0},{1,17},{17,1},{2,18},{18,2},{3,19},{19,3},{4,20},{20... | collective-permute-start | bytes 9437192 | tf_op jit(solution)/shard_map/ppermute | solution.py:66
  150.8 14.6 %collective-permute-start.4 = (bf16[1024,3,512]{2,0,1:T(8,128)(2,1)}, bf16[1024,3,512]{2,0,1:T(8,128)(2,1)}, u32[]{:S(2)}, u32[]{:S(2)}) collective-permute-start(bf16[1024,3,512]{2,0,1:T(8,128)(2,1)} %collective-permute-done), channel_id=1, source_target_pairs={{0,16},{16,0},{1,17},{17,1},{2,18},{18,2},{3,19},{19,3},{4,20},{20... | collective-permute-start | bytes 9437192 | tf_op jit(solution)/shard_map/ppermute | solution.py:66
  190.2 20.2 %copy-start.2 = (bf16[3,3,512]{2,1,0:T(4,128)(2,1)S(1)}, bf16[3,3,512]{2,1,0:T(4,128)(2,1)}, u32[]{:S(2)}) copy-start(bf16[3,3,512]{2,1,0:T(4,128)(2,1)} %param.9) | copy-start | bytes 27652
  207.0 8.1 %collective-permute-start.7 = (bf16[130,3,512]{2,0,1:T(8,128)(2,1)S(1)}, bf16[130,3,512]{2,0,1:T(8,128)(2,1)S(1)}, u32[]{:S(2)}, u32[]{:S(2)}) collective-permute-start(bf16[130,3,512]{2,0,1:T(8,128)(2,1)S(1)} %slice.77), channel_id=1, source_target_pairs={{0,16},{16,32},{32,48},{48,64},{64,80},{80,96},{96,112},{1,17},{17... | collective-permute-start | bytes 1198088 | tf_op jit(solution)/shard_map/ppermute | solution.py:83
  219.3 2.4 copy-start
  248.1 98.0 %copy-start.1 = (bf16[768,512]{1,0:T(8,128)(2,1)S(1)}, bf16[768,512]{1,0:T(8,128)(2,1)}, u32[]{:S(2)}) copy-start(bf16[768,512]{1,0:T(8,128)(2,1)} %param.6) | copy-start | bytes 2359300
Sparse Core Ops, SparseCore 0:
  9.5 101.1 all-gather.1
  248.3 97.8 reduce-scatter.1

commit v11 on v8

--- a/solution.py
+++ b/solution.py
@@ -59,15 +59,24 @@
     own = [in_weight]
     for k in range(1, x_count):
         own.append(lax.ppermute(in_weight, "x", [(i, (i + k) % x_count) for i in range(x_count)]))
-    mine = jnp.concatenate([block.transpose(1, 0, 2) for block in own], axis=1)
-    other = lax.ppermute(mine, "core", [(0, 1), (1, 0)])
-    projected = None
-    for parity, blocks in ((core_me, mine), (1 - core_me, other)):
+    ordered = []
+    for parity in (core_me, 1 - core_me):
         pieces = []
         for k in range(x_count):
             owner = 2 * lax.rem(x_me - k + x_count, x_count) + parity
             pieces.append(lax.dynamic_slice_in_dim(normed, owner * depth, depth, axis=1))
-        rows = jnp.concatenate(pieces, axis=1)
+        ordered.append(jnp.concatenate(pieces, axis=1))
+    ordered = tuple(ordered)
+    swap = [(0, 1), (1, 0)]
+    forwarded = [lax.ppermute(own[0], "core", swap)]
+    for block in own[1:]:
+        block, ordered = lax.optimization_barrier((block, ordered))
+        forwarded.append(lax.ppermute(block, "core", swap))
+    own, ordered, table = lax.optimization_barrier((tuple(own), ordered, table))
+    mine = jnp.concatenate([block.transpose(1, 0, 2) for block in own], axis=1)
+    other = jnp.concatenate([block.transpose(1, 0, 2) for block in forwarded], axis=1)
+    projected = None
+    for rows, blocks in zip(ordered, (mine, other)):
         term = jnp.einsum("rk,ikc->ric", rows, blocks, preferred_element_type=jnp.float32)
         projected = term if projected is None else projected + term
     streams = projected.astype(jnp.bfloat16)

time: 372 us -> 347 us (0.933)
  waiting for transfers between devices: 237 us -> 213 us
    ppermute x3, waiting for transfers between devices: 134 us -> 15.9 us  [local(): lax.ppermute(in_weight, 'x', [(i, (i + k) % x_count) for i in range(x_cou...]
    all_gather x1, waiting for transfers between devices: 0.02 us -> 79.9 us  [local(): whole_joined = lax.all_gather(joined, 'chan', axis=1, tiled=True)]
    ppermute x1 -> x4, waiting for transfers between devices: 0.01 us -> 14.1 us  [the longest x3 14.1 us: local(): forwarded.append(lax.ppermute(block, 'core', swap))]
  transfers between devices with their start and end apart: 7 -> 10, of which waited for: 4 -> 7; matrix products, arithmetic and copies ran while one was open for 11% -> 11% of each run, Pallas kernels for 0% -> 0%
where the time goes in v11:
time: 347 us; the launch traced here: 346 us
  waiting for transfers between devices  213 us (61%)
  matrix products  46.9 us (14%)
  local copies, waits for them, and re-layouts  31.2 us (9%)
  other arithmetic  29.4 us (8%)
  between operations  13.6 us (4%)
  starting transfers between devices  12.6 us (4%)
    reduce_scatter x1, waiting for transfers between devices, local(): lax.psum_scatter(partial_out.astype(jnp.bfloat16), 'chan', scatter_dimens...  98.1 us
    all_gather x1, waiting for transfers between devices, local(): whole_joined = lax.all_gather(joined, 'chan', axis=1, tiled=True)  79.9 us
    dot_general x2, matrix products, local(): jnp.einsum('rk,ikc->ric', rows, blocks, preferred_element_type=jnp.float32)  31.8 us
    ppermute x3, waiting for transfers between devices, local(): lax.ppermute(in_weight, 'x', [(i, (i + k) % x_count) for i in range(x_cou...  15.9 us
    ppermute x3, waiting for transfers between devices, local(): forwarded.append(lax.ppermute(block, 'core', swap))  14.1 us
    dot_general x1, matrix products, local(): partial_out = jnp.dot(gated, out_weight, preferred_element_type=jnp.float32)  13.2 us
    slice x7, local copies, waits for them, and re-layouts, hyena_core(): paired = jnp.concatenate([blocks[:-1], blocks[1:]], axis=1)  9.59 us
    reshape x1, local copies, waits for them, and re-layouts, lag_table(): rows = tiled.reshape(groups, length, width - 1)  7.99 us
  transfers between devices with their start and end apart: 10, of which 7 were waited for; matrix products, arithmetic and copies ran while one was open for 11% of the time, Pallas kernels for 0%

profile of v11, /device:TPU:1, one launch (start us, length us, event | category | flops | bytes accessed | tf_op | source)
XLA Modules:
  0.0 346.5 jit_solution(13258825067505012279)
XLA Ops:
  7.2 2.1 pad_maximum_fusion.2
  9.4 2.1 collective-permute-start
  11.5 2.5 collective-permute-start.1
  19.8 8.0 %reshape.30 = bf16[32,128,383]{2,1,0:T(8,128)(2,1)} reshape(bf16[32,49024]{1,0:T(8,128)(2,1)S(1)} %slice.75) | data formatting | bytes 6275072 | tf_op jit(solution)/shard_map/reshape | solution.py:14
  27.8 2.9 slice.76
  30.7 79.9 %all-gather.2.cloned.1.call-done = bf16[769,8192]{1,0:T(8,128)(2,1)} async-done(((bf16[769,512]{1,0:T(8,128)(2,1)}), bf16[769,8192]{1,0:T(8,128)(2,1)}) %all-gather.2.cloned.1.call-update) | async-done | bytes 12599312 | tf_op jit(solution)/shard_map/all_gather | solution.py:47
  111.5 7.1 %fusion = f32[768]{0:T(1024)S(1)} fusion(bf16[769,8192]{1,0:T(8,128)(2,1)} %all-gather.2.cloned.1.call-done), kind=kLoop, calls=%fused_computation.2 | loop fusion | flops 18873600 | bytes 12585984 | tf_op jit(solution)/shard_map/reduce_sum | solution.py:52
  118.6 7.7 %fusion.2 = bf16[768,8192]{1,0:T(8,128)(2,1)S(1)} fusion(f32[8192]{0:T(1024)S(1)} %bitcast.58, f32[768]{0:T(1024)S(1)} %add_rsqrt_fusion, bf16[769,8192]{1,0:T(8,128)(2,1)} %all-gather.2.cloned.1.call-done), kind=kLoop, calls=%fused_computation.4 | loop fusion | flops 25165824 | bytes 25201664 | tf_op jit(solution)/shard_map/convert_element_type | solution.py:53
  126.3 2.0 constant_dynamic-slice_fusion.3
  128.4 4.9 %pad_maximum_fusion = (bf16[768,4096]{1,0:T(8,128)(2,1)}, bf16[768,4096]{1,0:T(8,128)(2,1)}) fusion(bf16[768,1024]{1,0:T(8,128)(2,1)S(1)} %get-tuple-element.45, bf16[768,1024]{1,0:T(8,128)(2,1)S(1)} %get-tuple-element.46, bf16[768,1024]{1,0:T(8,128)(2,1)S(1)} %get-tuple-element.47, bf16[768,1024]{1,0:T(8,128)(2,1)S(1)} %get-tuple-element.48, ...), kind=kLoop, calls=%fused_computation.22 | loop fusion | flops 50331648 | bytes 25165824 | tf_op jit(solution)/shard_map/concatenate | solution.py:68
  133.3 15.9 %collective-permute-done.1 = bf16[1024,3,512]{2,0,1:T(8,128)(2,1)} collective-permute-done((bf16[1024,3,512]{2,0,1:T(8,128)(2,1)}, bf16[1024,3,512]{2,0,1:T(8,128)(2,1)}, u32[]{:S(2)}, u32[]{:S(2)}) %collective-permute-start.1) | collective-permute-done | bytes 3145760 | tf_op jit(solution)/shard_map/ppermute | solution.py:61
  151.2 5.0 %collective-permute-done.6 = bf16[1024,3,512]{2,0,1:T(8,128)(2,1)S(1)} collective-permute-done((bf16[1024,3,512]{2,0,1:T(8,128)(2,1)}, bf16[1024,3,512]{2,0,1:T(8,128)(2,1)S(1)}, u32[]{:S(2)}, u32[]{:S(2)}) %collective-permute-start.6) | collective-permute-done | bytes 3145760 | tf_op jit(solution)/shard_map/ppermute | solution.py:74
  156.2 4.6 %collective-permute-done.5 = bf16[1024,3,512]{2,0,1:T(8,128)(2,1)} collective-permute-done((bf16[1024,3,512]{2,0,1:T(8,128)(2,1)}, bf16[1024,3,512]{2,0,1:T(8,128)(2,1)}, u32[]{:S(2)}, u32[]{:S(2)}) %collective-permute-start.5) | collective-permute-done | bytes 3145760 | tf_op jit(solution)/shard_map/ppermute | solution.py:74
  160.8 4.5 %collective-permute-done.4 = bf16[1024,3,512]{2,0,1:T(8,128)(2,1)} collective-permute-done((bf16[1024,3,512]{2,0,1:T(8,128)(2,1)}, bf16[1024,3,512]{2,0,1:T(8,128)(2,1)}, u32[]{:S(2)}, u32[]{:S(2)}) %collective-permute-start.4) | collective-permute-done | bytes 3145760 | tf_op jit(solution)/shard_map/ppermute | solution.py:74
  165.3 15.2 %fusion.11 = f32[768,3,512]{2,0,1:T(8,128)} fusion(bf16[3,1024,512]{2,1,0:T(8,128)(2,1)S(1)} %bitcast.61, bf16[3,1024,512]{2,1,0:T(8,128)(2,1)} %bitcast.9, bf16[3,1024,512]{2,1,0:T(8,128)(2,1)} %bitcast.8, bf16[3,1024,512]{2,1,0:T(8,128)(2,1)} %bitcast.7, bf16[768,4096]{1,0:T(8,128)(2,1)} %get-tuple-element.36), kind=kOutput, calls=%fused_computation.14 | convolution fusion | flops 9714008064 | bytes 23592960 | tf_op jit(solution)/shard_map/rk,ikc->ric/dot_general | solution.py:80
  180.5 16.6 %add_convert_fusion = bf16[768,3,512]{2,0,1:T(8,128)(2,1)} fusion(f32[768,3,512]{2,0,1:T(8,128)} %fusion.11, bf16[3,1024,512]{2,1,0:T(8,128)(2,1)} %bitcast.5, bf16[3,1024,512]{2,1,0:T(8,128)(2,1)} %bitcast.4, bf16[3,1024,512]{2,1,0:T(8,128)(2,1)} %bitcast.3, bf16[3,1024,512]{2,1,0:T(8,128)(2,1)} %bitcast.60, bf16[768,4096]{1,0:T(8,128)(2,1)} %get-tuple-element.31), kind=kOutput, calls=%fused_computation.31 | convolution fusion | flops 9716367360 | bytes 25952256 | tf_op jit(solution)/shard_map/rk,ikc->ric/dot_general | solution.py:80
  198.2 3.3 collective-permute-start.7
  201.6 4.7 %collective-permute-done.7 = bf16[130,3,512]{2,0,1:T(8,128)(2,1)S(1)} collective-permute-done((bf16[130,3,512]{2,0,1:T(8,128)(2,1)S(1)}, bf16[130,3,512]{2,0,1:T(8,128)(2,1)S(1)}, u32[]{:S(2)}, u32[]{:S(2)}) %collective-permute-start.7) | collective-permute-done | bytes 399392 | tf_op jit(solution)/shard_map/ppermute | solution.py:86
  206.3 2.5 maximum_convert_fusion
  210.5 2.3 copy-done
  218.3 2.3 copy.11
  226.1 13.2 %convolution_convert_fusion = bf16[768,8192]{1,0:T(8,128)(2,1)} fusion(bf16[512,8192]{1,0:T(8,128)(2,1)} %param.11, f32[768,512]{1,0:T(8,128)S(1)} %copy.15, f32[896,3,512]{2,0,1:T(8,128)} %copy-done), kind=kOutput, calls=%fused_computation.5 | convolution fusion | flops 6449528832 | bytes 24117248 | tf_op jit(solution)/shard_map/dot_general | solution.py:89
  239.3 98.1 %reduce-scatter.2.cloned.1.call-done = bf16[768,512]{1,0:T(8,128)(2,1)} async-done(((bf16[768,8192]{1,0:T(8,128)(2,1)}), bf16[768,512]{1,0:T(8,128)(2,1)}) %reduce-scatter.2.cloned.1.call-update) | async-done | bytes 786448 | tf_op jit(solution)/shard_map/reduce_scatter | solution.py:90
  337.4 2.2 add_convert_fusion.1
  (42 shorter events, 23.3 us)
Async XLA Ops:
  6.5 104.1 %all-gather.2.cloned.1.call-start = ((), (), s32[]{:S(2)}) async-start(), calls=%async_computation.1 | async-start | bytes 13508608 | tf_op jit(solution)/shard_map/all_gather | solution.py:47
  9.3 328.1 %reduce-scatter.2.cloned.1.call-start = ((), (), s32[]{:S(2)}) async-start(), calls=%async_computation.2 | async-start | bytes 13369344 | tf_op jit(solution)/shard_map/reduce_scatter | solution.py:90
  9.4 123.9 %collective-permute-start = (bf16[1024,3,512]{2,0,1:T(8,128)(2,1)}, bf16[1024,3,512]{2,0,1:T(8,128)(2,1)}, u32[]{:S(2)}, u32[]{:S(2)}) collective-permute-start(bf16[1024,3,512]{2,0,1:T(8,128)(2,1)} %param.8), channel_id=1, source_target_pairs={{0,32},{32,64},{64,96},{96,0},{1,33},{33,65},{65,97},{97,1},{2,34}... | collective-permute-start | bytes 9437192 | tf_op jit(solution)/shard_map/ppermute | solution.py:61
  11.5 137.7 %collective-permute-start.1 = (bf16[1024,3,512]{2,0,1:T(8,128)(2,1)}, bf16[1024,3,512]{2,0,1:T(8,128)(2,1)}, u32[]{:S(2)}, u32[]{:S(2)}) collective-permute-start(bf16[1024,3,512]{2,0,1:T(8,128)(2,1)} %param.8), channel_id=1, source_target_pairs={{0,64},{32,96},{64,0},{96,32},{1,65},{33,97},{65,1},{97,33},{2,66}... | collective-permute-start | bytes 9437192 | tf_op jit(solution)/shard_map/ppermute | solution.py:61
  13.9 135.2 %collective-permute-start.2 = (bf16[1024,3,512]{2,0,1:T(8,128)(2,1)}, bf16[1024,3,512]{2,0,1:T(8,128)(2,1)}, u32[]{:S(2)}, u32[]{:S(2)}) collective-permute-start(bf16[1024,3,512]{2,0,1:T(8,128)(2,1)} %param.8), channel_id=1, source_target_pairs={{0,96},{32,0},{64,32},{96,64},{1,97},{33,1},{65,33},{97,65},{2,98}... | collective-permute-start | bytes 9437192 | tf_op jit(solution)/shard_map/ppermute | solution.py:61
  15.1 136.1 %collective-permute-start.3 = (bf16[1024,3,512]{2,0,1:T(8,128)(2,1)}, bf16[1024,3,512]{2,0,1:T(8,128)(2,1)}, u32[]{:S(2)}, u32[]{:S(2)}) collective-permute-start(bf16[1024,3,512]{2,0,1:T(8,128)(2,1)} %param.8), channel_id=1, source_target_pairs={{0,16},{16,0},{1,17},{17,1},{2,18},{18,2},{3,19},{19,3},{4,20},{20... | collective-permute-start | bytes 9437192 | tf_op jit(solution)/shard_map/ppermute | solution.py:71
  149.2 7.0 %collective-permute-start.6 = (bf16[1024,3,512]{2,0,1:T(8,128)(2,1)}, bf16[1024,3,512]{2,0,1:T(8,128)(2,1)S(1)}, u32[]{:S(2)}, u32[]{:S(2)}) collective-permute-start(bf16[1024,3,512]{2,0,1:T(8,128)(2,1)} %collective-permute-done.2), channel_id=1, source_target_pairs={{0,16},{16,0},{1,17},{17,1},{2,18},{18,2},{3,19},{19,3},{4,20},{20... | collective-permute-start | bytes 9437192 | tf_op jit(solution)/shard_map/ppermute | solution.py:74
  150.7 10.1 %collective-permute-start.5 = (bf16[1024,3,512]{2,0,1:T(8,128)(2,1)}, bf16[1024,3,512]{2,0,1:T(8,128)(2,1)}, u32[]{:S(2)}, u32[]{:S(2)}) collective-permute-start(bf16[1024,3,512]{2,0,1:T(8,128)(2,1)} %collective-permute-done.1), channel_id=1, source_target_pairs={{0,16},{16,0},{1,17},{17,1},{2,18},{18,2},{3,19},{19,3},{4,20},{20... | collective-permute-start | bytes 9437192 | tf_op jit(solution)/shard_map/ppermute | solution.py:74
  150.7 14.6 %collective-permute-start.4 = (bf16[1024,3,512]{2,0,1:T(8,128)(2,1)}, bf16[1024,3,512]{2,0,1:T(8,128)(2,1)}, u32[]{:S(2)}, u32[]{:S(2)}) collective-permute-start(bf16[1024,3,512]{2,0,1:T(8,128)(2,1)} %collective-permute-done), channel_id=1, source_target_pairs={{0,16},{16,0},{1,17},{17,1},{2,18},{18,2},{3,19},{19,3},{4,20},{20... | collective-permute-start | bytes 9437192 | tf_op jit(solution)/shard_map/ppermute | solution.py:74
  180.5 21.1 %copy-start.2 = (bf16[3,3,512]{2,1,0:T(4,128)(2,1)S(1)}, bf16[3,3,512]{2,1,0:T(4,128)(2,1)}, u32[]{:S(2)}) copy-start(bf16[3,3,512]{2,1,0:T(4,128)(2,1)} %param.9) | copy-start | bytes 27652
  198.2 8.1 %collective-permute-start.7 = (bf16[130,3,512]{2,0,1:T(8,128)(2,1)S(1)}, bf16[130,3,512]{2,0,1:T(8,128)(2,1)S(1)}, u32[]{:S(2)}, u32[]{:S(2)}) collective-permute-start(bf16[130,3,512]{2,0,1:T(8,128)(2,1)S(1)} %slice.77), channel_id=1, source_target_pairs={{0,16},{16,32},{32,48},{48,64},{64,80},{80,96},{96,112},{1,17},{17... | collective-permute-start | bytes 1198088 | tf_op jit(solution)/shard_map/ppermute | solution.py:86
  210.5 2.3 copy-start
  239.3 98.1 %copy-start.1 = (bf16[768,512]{1,0:T(8,128)(2,1)S(1)}, bf16[768,512]{1,0:T(8,128)(2,1)}, u32[]{:S(2)}) copy-start(bf16[768,512]{1,0:T(8,128)(2,1)} %param.6) | copy-start | bytes 2359300
Sparse Core Ops, SparseCore 0:
  9.5 101.1 all-gather.1
  239.5 97.9 reduce-scatter.1

commit v12 on v11

--- a/solution.py
+++ b/solution.py
@@ -74,11 +74,12 @@
         forwarded.append(lax.ppermute(block, "core", swap))
     own, ordered, table = lax.optimization_barrier((tuple(own), ordered, table))
     mine = jnp.concatenate([block.transpose(1, 0, 2) for block in own], axis=1)
+    projected = jnp.einsum("rk,ikc->ric", ordered[0], mine, preferred_element_type=jnp.float32)
+    projected, forwarded = lax.optimization_barrier((projected, tuple(forwarded)))
     other = jnp.concatenate([block.transpose(1, 0, 2) for block in forwarded], axis=1)
-    projected = None
-    for rows, blocks in zip(ordered, (mine, other)):
-        term = jnp.einsum("rk,ikc->ric", rows, blocks, preferred_element_type=jnp.float32)
-        projected = term if projected is None else projected + term
+    projected = projected + jnp.einsum(
+        "rk,ikc->ric", ordered[1], other, preferred_element_type=jnp.float32
+    )
     streams = projected.astype(jnp.bfloat16)
     parts_count = lax.axis_size(SEQ)
     halo_rows = length + 2

time: 347 us -> 334 us (0.963)
  waiting for transfers between devices: 213 us -> 198 us
    ppermute x3, waiting for transfers between devices: 14.1 us -> 0.01 us  [local(): forwarded.append(lax.ppermute(block, 'core', swap))]
    convert_element_type x0 -> x1, other arithmetic: none -> 4.61 us  [local(): streams = projected.astype(jnp.bfloat16)]
  transfers between devices with their start and end apart: 10 -> 10, of which waited for: 7 -> 4; matrix products, arithmetic and copies ran while one was open for 11% -> 16% of each run, Pallas kernels for 0% -> 0%
where the time goes in v12:
time: 334 us; the launch traced here: 333 us
  waiting for transfers between devices  198 us (59%)
  matrix products  46.5 us (14%)
  other arithmetic  32.3 us (10%)
  local copies, waits for them, and re-layouts  30.2 us (9%)
  between operations  13.7 us (4%)
  starting transfers between devices  12.3 us (4%)
    reduce_scatter x1, waiting for transfers between devices, local(): lax.psum_scatter(partial_out.astype(jnp.bfloat16), 'chan', scatter_dimens...  97.6 us
    all_gather x1, waiting for transfers between devices, local(): whole_joined = lax.all_gather(joined, 'chan', axis=1, tiled=True)  79.9 us
    dot_general x1, matrix products, local(): jnp.einsum('rk,ikc->ric', ordered[0], mine, preferred_element_type=jnp.fl...  16.2 us
    ppermute x3, waiting for transfers between devices, local(): lax.ppermute(in_weight, 'x', [(i, (i + k) % x_count) for i in range(x_cou...  15.9 us
    dot_general x1, matrix products, local(): jnp.einsum('rk,ikc->ric', ordered[1], other, preferred_element_type=jnp.f...  15.2 us
    dot_general x1, matrix products, local(): partial_out = jnp.dot(gated, out_weight, preferred_element_type=jnp.float32)  13.2 us
    slice x7, local copies, waits for them, and re-layouts, hyena_core(): paired = jnp.concatenate([blocks[:-1], blocks[1:]], axis=1)  9.59 us
    reshape x1, local copies, waits for them, and re-layouts, lag_table(): rows = tiled.reshape(groups, length, width - 1)  7.99 us
  transfers between devices with their start and end apart: 10, of which 4 were waited for; matrix products, arithmetic and copies ran while one was open for 16% of the time, Pallas kernels for 0%

profile of v12, /device:TPU:1, one launch (start us, length us, event | category | flops | bytes accessed | tf_op | source)
XLA Modules:
  0.0 333.2 jit_solution(17488564039129085752)
XLA Ops:
  7.2 2.1 pad_maximum_fusion.2
  9.4 2.1 collective-permute-start
  11.5 2.5 collective-permute-start.1
  19.8 8.0 %reshape.30 = bf16[32,128,383]{2,1,0:T(8,128)(2,1)} reshape(bf16[32,49024]{1,0:T(8,128)(2,1)S(1)} %slice.75) | data formatting | bytes 6275072 | tf_op jit(solution)/shard_map/reshape | solution.py:14
  27.8 2.9 slice.76
  30.7 79.9 %all-gather.2.cloned.1.call-done = bf16[769,8192]{1,0:T(8,128)(2,1)} async-done(((bf16[769,512]{1,0:T(8,128)(2,1)}), bf16[769,8192]{1,0:T(8,128)(2,1)}) %all-gather.2.cloned.1.call-update) | async-done | bytes 12599312 | tf_op jit(solution)/shard_map/all_gather | solution.py:47
  111.5 7.1 %fusion = f32[768]{0:T(1024)S(1)} fusion(bf16[769,8192]{1,0:T(8,128)(2,1)} %all-gather.2.cloned.1.call-done), kind=kLoop, calls=%fused_computation.2 | loop fusion | flops 18873600 | bytes 12585984 | tf_op jit(solution)/shard_map/reduce_sum | solution.py:52
  118.6 7.7 %fusion.2 = bf16[768,8192]{1,0:T(8,128)(2,1)S(1)} fusion(f32[8192]{0:T(1024)S(1)} %bitcast.56, f32[768]{0:T(1024)S(1)} %add_rsqrt_fusion, bf16[769,8192]{1,0:T(8,128)(2,1)} %all-gather.2.cloned.1.call-done), kind=kLoop, calls=%fused_computation.4 | loop fusion | flops 25165824 | bytes 25201664 | tf_op jit(solution)/shard_map/convert_element_type | solution.py:53
  126.3 2.0 constant_dynamic-slice_fusion.3
  128.4 4.9 %pad_maximum_fusion = (bf16[768,4096]{1,0:T(8,128)(2,1)}, bf16[768,4096]{1,0:T(8,128)(2,1)}) fusion(bf16[768,1024]{1,0:T(8,128)(2,1)S(1)} %get-tuple-element.55, bf16[768,1024]{1,0:T(8,128)(2,1)S(1)} %get-tuple-element.56, bf16[768,1024]{1,0:T(8,128)(2,1)S(1)} %get-tuple-element.57, bf16[768,1024]{1,0:T(8,128)(2,1)S(1)} %get-tuple-element.58, ...), kind=kLoop, calls=%fused_computation.22 | loop fusion | flops 50331648 | bytes 25165824 | tf_op jit(solution)/shard_map/concatenate | solution.py:68
  133.3 15.9 %collective-permute-done.1 = bf16[1024,3,512]{2,0,1:T(8,128)(2,1)} collective-permute-done((bf16[1024,3,512]{2,0,1:T(8,128)(2,1)}, bf16[1024,3,512]{2,0,1:T(8,128)(2,1)}, u32[]{:S(2)}, u32[]{:S(2)}) %collective-permute-start.1) | collective-permute-done | bytes 3145760 | tf_op jit(solution)/shard_map/ppermute | solution.py:61
  151.2 16.2 %fusion.3 = f32[768,3,512]{2,0,1:T(8,128)} fusion(bf16[3,1024,512]{2,1,0:T(8,128)(2,1)} %bitcast.5, bf16[3,1024,512]{2,1,0:T(8,128)(2,1)} %bitcast.4, bf16[3,1024,512]{2,1,0:T(8,128)(2,1)} %bitcast.3, bf16[3,1024,512]{2,1,0:T(8,128)(2,1)} %bitcast.58, bf16[768,4096]{1,0:T(8,128)(2,1)} %get-tuple-element.36), kind=kOutput, calls=%fused_computation.6 | convolution fusion | flops 9714008064 | bytes 23592960 | tf_op jit(solution)/shard_map/rk,ikc->ric/dot_general | solution.py:77
  167.5 15.2 %fusion.11 = f32[768,3,512]{2,0,1:T(8,128)} fusion(bf16[3,1024,512]{2,1,0:T(8,128)(2,1)S(1)} %bitcast.59, bf16[3,1024,512]{2,1,0:T(8,128)(2,1)} %bitcast.9, bf16[3,1024,512]{2,1,0:T(8,128)(2,1)} %bitcast.8, bf16[3,1024,512]{2,1,0:T(8,128)(2,1)} %bitcast.7, bf16[768,4096]{1,0:T(8,128)(2,1)} %get-tuple-element.45), kind=kOutput, calls=%fused_computation.14 | convolution fusion | flops 9714008064 | bytes 23592960 | tf_op jit(solution)/shard_map/rk,ikc->ric/dot_general | solution.py:80
  182.7 4.6 %add_convert_fusion = bf16[768,3,512]{2,0,1:T(8,128)(2,1)S(1)} fusion(f32[768,3,512]{2,0,1:T(8,128)} %fusion.3, f32[768,3,512]{2,0,1:T(8,128)} %fusion.11), kind=kLoop, calls=%fused_computation.31 | loop fusion | flops 2359296 | bytes 11796480 | tf_op jit(solution)/shard_map/convert_element_type | solution.py:83
  187.4 3.0 collective-permute-start.7
  190.5 4.7 %collective-permute-done.7 = bf16[130,3,512]{2,0,1:T(8,128)(2,1)S(1)} collective-permute-done((bf16[130,3,512]{2,0,1:T(8,128)(2,1)S(1)}, bf16[130,3,512]{2,0,1:T(8,128)(2,1)S(1)}, u32[]{:S(2)}, u32[]{:S(2)}) %collective-permute-start.7) | collective-permute-done | bytes 399392 | tf_op jit(solution)/shard_map/ppermute | solution.py:87
  197.6 2.3 copy-done
  202.5 2.0 slice.71
  205.5 2.3 copy.11
  207.8 2.0 slice.73
  209.9 1.9 fusion.31
  213.3 13.2 %convolution_convert_fusion = bf16[768,8192]{1,0:T(8,128)(2,1)} fusion(bf16[512,8192]{1,0:T(8,128)(2,1)} %param.11, f32[768,512]{1,0:T(8,128)S(1)} %copy.15, f32[896,3,512]{2,0,1:T(8,128)} %copy-done), kind=kOutput, calls=%fused_computation.5 | convolution fusion | flops 6449528832 | bytes 24117248 | tf_op jit(solution)/shard_map/dot_general | solution.py:90
  226.5 97.6 %reduce-scatter.2.cloned.1.call-done = bf16[768,512]{1,0:T(8,128)(2,1)} async-done(((bf16[768,8192]{1,0:T(8,128)(2,1)}), bf16[768,512]{1,0:T(8,128)(2,1)}) %reduce-scatter.2.cloned.1.call-update) | async-done | bytes 786448 | tf_op jit(solution)/shard_map/reduce_scatter | solution.py:91
  324.1 2.2 add_convert_fusion.1
  (43 shorter events, 17.2 us)
Async XLA Ops:
  6.5 104.1 %all-gather.2.cloned.1.call-start = ((), (), s32[]{:S(2)}) async-start(), calls=%async_computation.1 | async-start | bytes 13508608 | tf_op jit(solution)/shard_map/all_gather | solution.py:47
  9.3 314.8 %reduce-scatter.2.cloned.1.call-start = ((), (), s32[]{:S(2)}) async-start(), calls=%async_computation.2 | async-start | bytes 13369344 | tf_op jit(solution)/shard_map/reduce_scatter | solution.py:91
  9.4 123.9 %collective-permute-start = (bf16[1024,3,512]{2,0,1:T(8,128)(2,1)}, bf16[1024,3,512]{2,0,1:T(8,128)(2,1)}, u32[]{:S(2)}, u32[]{:S(2)}) collective-permute-start(bf16[1024,3,512]{2,0,1:T(8,128)(2,1)} %param.8), channel_id=1, source_target_pairs={{0,32},{32,64},{64,96},{96,0},{1,33},{33,65},{65,97},{97,1},{2,34}... | collective-permute-start | bytes 9437192 | tf_op jit(solution)/shard_map/ppermute | solution.py:61
  11.5 137.7 %collective-permute-start.1 = (bf16[1024,3,512]{2,0,1:T(8,128)(2,1)}, bf16[1024,3,512]{2,0,1:T(8,128)(2,1)}, u32[]{:S(2)}, u32[]{:S(2)}) collective-permute-start(bf16[1024,3,512]{2,0,1:T(8,128)(2,1)} %param.8), channel_id=1, source_target_pairs={{0,64},{32,96},{64,0},{96,32},{1,65},{33,97},{65,1},{97,33},{2,66}... | collective-permute-start | bytes 9437192 | tf_op jit(solution)/shard_map/ppermute | solution.py:61
  13.9 135.2 %collective-permute-start.2 = (bf16[1024,3,512]{2,0,1:T(8,128)(2,1)}, bf16[1024,3,512]{2,0,1:T(8,128)(2,1)}, u32[]{:S(2)}, u32[]{:S(2)}) collective-permute-start(bf16[1024,3,512]{2,0,1:T(8,128)(2,1)} %param.8), channel_id=1, source_target_pairs={{0,96},{32,0},{64,32},{96,64},{1,97},{33,1},{65,33},{97,65},{2,98}... | collective-permute-start | bytes 9437192 | tf_op jit(solution)/shard_map/ppermute | solution.py:61
  15.1 152.4 %collective-permute-start.3 = (bf16[1024,3,512]{2,0,1:T(8,128)(2,1)}, bf16[1024,3,512]{2,0,1:T(8,128)(2,1)}, u32[]{:S(2)}, u32[]{:S(2)}) collective-permute-start(bf16[1024,3,512]{2,0,1:T(8,128)(2,1)} %param.8), channel_id=1, source_target_pairs={{0,16},{16,0},{1,17},{17,1},{2,18},{18,2},{3,19},{19,3},{4,20},{20... | collective-permute-start | bytes 9437192 | tf_op jit(solution)/shard_map/ppermute | solution.py:71
  149.2 18.3 %collective-permute-start.6 = (bf16[1024,3,512]{2,0,1:T(8,128)(2,1)}, bf16[1024,3,512]{2,0,1:T(8,128)(2,1)S(1)}, u32[]{:S(2)}, u32[]{:S(2)}) collective-permute-start(bf16[1024,3,512]{2,0,1:T(8,128)(2,1)} %collective-permute-done.2), channel_id=1, source_target_pairs={{0,16},{16,0},{1,17},{17,1},{2,18},{18,2},{3,19},{19,3},{4,20},{20... | collective-permute-start | bytes 9437192 | tf_op jit(solution)/shard_map/ppermute | solution.py:74
  150.7 16.7 %collective-permute-start.5 = (bf16[1024,3,512]{2,0,1:T(8,128)(2,1)}, bf16[1024,3,512]{2,0,1:T(8,128)(2,1)}, u32[]{:S(2)}, u32[]{:S(2)}) collective-permute-start(bf16[1024,3,512]{2,0,1:T(8,128)(2,1)} %collective-permute-done.1), channel_id=1, source_target_pairs={{0,16},{16,0},{1,17},{17,1},{2,18},{18,2},{3,19},{19,3},{4,20},{20... | collective-permute-start | bytes 9437192 | tf_op jit(solution)/shard_map/ppermute | solution.py:74
  150.7 16.8 %collective-permute-start.4 = (bf16[1024,3,512]{2,0,1:T(8,128)(2,1)}, bf16[1024,3,512]{2,0,1:T(8,128)(2,1)}, u32[]{:S(2)}, u32[]{:S(2)}) collective-permute-start(bf16[1024,3,512]{2,0,1:T(8,128)(2,1)} %collective-permute-done), channel_id=1, source_target_pairs={{0,16},{16,0},{1,17},{17,1},{2,18},{18,2},{3,19},{19,3},{4,20},{20... | collective-permute-start | bytes 9437192 | tf_op jit(solution)/shard_map/ppermute | solution.py:74
  182.7 7.7 %copy-start.2 = (bf16[3,3,512]{2,1,0:T(4,128)(2,1)S(1)}, bf16[3,3,512]{2,1,0:T(4,128)(2,1)}, u32[]{:S(2)}) copy-start(bf16[3,3,512]{2,1,0:T(4,128)(2,1)} %param.9) | copy-start | bytes 27652
  187.4 7.7 %collective-permute-start.7 = (bf16[130,3,512]{2,0,1:T(8,128)(2,1)S(1)}, bf16[130,3,512]{2,0,1:T(8,128)(2,1)S(1)}, u32[]{:S(2)}, u32[]{:S(2)}) collective-permute-start(bf16[130,3,512]{2,0,1:T(8,128)(2,1)S(1)} %slice.77), channel_id=1, source_target_pairs={{0,16},{16,32},{32,48},{48,64},{64,80},{80,96},{96,112},{1,17},{17... | collective-permute-start | bytes 1198088 | tf_op jit(solution)/shard_map/ppermute | solution.py:87
  197.6 2.3 copy-start
  226.5 97.7 %copy-start.1 = (bf16[768,512]{1,0:T(8,128)(2,1)S(1)}, bf16[768,512]{1,0:T(8,128)(2,1)}, u32[]{:S(2)}) copy-start(bf16[768,512]{1,0:T(8,128)(2,1)} %param.6) | copy-start | bytes 2359300
Sparse Core Ops, SparseCore 0:
  9.5 101.1 all-gather.1
  226.6 97.4 reduce-scatter.1

commit v13 on v12

--- a/solution.py
+++ b/solution.py
@@ -59,27 +59,44 @@
     own = [in_weight]
     for k in range(1, x_count):
         own.append(lax.ppermute(in_weight, "x", [(i, (i + k) % x_count) for i in range(x_count)]))
+    late = x_count // 2
+    early = [k for k in range(x_count) if k != late]
     ordered = []
     for parity in (core_me, 1 - core_me):
         pieces = []
         for k in range(x_count):
             owner = 2 * lax.rem(x_me - k + x_count, x_count) + parity
             pieces.append(lax.dynamic_slice_in_dim(normed, owner * depth, depth, axis=1))
-        ordered.append(jnp.concatenate(pieces, axis=1))
+        ordered.append(jnp.concatenate([pieces[k] for k in early], axis=1))
+        ordered.append(pieces[late])
     ordered = tuple(ordered)
     swap = [(0, 1), (1, 0)]
-    forwarded = [lax.ppermute(own[0], "core", swap)]
-    for block in own[1:]:
-        block, ordered = lax.optimization_barrier((block, ordered))
-        forwarded.append(lax.ppermute(block, "core", swap))
-    own, ordered, table = lax.optimization_barrier((tuple(own), ordered, table))
-    mine = jnp.concatenate([block.transpose(1, 0, 2) for block in own], axis=1)
-    projected = jnp.einsum("rk,ikc->ric", ordered[0], mine, preferred_element_type=jnp.float32)
-    projected, forwarded = lax.optimization_barrier((projected, tuple(forwarded)))
-    other = jnp.concatenate([block.transpose(1, 0, 2) for block in forwarded], axis=1)
-    projected = projected + jnp.einsum(
-        "rk,ikc->ric", ordered[1], other, preferred_element_type=jnp.float32
+    forwarded = {0: lax.ppermute(own[0], "core", swap)}
+    for k in early[1:]:
+        block, ordered = lax.optimization_barrier((own[k], ordered))
+        forwarded[k] = lax.ppermute(block, "core", swap)
+    firsts, ordered, table = lax.optimization_barrier(
+        (tuple(own[k] for k in early), ordered, table)
     )
+
+    def joined_blocks(blocks):
+        return jnp.concatenate([block.transpose(1, 0, 2) for block in blocks], axis=1)
+
+    def product(rows, blocks):
+        return jnp.einsum(
+            "rk,ikc->ric", rows, joined_blocks(blocks), preferred_element_type=jnp.float32
+        )
+
+    projected = product(ordered[0], firsts)
+    last, projected = lax.optimization_barrier((own[late], projected))
+    forwarded[late] = lax.ppermute(last, "core", swap)
+    projected, seconds = lax.optimization_barrier(
+        (projected, tuple(forwarded[k] for k in early))
+    )
+    projected = projected + product(ordered[2], seconds)
+    projected = projected + product(ordered[1], (last,))
+    projected, second_last = lax.optimization_barrier((projected, forwarded[late]))
+    projected = projected + product(ordered[3], (second_last,))
     streams = projected.astype(jnp.bfloat16)
     parts_count = lax.axis_size(SEQ)
     halo_rows = length + 2

time: 334 us -> 329 us (0.985)
  other arithmetic: 32.3 us -> 24.5 us
    reduce_scatter x1, waiting for transfers between devices: 97.6 us -> 109 us  [local(): lax.psum_scatter(partial_out.astype(jnp.bfloat16), 'chan', scatter_dimens...]
    ppermute x3, waiting for transfers between devices: 15.9 us -> 6.12 us  [local(): lax.ppermute(in_weight, 'x', [(i, (i + k) % x_count) for i in range(x_cou...]
    concatenate x1, other arithmetic: 4.91 us -> 0.67 us  [local(): ordered.append(jnp.concatenate([pieces[k] for k in early], axis=1))]
    dot_general x2 -> x4, matrix products: 31.4 us -> 30.8 us  [product(): jnp.einsum('rk,ikc->ric', rows, joined_blocks(blocks), preferred_element_...]
  transfers between devices with their start and end apart: 10 -> 10, of which waited for: 4 -> 4; matrix products, arithmetic and copies ran while one was open for 16% -> 19% of each run, Pallas kernels for 0% -> 0%
where the time goes in v13:
time: 329 us
  waiting for transfers between devices  200 us (61%)
  matrix products  45.9 us (14%)
  local copies, waits for them, and re-layouts  30.9 us (9%)
  other arithmetic  24.5 us (7%)
  between operations  13.7 us (4%)
  starting transfers between devices  13.5 us (4%)
    reduce_scatter x1, waiting for transfers between devices, local(): lax.psum_scatter(partial_out.astype(jnp.bfloat16), 'chan', scatter_dimens...  109 us
    all_gather x1, waiting for transfers between devices, local(): whole_joined = lax.all_gather(joined, 'chan', axis=1, tiled=True)  80.5 us
    dot_general x4, matrix products, product(): jnp.einsum('rk,ikc->ric', rows, joined_blocks(blocks), preferred_element_...  30.8 us
    dot_general x1, matrix products, local(): partial_out = jnp.dot(gated, out_weight, preferred_element_type=jnp.float32)  13.2 us
    slice x7, local copies, waits for them, and re-layouts, hyena_core(): paired = jnp.concatenate([blocks[:-1], blocks[1:]], axis=1)  9.55 us
    reshape x1, local copies, waits for them, and re-layouts, lag_table(): rows = tiled.reshape(groups, length, width - 1)  7.95 us
    convert_element_type x1, other arithmetic, local(): (values * lax.rsqrt(mean_square + 1e-06) * gain_whole.astype(jnp.float32)...  7.48 us
    reduce_sum x1, other arithmetic, local(): mean_square = jnp.mean(values * values, axis=1, keepdims=True)  7.1 us
  transfers between devices with their start and end apart: 10, of which 4 were waited for; matrix products, arithmetic and copies ran while one was open for 19% of the time, Pallas kernels for 0%

profile of v13, /device:TPU:1, one launch (start us, length us, event | category | flops | bytes accessed | tf_op | source)
XLA Modules:
  0.0 328.7 jit_solution(14919796020296831205)
XLA Ops:
  7.2 2.1 pad_maximum_fusion.2
  9.4 2.1 collective-permute-start.1
  19.2 7.9 %reshape.30 = bf16[32,128,383]{2,1,0:T(8,128)(2,1)} reshape(bf16[32,49024]{1,0:T(8,128)(2,1)S(1)} %slice.75) | data formatting | bytes 6275072 | tf_op jit(solution)/shard_map/reshape | solution.py:14
  27.1 2.9 slice.76
  30.1 80.5 %all-gather.2.cloned.1.call-done = bf16[769,8192]{1,0:T(8,128)(2,1)} async-done(((bf16[769,512]{1,0:T(8,128)(2,1)}), bf16[769,8192]{1,0:T(8,128)(2,1)}) %all-gather.2.cloned.1.call-update) | async-done | bytes 12599312 | tf_op jit(solution)/shard_map/all_gather | solution.py:47
  111.5 7.1 %fusion = f32[768]{0:T(1024)S(1)} fusion(bf16[769,8192]{1,0:T(8,128)(2,1)} %all-gather.2.cloned.1.call-done), kind=kLoop, calls=%fused_computation.2 | loop fusion | flops 18873600 | bytes 12585984 | tf_op jit(solution)/shard_map/reduce_sum | solution.py:52
  118.6 7.5 %fusion.2 = bf16[768,8192]{1,0:T(8,128)(2,1)S(1)} fusion(f32[8192]{0:T(1024)S(1)} %bitcast.68, f32[768]{0:T(1024)S(1)} %add_rsqrt_fusion, bf16[769,8192]{1,0:T(8,128)(2,1)} %all-gather.2.cloned.1.call-done), kind=kLoop, calls=%fused_computation.4 | loop fusion | flops 25165824 | bytes 25201664 | tf_op jit(solution)/shard_map/convert_element_type | solution.py:53
  126.1 2.7 constant_dynamic-slice_fusion
  129.5 2.1 collective-permute-start.5
  131.9 11.1 %fusion.3 = f32[768,3,512]{2,0,1:T(8,128)} fusion(bf16[3,1024,512]{2,1,0:T(8,128)(2,1)} %bitcast.4, bf16[3,1024,512]{2,1,0:T(8,128)(2,1)} %bitcast.3, bf16[3,1024,512]{2,1,0:T(8,128)(2,1)S(1)} %bitcast.70, bf16[768,3072]{1,0:T(8,128)(2,1)S(1)} %get-tuple-element.43), kind=kOutput, calls=%fused_computation.6 | convolution fusion | flops 7276068864 | bytes 18874368 | tf_op jit(solution)/shard_map/rk,ikc->ric/dot_general | solution.py:86
  143.0 6.1 %collective-permute-done = bf16[1024,3,512]{2,0,1:T(8,128)(2,1)} collective-permute-done((bf16[1024,3,512]{2,0,1:T(8,128)(2,1)}, bf16[1024,3,512]{2,0,1:T(8,128)(2,1)}, u32[]{:S(2)}, u32[]{:S(2)}) %collective-permute-start) | collective-permute-done | bytes 3145760 | tf_op jit(solution)/shard_map/ppermute | solution.py:61
  150.7 11.3 %fusion.9 = f32[768,3,512]{2,0,1:T(8,128)} fusion(bf16[3,1024,512]{2,1,0:T(8,128)(2,1)S(1)} %bitcast.71, bf16[3,1024,512]{2,1,0:T(8,128)(2,1)} %bitcast.7, bf16[3,1024,512]{2,1,0:T(8,128)(2,1)} %bitcast.6, bf16[768,3072]{1,0:T(8,128)(2,1)S(1)} %get-tuple-element.51), kind=kOutput, calls=%fused_computation.12 | convolution fusion | flops 7276068864 | bytes 18874368 | tf_op jit(solution)/shard_map/rk,ikc->ric/dot_general | solution.py:86
  162.1 5.7 %add_add_fusion = f32[768,3,512]{2,0,1:T(8,128)S(1)} fusion(f32[768,3,512]{2,0,1:T(8,128)S(1)} %copy-done.6, f32[768,3,512]{2,0,1:T(8,128)} %fusion.9, bf16[1024,3,512]{2,0,1:T(8,128)(2,1)} %collective-permute-done, bf16[768,1024]{1,0:T(8,128)(2,1)S(1)} %copy-done.3), kind=kOutput, calls=%fused_computation.28 | convolution fusion | flops 2418278400 | bytes 18874368 | tf_op jit(solution)/shard_map/rk,ikc->ric/dot_general | solution.py:86
  167.8 2.6 fusion.19
  171.8 2.9 collective-permute-start.7
  174.8 4.7 %collective-permute-done.7 = bf16[130,3,512]{2,0,1:T(8,128)(2,1)S(1)} collective-permute-done((bf16[130,3,512]{2,0,1:T(8,128)(2,1)S(1)}, bf16[130,3,512]{2,0,1:T(8,128)(2,1)S(1)}, u32[]{:S(2)}, u32[]{:S(2)}) %collective-permute-start.7) | collective-permute-done | bytes 399392 | tf_op jit(solution)/shard_map/ppermute | solution.py:104
  182.0 2.3 copy-done
  186.8 2.0 slice.71
  189.7 2.3 copy.11
  192.1 2.0 slice.73
  194.2 1.9 fusion.35
  197.6 13.2 %convolution_convert_fusion = bf16[768,8192]{1,0:T(8,128)(2,1)} fusion(bf16[512,8192]{1,0:T(8,128)(2,1)} %param.11, f32[768,512]{1,0:T(8,128)S(1)} %copy.15, f32[896,3,512]{2,0,1:T(8,128)} %copy-done), kind=kOutput, calls=%fused_computation.5 | convolution fusion | flops 6449528832 | bytes 24117248 | tf_op jit(solution)/shard_map/dot_general | solution.py:107
  210.8 108.9 %reduce-scatter.2.cloned.1.call-done = bf16[768,512]{1,0:T(8,128)(2,1)} async-done(((bf16[768,8192]{1,0:T(8,128)(2,1)}), bf16[768,512]{1,0:T(8,128)(2,1)}) %reduce-scatter.2.cloned.1.call-update) | async-done | bytes 786448 | tf_op jit(solution)/shard_map/reduce_scatter | solution.py:108
  319.7 2.2 add_convert_fusion.1
  (53 shorter events, 20.8 us)
Async XLA Ops:
  6.5 104.1 %all-gather.2.cloned.1.call-start = ((), (), s32[]{:S(2)}) async-start(), calls=%async_computation.1 | async-start | bytes 13508608 | tf_op jit(solution)/shard_map/all_gather | solution.py:47
  9.3 310.3 %reduce-scatter.2.cloned.1.call-start = ((), (), s32[]{:S(2)}) async-start(), calls=%async_computation.2 | async-start | bytes 13369344 | tf_op jit(solution)/shard_map/reduce_scatter | solution.py:108
  9.4 120.2 %collective-permute-start.1 = (bf16[1024,3,512]{2,0,1:T(8,128)(2,1)}, bf16[1024,3,512]{2,0,1:T(8,128)(2,1)}, u32[]{:S(2)}, u32[]{:S(2)}) collective-permute-start(bf16[1024,3,512]{2,0,1:T(8,128)(2,1)} %param.8), channel_id=1, source_target_pairs={{0,32},{32,64},{64,96},{96,0},{1,33},{33,65},{65,97},{97,1},{2,34}... | collective-permute-start | bytes 9437192 | tf_op jit(solution)/shard_map/ppermute | solution.py:61
  11.5 118.1 %collective-permute-start.2 = (bf16[1024,3,512]{2,0,1:T(8,128)(2,1)}, bf16[1024,3,512]{2,0,1:T(8,128)(2,1)}, u32[]{:S(2)}, u32[]{:S(2)}) collective-permute-start(bf16[1024,3,512]{2,0,1:T(8,128)(2,1)} %param.8), channel_id=1, source_target_pairs={{0,96},{32,0},{64,32},{96,64},{1,97},{33,1},{65,33},{97,65},{2,98}... | collective-permute-start | bytes 9437192 | tf_op jit(solution)/shard_map/ppermute | solution.py:61
  12.8 136.3 %collective-permute-start = (bf16[1024,3,512]{2,0,1:T(8,128)(2,1)}, bf16[1024,3,512]{2,0,1:T(8,128)(2,1)}, u32[]{:S(2)}, u32[]{:S(2)}) collective-permute-start(bf16[1024,3,512]{2,0,1:T(8,128)(2,1)} %param.8), channel_id=1, source_target_pairs={{0,64},{32,96},{64,0},{96,32},{1,65},{33,97},{65,1},{97,33},{2,66}... | collective-permute-start | bytes 9437192 | tf_op jit(solution)/shard_map/ppermute | solution.py:61
  14.5 136.2 %collective-permute-start.3 = (bf16[1024,3,512]{2,0,1:T(8,128)(2,1)}, bf16[1024,3,512]{2,0,1:T(8,128)(2,1)}, u32[]{:S(2)}, u32[]{:S(2)}) collective-permute-start(bf16[1024,3,512]{2,0,1:T(8,128)(2,1)} %param.8), channel_id=1, source_target_pairs={{0,16},{16,0},{1,17},{17,1},{2,18},{18,2},{3,19},{19,3},{4,20},{20... | collective-permute-start | bytes 9437192 | tf_op jit(solution)/shard_map/ppermute | solution.py:74
  128.8 3.1 copy-start.5
  129.5 21.2 %collective-permute-start.5 = (bf16[1024,3,512]{2,0,1:T(8,128)(2,1)}, bf16[1024,3,512]{2,0,1:T(8,128)(2,1)S(1)}, u32[]{:S(2)}, u32[]{:S(2)}) collective-permute-start(bf16[1024,3,512]{2,0,1:T(8,128)(2,1)} %collective-permute-done.2), channel_id=1, source_target_pairs={{0,16},{16,0},{1,17},{17,1},{2,18},{18,2},{3,19},{19,3},{4,20},{20... | collective-permute-start | bytes 9437192 | tf_op jit(solution)/shard_map/ppermute | solution.py:77
  131.7 19.0 %collective-permute-start.4 = (bf16[1024,3,512]{2,0,1:T(8,128)(2,1)}, bf16[1024,3,512]{2,0,1:T(8,128)(2,1)}, u32[]{:S(2)}, u32[]{:S(2)}) collective-permute-start(bf16[1024,3,512]{2,0,1:T(8,128)(2,1)} %collective-permute-done.1), channel_id=1, source_target_pairs={{0,16},{16,0},{1,17},{17,1},{2,18},{18,2},{3,19},{19,3},{4,20},{20... | collective-permute-start | bytes 9437192 | tf_op jit(solution)/shard_map/ppermute | solution.py:77
  149.2 18.6 %collective-permute-start.6 = (bf16[1024,3,512]{2,0,1:T(8,128)(2,1)}, bf16[1024,3,512]{2,0,1:T(8,128)(2,1)S(1)}, u32[]{:S(2)}, u32[]{:S(2)}) collective-permute-start(bf16[1024,3,512]{2,0,1:T(8,128)(2,1)} %collective-permute-done), channel_id=1, source_target_pairs={{0,16},{16,0},{1,17},{17,1},{2,18},{18,2},{3,19},{19,3},{4,20},{20... | collective-permute-start | bytes 9437192 | tf_op jit(solution)/shard_map/ppermute | solution.py:92
  150.7 11.3 %copy-start.3 = (bf16[768,1024]{1,0:T(8,128)(2,1)S(1)}, bf16[768,1024]{1,0:T(8,128)(2,1)}, u32[]{:S(2)}) copy-start(bf16[768,1024]{1,0:T(8,128)(2,1)} %get-tuple-element.55) | copy-start | bytes 4718596
  150.7 11.3 %copy-start.6 = (f32[768,3,512]{2,0,1:T(8,128)S(1)}, f32[768,3,512]{2,0,1:T(8,128)}, u32[]{:S(2)}) copy-start(f32[768,3,512]{2,0,1:T(8,128)} %fusion.3) | copy-start | bytes 14155780
  162.1 5.7 %copy-start.2 = (bf16[768,1024]{1,0:T(8,128)(2,1)S(1)}, bf16[768,1024]{1,0:T(8,128)(2,1)}, u32[]{:S(2)}) copy-start(bf16[768,1024]{1,0:T(8,128)(2,1)} %get-tuple-element.58) | copy-start | bytes 4718596
  170.4 4.3 %copy-start.4 = (bf16[3,3,512]{2,1,0:T(4,128)(2,1)S(1)}, bf16[3,3,512]{2,1,0:T(4,128)(2,1)}, u32[]{:S(2)}) copy-start(bf16[3,3,512]{2,1,0:T(4,128)(2,1)} %param.9) | copy-start | bytes 27652
  171.8 7.6 %collective-permute-start.7 = (bf16[130,3,512]{2,0,1:T(8,128)(2,1)S(1)}, bf16[130,3,512]{2,0,1:T(8,128)(2,1)S(1)}, u32[]{:S(2)}, u32[]{:S(2)}) collective-permute-start(bf16[130,3,512]{2,0,1:T(8,128)(2,1)S(1)} %slice.77), channel_id=1, source_target_pairs={{0,16},{16,32},{32,48},{48,64},{64,80},{80,96},{96,112},{1,17},{17... | collective-permute-start | bytes 1198088 | tf_op jit(solution)/shard_map/ppermute | solution.py:104
  181.9 2.3 copy-start
  210.7 108.9 %copy-start.1 = (bf16[768,512]{1,0:T(8,128)(2,1)S(1)}, bf16[768,512]{1,0:T(8,128)(2,1)}, u32[]{:S(2)}) copy-start(bf16[768,512]{1,0:T(8,128)(2,1)} %param.6) | copy-start | bytes 2359300
Sparse Core Ops, SparseCore 0:
  9.4 101.1 all-gather.1
  210.9 108.7 reduce-scatter.1

commit v14 on v13

--- a/solution.py
+++ b/solution.py
@@ -88,12 +88,12 @@
         )
 
     projected = product(ordered[0], firsts)
-    last, projected = lax.optimization_barrier((own[late], projected))
-    forwarded[late] = lax.ppermute(last, "core", swap)
     projected, seconds = lax.optimization_barrier(
         (projected, tuple(forwarded[k] for k in early))
     )
     projected = projected + product(ordered[2], seconds)
+    last, projected = lax.optimization_barrier((own[late], projected))
+    forwarded[late] = lax.ppermute(last, "core", swap)
     projected = projected + product(ordered[1], (last,))
     projected, second_last = lax.optimization_barrier((projected, forwarded[late]))
     projected = projected + product(ordered[3], (second_last,))

time: 329 us -> 328 us (level)
  matrix products: 45.9 us -> 41.7 us
    reduce_scatter x1, waiting for transfers between devices: 109 us -> 115 us  [local(): lax.psum_scatter(partial_out.astype(jnp.bfloat16), 'chan', scatter_dimens...]
    ppermute x3, waiting for transfers between devices: 6.12 us -> 0.01 us  [local(): lax.ppermute(in_weight, 'x', [(i, (i + k) % x_count) for i in range(x_cou...]
    dot_general x4, matrix products: 30.8 us -> 26.6 us  [product(): jnp.einsum('rk,ikc->ric', rows, joined_blocks(blocks), preferred_element_...]
  transfers between devices with their start and end apart: 10 -> 10, of which waited for: 4 -> 3; matrix products, arithmetic and copies ran while one was open for 19% -> 18% of each run, Pallas kernels for 0% -> 0%
where the time goes in v14:
time: 328 us
  waiting for transfers between devices  201 us (61%)
  matrix products  41.7 us (13%)
  local copies, waits for them, and re-layouts  31.1 us (9%)
  other arithmetic  26.9 us (8%)
  between operations  13.7 us (4%)
  starting transfers between devices  13 us (4%)
    reduce_scatter x1, waiting for transfers between devices, local(): lax.psum_scatter(partial_out.astype(jnp.bfloat16), 'chan', scatter_dimens...  115 us
    all_gather x1, waiting for transfers between devices, local(): whole_joined = lax.all_gather(joined, 'chan', axis=1, tiled=True)  80.8 us
    dot_general x4, matrix products, product(): jnp.einsum('rk,ikc->ric', rows, joined_blocks(blocks), preferred_element_...  26.6 us
    dot_general x1, matrix products, local(): partial_out = jnp.dot(gated, out_weight, preferred_element_type=jnp.float32)  13.2 us
    slice x7, local copies, waits for them, and re-layouts, hyena_core(): paired = jnp.concatenate([blocks[:-1], blocks[1:]], axis=1)  9.55 us
    reshape x1, local copies, waits for them, and re-layouts, lag_table(): rows = tiled.reshape(groups, length, width - 1)  7.95 us
    convert_element_type x1, other arithmetic, local(): (values * lax.rsqrt(mean_square + 1e-06) * gain_whole.astype(jnp.float32)...  7.48 us
    reduce_sum x1, other arithmetic, local(): mean_square = jnp.mean(values * values, axis=1, keepdims=True)  7.1 us
  transfers between devices with their start and end apart: 10, of which 3 were waited for; matrix products, arithmetic and copies ran while one was open for 18% of the time, Pallas kernels for 0%

profile of v14, /device:TPU:1, one launch (start us, length us, event | category | flops | bytes accessed | tf_op | source)
XLA Modules:
  0.0 327.6 jit_solution(14875868253166959768)
XLA Ops:
  7.2 2.1 pad_maximum_fusion.2
  9.4 2.1 collective-permute-start.1
  16.8 1.9 copy.20
  18.9 7.9 %reshape.30 = bf16[32,128,383]{2,1,0:T(8,128)(2,1)} reshape(bf16[32,49024]{1,0:T(8,128)(2,1)S(1)} %slice.75) | data formatting | bytes 6275072 | tf_op jit(solution)/shard_map/reshape | solution.py:14
  26.8 2.9 slice.76
  29.8 80.8 %all-gather.2.cloned.1.call-done = bf16[769,8192]{1,0:T(8,128)(2,1)} async-done(((bf16[769,512]{1,0:T(8,128)(2,1)}), bf16[769,8192]{1,0:T(8,128)(2,1)}) %all-gather.2.cloned.1.call-update) | async-done | bytes 12599312 | tf_op jit(solution)/shard_map/all_gather | solution.py:47
  111.5 7.1 %fusion = f32[768]{0:T(1024)S(1)} fusion(bf16[769,8192]{1,0:T(8,128)(2,1)} %all-gather.2.cloned.1.call-done), kind=kLoop, calls=%fused_computation.2 | loop fusion | flops 18873600 | bytes 12585984 | tf_op jit(solution)/shard_map/reduce_sum | solution.py:52
  118.6 7.5 %fusion.2 = bf16[768,8192]{1,0:T(8,128)(2,1)S(1)} fusion(f32[8192]{0:T(1024)S(1)} %bitcast.66, f32[768]{0:T(1024)S(1)} %add_rsqrt_fusion, bf16[769,8192]{1,0:T(8,128)(2,1)} %all-gather.2.cloned.1.call-done), kind=kLoop, calls=%fused_computation.4 | loop fusion | flops 25165824 | bytes 25201664 | tf_op jit(solution)/shard_map/convert_element_type | solution.py:53
  126.1 2.8 constant_dynamic-slice_fusion
  129.6 2.1 collective-permute-start.5
  132.0 9.8 %fusion.3 = f32[768,3,512]{2,0,1:T(8,128)S(1)} fusion(bf16[3,1024,512]{2,1,0:T(8,128)(2,1)} %bitcast.4, bf16[3,1024,512]{2,1,0:T(8,128)(2,1)} %bitcast.3, bf16[3,1024,512]{2,1,0:T(8,128)(2,1)S(1)} %bitcast.68, bf16[768,3072]{1,0:T(8,128)(2,1)S(1)} %get-tuple-element.43), kind=kOutput, calls=%fused_computation.6 | convolution fusion | flops 7276068864 | bytes 18874368 | tf_op jit(solution)/shard_map/rk,ikc->ric/dot_general | solution.py:86
  141.8 9.7 %fusion.9 = f32[768,3,512]{2,0,1:T(8,128)S(1)} fusion(bf16[3,1024,512]{2,1,0:T(8,128)(2,1)} %bitcast.8, bf16[3,1024,512]{2,1,0:T(8,128)(2,1)} %bitcast.7, bf16[3,1024,512]{2,1,0:T(8,128)(2,1)} %bitcast.6, bf16[768,3072]{1,0:T(8,128)(2,1)S(1)} %get-tuple-element.50), kind=kOutput, calls=%fused_computation.12 | convolution fusion | flops 7276068864 | bytes 18874368 | tf_op jit(solution)/shard_map/rk,ikc->ric/dot_general | solution.py:86
  153.7 4.5 %fusion.21 = f32[768,3,512]{2,0,1:T(8,128)S(1)} fusion(bf16[1024,3,512]{2,0,1:T(8,128)(2,1)} %collective-permute-done, bf16[768,1024]{1,0:T(8,128)(2,1)S(1)} %copy-done.3), kind=kOutput, calls=%fused_computation.30 | convolution fusion | flops 2415919104 | bytes 9437184 | tf_op jit(solution)/shard_map/rk,ikc->ric/dot_general | solution.py:86
  159.6 2.6 fusion.19
  163.7 3.3 %collective-permute-start.7 = (bf16[130,3,512]{2,0,1:T(8,128)(2,1)S(1)}, bf16[130,3,512]{2,0,1:T(8,128)(2,1)S(1)}, u32[]{:S(2)}, u32[]{:S(2)}) collective-permute-start(bf16[130,3,512]{2,0,1:T(8,128)(2,1)S(1)} %slice.77), channel_id=1, source_target_pairs={{0,16},{16,32},{32,48},{48,64},{64,80},{80,96},{96,112},{1,17},{17... | collective-permute-start | bytes 1198088 | tf_op jit(solution)/shard_map/ppermute | solution.py:104
  167.1 4.7 %collective-permute-done.7 = bf16[130,3,512]{2,0,1:T(8,128)(2,1)S(1)} collective-permute-done((bf16[130,3,512]{2,0,1:T(8,128)(2,1)S(1)}, bf16[130,3,512]{2,0,1:T(8,128)(2,1)S(1)}, u32[]{:S(2)}, u32[]{:S(2)}) %collective-permute-start.7) | collective-permute-done | bytes 399392 | tf_op jit(solution)/shard_map/ppermute | solution.py:104
  174.2 2.3 copy-done
  179.1 2.0 slice.71
  182.0 2.3 copy.11
  184.4 2.0 slice.73
  186.5 2.0 fusion.33
  189.9 13.2 %convolution_convert_fusion = bf16[768,8192]{1,0:T(8,128)(2,1)} fusion(bf16[512,8192]{1,0:T(8,128)(2,1)} %param.11, f32[768,512]{1,0:T(8,128)S(1)} %copy.15, f32[896,3,512]{2,0,1:T(8,128)} %copy-done), kind=kOutput, calls=%fused_computation.5 | convolution fusion | flops 6449528832 | bytes 24117248 | tf_op jit(solution)/shard_map/dot_general | solution.py:107
  203.0 115.5 %reduce-scatter.2.cloned.1.call-done = bf16[768,512]{1,0:T(8,128)(2,1)} async-done(((bf16[768,8192]{1,0:T(8,128)(2,1)}), bf16[768,512]{1,0:T(8,128)(2,1)}) %reduce-scatter.2.cloned.1.call-update) | async-done | bytes 786448 | tf_op jit(solution)/shard_map/reduce_scatter | solution.py:108
  318.5 2.2 add_convert_fusion.1
  (53 shorter events, 20.7 us)
Async XLA Ops:
  6.5 104.1 %all-gather.2.cloned.1.call-start = ((), (), s32[]{:S(2)}) async-start(), calls=%async_computation.1 | async-start | bytes 13508608 | tf_op jit(solution)/shard_map/all_gather | solution.py:47
  9.3 309.2 %reduce-scatter.2.cloned.1.call-start = ((), (), s32[]{:S(2)}) async-start(), calls=%async_computation.2 | async-start | bytes 13369344 | tf_op jit(solution)/shard_map/reduce_scatter | solution.py:108
  9.4 120.2 %collective-permute-start.1 = (bf16[1024,3,512]{2,0,1:T(8,128)(2,1)}, bf16[1024,3,512]{2,0,1:T(8,128)(2,1)}, u32[]{:S(2)}, u32[]{:S(2)}) collective-permute-start(bf16[1024,3,512]{2,0,1:T(8,128)(2,1)} %param.8), channel_id=1, source_target_pairs={{0,32},{32,64},{64,96},{96,0},{1,33},{33,65},{65,97},{97,1},{2,34}... | collective-permute-start | bytes 9437192 | tf_op jit(solution)/shard_map/ppermute | solution.py:61
  11.5 118.1 %collective-permute-start.2 = (bf16[1024,3,512]{2,0,1:T(8,128)(2,1)}, bf16[1024,3,512]{2,0,1:T(8,128)(2,1)}, u32[]{:S(2)}, u32[]{:S(2)}) collective-permute-start(bf16[1024,3,512]{2,0,1:T(8,128)(2,1)} %param.8), channel_id=1, source_target_pairs={{0,96},{32,0},{64,32},{96,64},{1,97},{33,1},{65,33},{97,65},{2,98}... | collective-permute-start | bytes 9437192 | tf_op jit(solution)/shard_map/ppermute | solution.py:61
  12.8 128.9 %collective-permute-start.3 = (bf16[1024,3,512]{2,0,1:T(8,128)(2,1)}, bf16[1024,3,512]{2,0,1:T(8,128)(2,1)}, u32[]{:S(2)}, u32[]{:S(2)}) collective-permute-start(bf16[1024,3,512]{2,0,1:T(8,128)(2,1)} %param.8), channel_id=1, source_target_pairs={{0,16},{16,0},{1,17},{17,1},{2,18},{18,2},{3,19},{19,3},{4,20},{20... | collective-permute-start | bytes 9437192 | tf_op jit(solution)/shard_map/ppermute | solution.py:74
  14.1 138.7 %collective-permute-start = (bf16[1024,3,512]{2,0,1:T(8,128)(2,1)}, bf16[1024,3,512]{2,0,1:T(8,128)(2,1)}, u32[]{:S(2)}, u32[]{:S(2)}) collective-permute-start(bf16[1024,3,512]{2,0,1:T(8,128)(2,1)} %param.8), channel_id=1, source_target_pairs={{0,64},{32,96},{64,0},{96,32},{1,65},{33,97},{65,1},{97,33},{2,66}... | collective-permute-start | bytes 9437192 | tf_op jit(solution)/shard_map/ppermute | solution.py:61
  128.9 3.1 copy-start.5
  129.6 12.2 %collective-permute-start.5 = (bf16[1024,3,512]{2,0,1:T(8,128)(2,1)}, bf16[1024,3,512]{2,0,1:T(8,128)(2,1)}, u32[]{:S(2)}, u32[]{:S(2)}) collective-permute-start(bf16[1024,3,512]{2,0,1:T(8,128)(2,1)} %collective-permute-done.2), channel_id=1, source_target_pairs={{0,16},{16,0},{1,17},{17,1},{2,18},{18,2},{3,19},{19,3},{4,20},{20... | collective-permute-start | bytes 9437192 | tf_op jit(solution)/shard_map/ppermute | solution.py:77
  131.7 10.1 %collective-permute-start.4 = (bf16[1024,3,512]{2,0,1:T(8,128)(2,1)}, bf16[1024,3,512]{2,0,1:T(8,128)(2,1)}, u32[]{:S(2)}, u32[]{:S(2)}) collective-permute-start(bf16[1024,3,512]{2,0,1:T(8,128)(2,1)} %collective-permute-done.1), channel_id=1, source_target_pairs={{0,16},{16,0},{1,17},{17,1},{2,18},{18,2},{3,19},{19,3},{4,20},{20... | collective-permute-start | bytes 9437192 | tf_op jit(solution)/shard_map/ppermute | solution.py:77
  151.6 2.1 copy-start.3
  152.8 6.6 %collective-permute-start.6 = (bf16[1024,3,512]{2,0,1:T(8,128)(2,1)}, bf16[1024,3,512]{2,0,1:T(8,128)(2,1)S(1)}, u32[]{:S(2)}, u32[]{:S(2)}) collective-permute-start(bf16[1024,3,512]{2,0,1:T(8,128)(2,1)} %collective-permute-done), channel_id=1, source_target_pairs={{0,16},{16,0},{1,17},{17,1},{2,18},{18,2},{3,19},{19,3},{4,20},{20... | collective-permute-start | bytes 9437192 | tf_op jit(solution)/shard_map/ppermute | solution.py:96
  158.2 1.4 copy-start.2
  162.2 4.8 %copy-start.4 = (bf16[3,3,512]{2,1,0:T(4,128)(2,1)S(1)}, bf16[3,3,512]{2,1,0:T(4,128)(2,1)}, u32[]{:S(2)}) copy-start(bf16[3,3,512]{2,1,0:T(4,128)(2,1)} %param.9) | copy-start | bytes 27652
  163.7 8.1 %collective-permute-start.7 = (bf16[130,3,512]{2,0,1:T(8,128)(2,1)S(1)}, bf16[130,3,512]{2,0,1:T(8,128)(2,1)S(1)}, u32[]{:S(2)}, u32[]{:S(2)}) collective-permute-start(bf16[130,3,512]{2,0,1:T(8,128)(2,1)S(1)} %slice.77), channel_id=1, source_target_pairs={{0,16},{16,32},{32,48},{48,64},{64,80},{80,96},{96,112},{1,17},{17... | collective-permute-start | bytes 1198088 | tf_op jit(solution)/shard_map/ppermute | solution.py:104
  174.2 2.4 copy-start
  203.0 115.5 %copy-start.1 = (bf16[768,512]{1,0:T(8,128)(2,1)S(1)}, bf16[768,512]{1,0:T(8,128)(2,1)}, u32[]{:S(2)}) copy-start(bf16[768,512]{1,0:T(8,128)(2,1)} %param.6) | copy-start | bytes 2359300
Sparse Core Ops, SparseCore 0:
  9.4 101.1 all-gather.1
  203.2 115.3 reduce-scatter.1

commit v15 on v14

--- a/solution.py
+++ b/solution.py
@@ -94,9 +94,9 @@
     projected = projected + product(ordered[2], seconds)
     last, projected = lax.optimization_barrier((own[late], projected))
     forwarded[late] = lax.ppermute(last, "core", swap)
-    projected = projected + product(ordered[1], (last,))
     projected, second_last = lax.optimization_barrier((projected, forwarded[late]))
-    projected = projected + product(ordered[3], (second_last,))
+    tail_rows = jnp.concatenate([ordered[1], ordered[3]], axis=1)
+    projected = projected + product(tail_rows, (last, second_last))
     streams = projected.astype(jnp.bfloat16)
     parts_count = lax.axis_size(SEQ)
     halo_rows = length + 2

time: 328 us -> 332 us (1.012)
  waiting for transfers between devices: 201 us -> 207 us
    ppermute x1, waiting for transfers between devices: 0.01 us -> 5.5 us  [local(): forwarded[late] = lax.ppermute(last, 'core', swap)]
    dot_general x4 -> x3, matrix products: 26.6 us -> 26.4 us  [product(): jnp.einsum('rk,ikc->ric', rows, joined_blocks(blocks), preferred_element_...]
  transfers between devices with their start and end apart: 10 -> 10, of which waited for: 3 -> 4; matrix products, arithmetic and copies ran while one was open for 18% -> 16% of each run, Pallas kernels for 0% -> 0%
where the time goes in v15:
time: 332 us
  waiting for transfers between devices  207 us (62%)
  matrix products  41.5 us (12%)
  local copies, waits for them, and re-layouts  30.9 us (9%)
  other arithmetic  25.8 us (8%)
  between operations  13.7 us (4%)
  starting transfers between devices  13.2 us (4%)
    reduce_scatter x1, waiting for transfers between devices, local(): lax.psum_scatter(partial_out.astype(jnp.bfloat16), 'chan', scatter_dimens...  116 us
    all_gather x1, waiting for transfers between devices, local(): whole_joined = lax.all_gather(joined, 'chan', axis=1, tiled=True)  80.8 us
    dot_general x3, matrix products, product(): jnp.einsum('rk,ikc->ric', rows, joined_blocks(blocks), preferred_element_...  26.4 us
    dot_general x1, matrix products, local(): partial_out = jnp.dot(gated, out_weight, preferred_element_type=jnp.float32)  13.2 us
    slice x7, local copies, waits for them, and re-layouts, hyena_core(): paired = jnp.concatenate([blocks[:-1], blocks[1:]], axis=1)  9.55 us
    reshape x1, local copies, waits for them, and re-layouts, lag_table(): rows = tiled.reshape(groups, length, width - 1)  7.95 us
    convert_element_type x1, other arithmetic, local(): (values * lax.rsqrt(mean_square + 1e-06) * gain_whole.astype(jnp.float32)...  7.48 us
    reduce_sum x1, other arithmetic, local(): mean_square = jnp.mean(values * values, axis=1, keepdims=True)  7.1 us
  transfers between devices with their start and end apart: 10, of which 4 were waited for; matrix products, arithmetic and copies ran while one was open for 16% of the time, Pallas kernels for 0%

profile of v15, /device:TPU:1, one launch (start us, length us, event | category | flops | bytes accessed | tf_op | source)
XLA Modules:
  0.0 331.8 jit_solution(8874242306524865133)
XLA Ops:
  7.2 2.1 pad_maximum_fusion.2
  9.4 2.1 collective-permute-start.1
  16.8 1.9 copy.20
  18.9 7.9 %reshape.30 = bf16[32,128,383]{2,1,0:T(8,128)(2,1)} reshape(bf16[32,49024]{1,0:T(8,128)(2,1)S(1)} %slice.75) | data formatting | bytes 6275072 | tf_op jit(solution)/shard_map/reshape | solution.py:14
  26.8 2.9 slice.76
  29.8 80.8 %all-gather.2.cloned.1.call-done = bf16[769,8192]{1,0:T(8,128)(2,1)} async-done(((bf16[769,512]{1,0:T(8,128)(2,1)}), bf16[769,8192]{1,0:T(8,128)(2,1)}) %all-gather.2.cloned.1.call-update) | async-done | bytes 12599312 | tf_op jit(solution)/shard_map/all_gather | solution.py:47
  111.5 7.1 %fusion = f32[768]{0:T(1024)S(1)} fusion(bf16[769,8192]{1,0:T(8,128)(2,1)} %all-gather.2.cloned.1.call-done), kind=kLoop, calls=%fused_computation.2 | loop fusion | flops 18873600 | bytes 12585984 | tf_op jit(solution)/shard_map/reduce_sum | solution.py:52
  118.6 7.5 %fusion.2 = bf16[768,8192]{1,0:T(8,128)(2,1)S(1)} fusion(f32[8192]{0:T(1024)S(1)} %bitcast.59, f32[768]{0:T(1024)S(1)} %add_rsqrt_fusion, bf16[769,8192]{1,0:T(8,128)(2,1)} %all-gather.2.cloned.1.call-done), kind=kLoop, calls=%fused_computation.4 | loop fusion | flops 25165824 | bytes 25201664 | tf_op jit(solution)/shard_map/convert_element_type | solution.py:53
  126.1 2.8 constant_dynamic-slice_fusion
  129.6 2.1 collective-permute-start.5
  132.0 9.8 %fusion.3 = f32[768,3,512]{2,0,1:T(8,128)S(1)} fusion(bf16[3,1024,512]{2,1,0:T(8,128)(2,1)} %bitcast.4, bf16[3,1024,512]{2,1,0:T(8,128)(2,1)} %bitcast.3, bf16[3,1024,512]{2,1,0:T(8,128)(2,1)S(1)} %bitcast.61, bf16[768,3072]{1,0:T(8,128)(2,1)S(1)} %get-tuple-element.43), kind=kOutput, calls=%fused_computation.6 | convolution fusion | flops 7276068864 | bytes 18874368 | tf_op jit(solution)/shard_map/rk,ikc->ric/dot_general | solution.py:86
  141.8 9.7 %fusion.9 = f32[768,3,512]{2,0,1:T(8,128)S(1)} fusion(bf16[3,1024,512]{2,1,0:T(8,128)(2,1)} %bitcast.8, bf16[3,1024,512]{2,1,0:T(8,128)(2,1)} %bitcast.7, bf16[3,1024,512]{2,1,0:T(8,128)(2,1)} %bitcast.6, bf16[768,3072]{1,0:T(8,128)(2,1)S(1)} %get-tuple-element.50), kind=kOutput, calls=%fused_computation.12 | convolution fusion | flops 7276068864 | bytes 18874368 | tf_op jit(solution)/shard_map/rk,ikc->ric/dot_general | solution.py:86
  153.7 5.5 %collective-permute-done.6 = bf16[1024,3,512]{2,0,1:T(8,128)(2,1)S(1)} collective-permute-done((bf16[1024,3,512]{2,0,1:T(8,128)(2,1)}, bf16[1024,3,512]{2,0,1:T(8,128)(2,1)S(1)}, u32[]{:S(2)}, u32[]{:S(2)}) %collective-permute-start.6) | collective-permute-done | bytes 3145760 | tf_op jit(solution)/shard_map/ppermute | solution.py:96
  159.2 6.9 %fusion.15 = f32[768,3,512]{2,0,1:T(8,128)S(1)} fusion(bf16[3,1024,512]{2,1,0:T(8,128)(2,1)S(1)} %bitcast.62, bf16[3,1024,512]{2,1,0:T(8,128)(2,1)} %bitcast.10, bf16[768,1024]{1,0:T(8,128)(2,1)S(1)} %copy-done.2, bf16[768,1024]{1,0:T(8,128)(2,1)S(1)} %copy-done.3), kind=kOutput, calls=%fused_computation.18 | convolution fusion | flops 4850712576 | bytes 14155776 | tf_op jit(solution)/shard_map/rk,ikc->ric/dot_general | solution.py:86
  167.6 3.6 %collective-permute-start.7 = (bf16[130,3,512]{2,0,1:T(8,128)(2,1)S(1)}, bf16[130,3,512]{2,0,1:T(8,128)(2,1)S(1)}, u32[]{:S(2)}, u32[]{:S(2)}) collective-permute-start(bf16[130,3,512]{2,0,1:T(8,128)(2,1)S(1)} %slice.77), channel_id=1, source_target_pairs={{0,16},{16,32},{32,48},{48,64},{64,80},{80,96},{96,112},{1,17},{17... | collective-permute-start | bytes 1198088 | tf_op jit(solution)/shard_map/ppermute | solution.py:104
  171.2 4.7 %collective-permute-done.7 = bf16[130,3,512]{2,0,1:T(8,128)(2,1)S(1)} collective-permute-done((bf16[130,3,512]{2,0,1:T(8,128)(2,1)S(1)}, bf16[130,3,512]{2,0,1:T(8,128)(2,1)S(1)}, u32[]{:S(2)}, u32[]{:S(2)}) %collective-permute-start.7) | collective-permute-done | bytes 399392 | tf_op jit(solution)/shard_map/ppermute | solution.py:104
  178.4 2.3 copy-done
  183.2 2.0 slice.71
  186.2 2.3 copy.11
  188.5 2.0 slice.73
  190.6 1.9 fusion.33
  194.0 13.2 %convolution_convert_fusion = bf16[768,8192]{1,0:T(8,128)(2,1)} fusion(bf16[512,8192]{1,0:T(8,128)(2,1)} %param.11, f32[768,512]{1,0:T(8,128)S(1)} %copy.15, f32[896,3,512]{2,0,1:T(8,128)} %copy-done), kind=kOutput, calls=%fused_computation.5 | convolution fusion | flops 6449528832 | bytes 24117248 | tf_op jit(solution)/shard_map/dot_general | solution.py:107
  207.2 115.6 %reduce-scatter.2.cloned.1.call-done = bf16[768,512]{1,0:T(8,128)(2,1)} async-done(((bf16[768,8192]{1,0:T(8,128)(2,1)}), bf16[768,512]{1,0:T(8,128)(2,1)}) %reduce-scatter.2.cloned.1.call-update) | async-done | bytes 786448 | tf_op jit(solution)/shard_map/reduce_scatter | solution.py:108
  322.7 2.2 add_convert_fusion.1
  (51 shorter events, 19.2 us)
Async XLA Ops:
  6.5 104.1 %all-gather.2.cloned.1.call-start = ((), (), s32[]{:S(2)}) async-start(), calls=%async_computation.1 | async-start | bytes 13508608 | tf_op jit(solution)/shard_map/all_gather | solution.py:47
  9.3 313.4 %reduce-scatter.2.cloned.1.call-start = ((), (), s32[]{:S(2)}) async-start(), calls=%async_computation.2 | async-start | bytes 13369344 | tf_op jit(solution)/shard_map/reduce_scatter | solution.py:108
  9.4 120.2 %collective-permute-start.1 = (bf16[1024,3,512]{2,0,1:T(8,128)(2,1)}, bf16[1024,3,512]{2,0,1:T(8,128)(2,1)}, u32[]{:S(2)}, u32[]{:S(2)}) collective-permute-start(bf16[1024,3,512]{2,0,1:T(8,128)(2,1)} %param.8), channel_id=1, source_target_pairs={{0,32},{32,64},{64,96},{96,0},{1,33},{33,65},{65,97},{97,1},{2,34}... | collective-permute-start | bytes 9437192 | tf_op jit(solution)/shard_map/ppermute | solution.py:61
  11.5 118.1 %collective-permute-start.2 = (bf16[1024,3,512]{2,0,1:T(8,128)(2,1)}, bf16[1024,3,512]{2,0,1:T(8,128)(2,1)}, u32[]{:S(2)}, u32[]{:S(2)}) collective-permute-start(bf16[1024,3,512]{2,0,1:T(8,128)(2,1)} %param.8), channel_id=1, source_target_pairs={{0,96},{32,0},{64,32},{96,64},{1,97},{33,1},{65,33},{97,65},{2,98}... | collective-permute-start | bytes 9437192 | tf_op jit(solution)/shard_map/ppermute | solution.py:61
  12.8 128.9 %collective-permute-start.3 = (bf16[1024,3,512]{2,0,1:T(8,128)(2,1)}, bf16[1024,3,512]{2,0,1:T(8,128)(2,1)}, u32[]{:S(2)}, u32[]{:S(2)}) collective-permute-start(bf16[1024,3,512]{2,0,1:T(8,128)(2,1)} %param.8), channel_id=1, source_target_pairs={{0,16},{16,0},{1,17},{17,1},{2,18},{18,2},{3,19},{19,3},{4,20},{20... | collective-permute-start | bytes 9437192 | tf_op jit(solution)/shard_map/ppermute | solution.py:74
  14.1 138.7 %collective-permute-start = (bf16[1024,3,512]{2,0,1:T(8,128)(2,1)}, bf16[1024,3,512]{2,0,1:T(8,128)(2,1)}, u32[]{:S(2)}, u32[]{:S(2)}) collective-permute-start(bf16[1024,3,512]{2,0,1:T(8,128)(2,1)} %param.8), channel_id=1, source_target_pairs={{0,64},{32,96},{64,0},{96,32},{1,65},{33,97},{65,1},{97,33},{2,66}... | collective-permute-start | bytes 9437192 | tf_op jit(solution)/shard_map/ppermute | solution.py:61
  128.9 3.1 copy-start.5
  129.6 12.2 %collective-permute-start.5 = (bf16[1024,3,512]{2,0,1:T(8,128)(2,1)}, bf16[1024,3,512]{2,0,1:T(8,128)(2,1)}, u32[]{:S(2)}, u32[]{:S(2)}) collective-permute-start(bf16[1024,3,512]{2,0,1:T(8,128)(2,1)} %collective-permute-done.2), channel_id=1, source_target_pairs={{0,16},{16,0},{1,17},{17,1},{2,18},{18,2},{3,19},{19,3},{4,20},{20... | collective-permute-start | bytes 9437192 | tf_op jit(solution)/shard_map/ppermute | solution.py:77
  131.7 10.1 %collective-permute-start.4 = (bf16[1024,3,512]{2,0,1:T(8,128)(2,1)}, bf16[1024,3,512]{2,0,1:T(8,128)(2,1)}, u32[]{:S(2)}, u32[]{:S(2)}) collective-permute-start(bf16[1024,3,512]{2,0,1:T(8,128)(2,1)} %collective-permute-done.1), channel_id=1, source_target_pairs={{0,16},{16,0},{1,17},{17,1},{2,18},{18,2},{3,19},{19,3},{4,20},{20... | collective-permute-start | bytes 9437192 | tf_op jit(solution)/shard_map/ppermute | solution.py:77
  151.6 7.6 %copy-start.2 = (bf16[768,1024]{1,0:T(8,128)(2,1)S(1)}, bf16[768,1024]{1,0:T(8,128)(2,1)}, u32[]{:S(2)}) copy-start(bf16[768,1024]{1,0:T(8,128)(2,1)} %get-tuple-element.58) | copy-start | bytes 4718596
  151.6 7.6 %copy-start.3 = (bf16[768,1024]{1,0:T(8,128)(2,1)S(1)}, bf16[768,1024]{1,0:T(8,128)(2,1)}, u32[]{:S(2)}) copy-start(bf16[768,1024]{1,0:T(8,128)(2,1)} %get-tuple-element.57) | copy-start | bytes 4718596
  152.8 6.4 %collective-permute-start.6 = (bf16[1024,3,512]{2,0,1:T(8,128)(2,1)}, bf16[1024,3,512]{2,0,1:T(8,128)(2,1)S(1)}, u32[]{:S(2)}, u32[]{:S(2)}) collective-permute-start(bf16[1024,3,512]{2,0,1:T(8,128)(2,1)} %collective-permute-done), channel_id=1, source_target_pairs={{0,16},{16,0},{1,17},{17,1},{2,18},{18,2},{3,19},{19,3},{4,20},{20... | collective-permute-start | bytes 9437192 | tf_op jit(solution)/shard_map/ppermute | solution.py:96
  166.1 5.0 %copy-start.4 = (bf16[3,3,512]{2,1,0:T(4,128)(2,1)S(1)}, bf16[3,3,512]{2,1,0:T(4,128)(2,1)}, u32[]{:S(2)}) copy-start(bf16[3,3,512]{2,1,0:T(4,128)(2,1)} %param.9) | copy-start | bytes 27652
  167.6 8.3 %collective-permute-start.7 = (bf16[130,3,512]{2,0,1:T(8,128)(2,1)S(1)}, bf16[130,3,512]{2,0,1:T(8,128)(2,1)S(1)}, u32[]{:S(2)}, u32[]{:S(2)}) collective-permute-start(bf16[130,3,512]{2,0,1:T(8,128)(2,1)S(1)} %slice.77), channel_id=1, source_target_pairs={{0,16},{16,32},{32,48},{48,64},{64,80},{80,96},{96,112},{1,17},{17... | collective-permute-start | bytes 1198088 | tf_op jit(solution)/shard_map/ppermute | solution.py:104
  178.4 2.4 copy-start
  207.2 115.6 %copy-start.1 = (bf16[768,512]{1,0:T(8,128)(2,1)S(1)}, bf16[768,512]{1,0:T(8,128)(2,1)}, u32[]{:S(2)}) copy-start(bf16[768,512]{1,0:T(8,128)(2,1)} %param.6) | copy-start | bytes 2359300
Sparse Core Ops, SparseCore 0:
  9.4 101.1 all-gather.1
  207.3 115.3 reduce-scatter.1
